TPU v7x, 32 devices: a whole 2x2x4 slice. The times are simulated.
32 devices in a mesh: groups: 2 (over x), band: 16 (over z, y, core).
Axes of the slice: x: 2, y: 2, z: 4, core: 2. Of those that a mesh axis runs over, the one named last changes fastest.
Arguments:
- images: float32 [32, 8, 16, 32, 128], P(('groups', 'band')), parts along dimension 0, may hold values from -6 to 6
- coeffs: float32 [32, 8, 27, 3], P(('groups', 'band')), parts along dimension 0, may hold values from -3 to 3
- weights: float32 [32, 8], P(('groups', 'band')), parts along dimension 0, may hold values from 0.25 to 4
- scales: float32 [32, 8], P(('groups', 'band')), parts along dimension 0, may hold values from 0.5 to 2
- valid_epoch: int32 [32, 8], P(('groups', 'band')), parts along dimension 0, may hold values 0 or 1
- patch_owner: int32 [32, 8, 16, 1], P(('groups', 'band')), parts along dimension 0, may hold values from 0 to 15; in each aligned block of 128 rows (0 to 127, 128 to 255, ..., all dimensions but the last counted through in order) at most 16 rows name the same one
- patch_local: int32 [32, 8, 16], P(('groups', 'band')), parts along dimension 0, may hold values from 0 to 3
Outputs:
- difference: float32 [32, 8, 16, 32, 128], P(('groups', 'band')), parts along dimension 0
- templates: bfloat16 [128, 32, 128], P(('groups', 'band')), parts along dimension 0
There are 2 independent parts, one for each index of `groups`. A program takes and returns all parts, laid end to end along the dimension named above; each array names one. Nothing has to cross between parts.
Inputs may be any that keep to these rules, and one draw needn't show every extreme that they name: `patch_owner`: no band sends more than 16 of its tiles to one owner, and some band sends exactly 16 tiles to some owner; every owner receives some tile.
All inputs are finite; a program needn't handle non-finite values. No bound on the sum of `valid_epoch` on one device may be relied on, other than what follows from the above.
Results may differ from a plain program's by a relative error of at most 0.0078.
Values may be sent and summed in bfloat16 or wider, within the bound.
No kernel may reach another device: no remote copies, remote signals or barrier semaphores. Data moves between devices by JAX's collectives and lax.ppermute only.
A program may use at most 64 MiB of HBM per device.

v0:
```python
import jax
import jax.numpy as jnp
import numpy as np
from jax import lax
from jax.sharding import PartitionSpec as P

PD = 4
HALF = 9
P_SIZE = 3


sigmas = (0.75, 1.5, 3.0)
degrees = (4, 2, 2)


def kernel_matrices(tile_side):
    rows_out = lax.broadcasted_iota(jnp.int32, (tile_side, tile_side), 0)
    rows_in = lax.broadcasted_iota(jnp.int32, (tile_side, tile_side), 1)
    offset = (rows_out - rows_in).astype(jnp.float32)
    inside = (jnp.abs(rows_out - rows_in) <= HALF).astype(jnp.float32)
    taps = jnp.arange(-HALF, HALF + 1).astype(jnp.float32)
    tables = []
    for width_sigma, degree in zip(sigmas, degrees):
        normal_total = jnp.sum(jnp.exp(-taps * taps / (2.0 * width_sigma * width_sigma)))
        envelope = (
            jnp.exp(-offset * offset / (2.0 * width_sigma * width_sigma)) * inside / normal_total
        )
        for power in range(degree + 1):
            tables.append(envelope * (offset / width_sigma) ** power)
    return jnp.stack(tables)


def basis_pairs():
    kernel_list = []
    base_index = 0
    for degree in degrees:
        for column_power in range(degree + 1):
            for row_power in range(degree + 1 - column_power):
                kernel_list.append((base_index + row_power, base_index + column_power))
        base_index = base_index + degree + 1
    return kernel_list


def row_selector():
    kernel_list = basis_pairs()
    row_count = sum((degree + 1 for degree in degrees))
    table = np.zeros((len(kernel_list), row_count), np.float32)
    for basis_index, kernel_pair in enumerate(kernel_list):
        table[basis_index, kernel_pair[0]] = 1.0
    return jnp.asarray(table, jnp.float32)


def coordinates(per_epoch, tile_rows, tile_side):
    tile_index = lax.broadcasted_iota(jnp.float32, (per_epoch, tile_side), 0)
    column = lax.broadcasted_iota(jnp.float32, (per_epoch, tile_side), 1)
    across = 2.0 * (tile_index * tile_side + column + 0.5) / (per_epoch * tile_side) - 1.0
    down = 2.0 * (jnp.arange(tile_rows).astype(jnp.float32) + 0.5) / tile_rows - 1.0
    return (across, down)


def body(images, coeffs, weights, scales, valid_epoch, patch_owner, patch_local):
    band_count = lax.axis_size("band")
    epochs = images.shape[1]
    per_epoch = images.shape[2]
    tile_rows = images.shape[3]
    tile_side = images.shape[4]
    pixel_count = tile_rows * tile_side
    tile_count = epochs * per_epoch
    capacity = max(2, 2 * tile_count // band_count)
    column_kernels = kernel_matrices(tile_side)
    row_tables = kernel_matrices(tile_rows).astype(jnp.bfloat16)
    kernel_list = basis_pairs()
    column_stack = jnp.stack([column_kernels[kernel_pair[1]] for kernel_pair in kernel_list])
    selector = row_selector()
    row_count = column_kernels.shape[0]
    across, down = coordinates(per_epoch, tile_rows, tile_side)

    def one_epoch(epoch_inputs):
        tile_stack, coef_epoch = epoch_inputs
        mixing = selector[:, :, None] * coef_epoch[:, None, :]
        combined = jnp.einsum(
            "bjp,box->jxpo", mixing, column_stack, precision=lax.Precision.HIGHEST
        )
        mixer = combined.reshape(row_count * tile_side, P_SIZE * tile_side).astype(jnp.bfloat16)
        pixels = tile_stack.astype(jnp.bfloat16)
        rowed = jnp.einsum(
            "jpy,tyx->tpjx", row_tables, pixels, preferred_element_type=jnp.float32
        ).astype(jnp.bfloat16)
        flat = rowed.reshape(per_epoch, tile_rows, row_count * tile_side)
        spatial = jnp.einsum("tpk,kq->tpq", flat, mixer, preferred_element_type=jnp.float32)
        spatial = spatial.reshape(per_epoch, tile_rows, P_SIZE, tile_side)
        return (
            spatial[:, :, 0, :]
            + across[:, None, :] * spatial[:, :, 1, :]
            + down[None, :, None] * spatial[:, :, 2, :]
        )

    homogenized = lax.map(one_epoch, (images[0], coeffs[0])).reshape(tile_count, pixel_count)
    owners = patch_owner[0].reshape(tile_count)
    local_patch = patch_local[0].reshape(tile_count)
    order_index = jnp.arange(tile_count)
    earlier = (owners[:, None] == owners[None, :]) & (order_index[None, :] < order_index[:, None])
    send_rank = jnp.sum(earlier.astype(jnp.int32), axis=1)
    send_slot = owners * capacity + send_rank
    slot_total = band_count * capacity
    epoch_weight = (weights[0] * valid_epoch[0].astype(jnp.float32)).astype(jnp.bfloat16)
    tile_weight = jnp.broadcast_to(epoch_weight[:, None], (epochs, per_epoch)).reshape(tile_count)
    placement_table = (local_patch[:, None] == jnp.arange(PD)[None, :]).astype(jnp.bfloat16)
    weight_table = (
        placement_table.astype(jnp.float32) * tile_weight.astype(jnp.float32)[:, None]
    ).astype(jnp.bfloat16)
    outgoing = (
        jnp.zeros((slot_total, pixel_count), jnp.bfloat16)
        .at[send_slot]
        .set(homogenized.astype(jnp.bfloat16))
    )
    out_place = jnp.zeros((slot_total, PD), jnp.bfloat16).at[send_slot].set(placement_table)
    out_weight = jnp.zeros((slot_total, PD), jnp.bfloat16).at[send_slot].set(weight_table)
    received, got_place, got_weight = (
        lax.all_to_all(
            outgoing.reshape(band_count, capacity, pixel_count),
            "band",
            split_axis=0,
            concat_axis=0,
            tiled=True,
        ),
        lax.all_to_all(
            out_place.reshape(band_count, capacity, PD),
            "band",
            split_axis=0,
            concat_axis=0,
            tiled=True,
        ),
        lax.all_to_all(
            out_weight.reshape(band_count, capacity, PD),
            "band",
            split_axis=0,
            concat_axis=0,
            tiled=True,
        ),
    )
    flat_weight = got_weight.reshape(slot_total, PD)
    numerator = jnp.einsum(
        "sq,sk->qk",
        flat_weight,
        received.reshape(slot_total, pixel_count),
        preferred_element_type=jnp.float32,
    )
    denominator = 1.0 + jnp.sum(flat_weight.astype(jnp.float32), axis=0)
    templates = (numerator / denominator[:, None]).astype(jnp.bfloat16)
    global_patch = owners * PD + local_patch
    shard_rows = lax.all_gather(templates, "band", axis=0, tiled=True)
    row_total = shard_rows.shape[0]
    chooser = (global_patch[:, None] == jnp.arange(row_total)[None, :]).astype(jnp.bfloat16)
    matched = jnp.dot(chooser, shard_rows, preferred_element_type=jnp.float32)
    tile_scale = jnp.broadcast_to(scales[0][:, None], (epochs, per_epoch)).reshape(tile_count)
    difference = homogenized - tile_scale[:, None] * matched
    return (
        difference.reshape(1, epochs, per_epoch, tile_rows, tile_side),
        templates.reshape(PD, tile_rows, tile_side),
    )


def solution(mesh):
    return jax.shard_map(
        body,
        mesh=mesh,
        in_specs=(
            P(("groups", "band"), None, None, None, None),
            P(("groups", "band"), None, None, None),
            P(("groups", "band"), None),
            P(("groups", "band"), None),
            P(("groups", "band"), None),
            P(("groups", "band"), None, None, None),
            P(("groups", "band"), None, None),
        ),
        out_specs=(
            P(("groups", "band"), None, None, None, None),
            P(("groups", "band"), None, None),
        ),
        check_vma=False,
    )
```

profile of v0, /device:TPU:0, one launch (start us, length us, event | category | flops | bytes accessed | tf_op | source)
XLA Modules:
  0.0 226.5 jit_solution(9913890451470285794)
XLA Ops:
  2.7 1.4 fusion.47
  4.7 0.9 scatter_custom_fusion
  6.4 7.5 %all-to-all-start = ((bf16[16,16,4]{1,2,0:T(4,128)(2,1)}), bf16[16,16,4]{1,2,0:T(4,128)(2,1)}, u32[]{:S(2)}, u32[]{:S(2)}) async-start(bf16[16,16,4]{1,2,0:T(4,128)(2,1)} %copy.53), calls=%async_computation | async-start | bytes 32768 | tf_op jit(solution)/shard_map/all_to_all | solution.py:134
  15.9 1.2 constant_dynamic-update-slice_fusion.10
  18.5 1.2 constant_dynamic-update-slice_fusion.9
  19.8 1.2 constant_dynamic-update-slice_fusion.8
  21.0 1.2 constant_dynamic-update-slice_fusion.7
  22.3 1.3 constant_dynamic-update-slice_fusion.6
  23.5 1.2 constant_dynamic-update-slice_fusion.5
  24.7 1.2 constant_dynamic-update-slice_fusion.4
  26.0 1.2 constant_dynamic-update-slice_fusion.3
  27.2 1.2 constant_dynamic-update-slice_fusion.2
  28.5 1.2 constant_dynamic-update-slice_fusion.1
  29.7 1.2 constant_dynamic-update-slice_fusion
  31.0 2.8 %bitcast_convert_fusion.3 = bf16[8,16,32,128]{3,2,1,0:T(8,128)(2,1)} fusion(f32[1,8,16,32,128]{4,3,2,1,0:T(8,128)} %param.10), kind=kLoop, calls=%fused_computation.143 | loop fusion | flops 524288 | bytes 3145728
  51.4 2.3 %copy.50 = f32[27,128,128]{2,0,1:T(8,128)} copy(f32[27,128,128]{2,1,0:T(8,128)S(1)} %constant_dynamic-update-slice_fusion.11) | data formatting | bytes 3538944
  53.8 85.4 %while.12 = (s32[]{:T(128)}, f32[8,16,32,128]{3,2,1,0:T(8,128)}, bf16[8,16,32,128]{3,2,1,0:T(8,128)(2,1)}, bf16[11,32,32]{2,1,0:T(8,128)(2,1)}, f32[8,27,3]{1,2,...) while((s32[]{:T(128)}, f32[8,16,32,128]{3,2,1,0:T(8,128)}, ...), condition=%wide.region_4.0_spmd.clone.clone, body=%wide.region_3.0_spmd.sunk.clone.clone.sunk | while | flops 776496128 | bytes 16842668 | solution.py:98
  54.9 1.5 fusion.69
  57.1 1.0 reshape.451
  58.1 4.2 %fusion.68 = bf16[11,3,128,128]{3,0,2,1:T(8,128)(2,1)S(1)} fusion(f32[27,128,128]{2,0,1:T(8,128)} %get-tuple-element.184, f32[27,3]{0,1:T(4,128)} %dynamic-slice_bitcast_fusion.2, f32[27,11]{0,1:T(8,128)S(1)} %get-tuple-element.187), kind=kOutput, calls=%fused_computation.6.clone.1 | convolution fusion | flops 175719296 | bytes 2852328 | tf_op jit(solution)/shard_map/while/body/eval_jaxpr/bjp,box->jxpo/dot_general | solution.py:81
  62.7 0.9 fusion.70
  63.6 0.8 fusion.71
  65.6 1.5 fusion.69
  67.8 1.0 reshape.451
  68.8 4.2 %fusion.68 = bf16[11,3,128,128]{3,0,2,1:T(8,128)(2,1)S(1)} fusion(f32[27,128,128]{2,0,1:T(8,128)} %get-tuple-element.184, f32[27,3]{0,1:T(4,128)} %dynamic-slice_bitcast_fusion.2, f32[27,11]{0,1:T(8,128)S(1)} %get-tuple-element.187), kind=kOutput, calls=%fused_computation.6.clone.1 | convolution fusion | flops 175719296 | bytes 2852328 | tf_op jit(solution)/shard_map/while/body/eval_jaxpr/bjp,box->jxpo/dot_general | solution.py:81
  73.3 0.9 fusion.70
  74.3 0.8 fusion.71
  76.3 1.5 fusion.69
  78.5 1.0 reshape.451
  79.4 4.2 %fusion.68 = bf16[11,3,128,128]{3,0,2,1:T(8,128)(2,1)S(1)} fusion(f32[27,128,128]{2,0,1:T(8,128)} %get-tuple-element.184, f32[27,3]{0,1:T(4,128)} %dynamic-slice_bitcast_fusion.2, f32[27,11]{0,1:T(8,128)S(1)} %get-tuple-element.187), kind=kOutput, calls=%fused_computation.6.clone.1 | convolution fusion | flops 175719296 | bytes 2852328 | tf_op jit(solution)/shard_map/while/body/eval_jaxpr/bjp,box->jxpo/dot_general | solution.py:81
  84.0 0.9 fusion.70
  85.0 0.8 fusion.71
  87.0 1.5 fusion.69
  89.2 1.0 reshape.451
  90.1 4.2 %fusion.68 = bf16[11,3,128,128]{3,0,2,1:T(8,128)(2,1)S(1)} fusion(f32[27,128,128]{2,0,1:T(8,128)} %get-tuple-element.184, f32[27,3]{0,1:T(4,128)} %dynamic-slice_bitcast_fusion.2, f32[27,11]{0,1:T(8,128)S(1)} %get-tuple-element.187), kind=kOutput, calls=%fused_computation.6.clone.1 | convolution fusion | flops 175719296 | bytes 2852328 | tf_op jit(solution)/shard_map/while/body/eval_jaxpr/bjp,box->jxpo/dot_general | solution.py:81
  94.7 0.9 fusion.70
  95.7 0.8 fusion.71
  97.6 1.5 fusion.69
  99.8 1.0 reshape.451
  100.8 4.2 %fusion.68 = bf16[11,3,128,128]{3,0,2,1:T(8,128)(2,1)S(1)} fusion(f32[27,128,128]{2,0,1:T(8,128)} %get-tuple-element.184, f32[27,3]{0,1:T(4,128)} %dynamic-slice_bitcast_fusion.2, f32[27,11]{0,1:T(8,128)S(1)} %get-tuple-element.187), kind=kOutput, calls=%fused_computation.6.clone.1 | convolution fusion | flops 175719296 | bytes 2852328 | tf_op jit(solution)/shard_map/while/body/eval_jaxpr/bjp,box->jxpo/dot_general | solution.py:81
  105.4 0.9 fusion.70
  106.3 0.8 fusion.71
  108.3 1.5 fusion.69
  110.5 1.0 reshape.451
  111.5 4.2 %fusion.68 = bf16[11,3,128,128]{3,0,2,1:T(8,128)(2,1)S(1)} fusion(f32[27,128,128]{2,0,1:T(8,128)} %get-tuple-element.184, f32[27,3]{0,1:T(4,128)} %dynamic-slice_bitcast_fusion.2, f32[27,11]{0,1:T(8,128)S(1)} %get-tuple-element.187), kind=kOutput, calls=%fused_computation.6.clone.1 | convolution fusion | flops 175719296 | bytes 2852328 | tf_op jit(solution)/shard_map/while/body/eval_jaxpr/bjp,box->jxpo/dot_general | solution.py:81
  116.0 0.9 fusion.70
  117.0 0.8 fusion.71
  119.0 1.5 fusion.69
  121.2 1.0 reshape.451
  122.2 4.2 %fusion.68 = bf16[11,3,128,128]{3,0,2,1:T(8,128)(2,1)S(1)} fusion(f32[27,128,128]{2,0,1:T(8,128)} %get-tuple-element.184, f32[27,3]{0,1:T(4,128)} %dynamic-slice_bitcast_fusion.2, f32[27,11]{0,1:T(8,128)S(1)} %get-tuple-element.187), kind=kOutput, calls=%fused_computation.6.clone.1 | convolution fusion | flops 175719296 | bytes 2852328 | tf_op jit(solution)/shard_map/while/body/eval_jaxpr/bjp,box->jxpo/dot_general | solution.py:81
  126.7 0.9 fusion.70
  127.7 0.8 fusion.71
  129.7 1.5 fusion.69
  131.9 1.0 reshape.451
  132.8 4.2 %fusion.68 = bf16[11,3,128,128]{3,0,2,1:T(8,128)(2,1)S(1)} fusion(f32[27,128,128]{2,0,1:T(8,128)} %get-tuple-element.184, f32[27,3]{0,1:T(4,128)} %dynamic-slice_bitcast_fusion.2, f32[27,11]{0,1:T(8,128)S(1)} %get-tuple-element.187), kind=kOutput, calls=%fused_computation.6.clone.1 | convolution fusion | flops 175719296 | bytes 2852328 | tf_op jit(solution)/shard_map/while/body/eval_jaxpr/bjp,box->jxpo/dot_general | solution.py:81
  137.4 0.9 fusion.70
  139.2 5.7 %scatter_custom_fusion.1 = bf16[256,4096]{1,0:T(8,128)(2,1)} fusion(s32[128]{0:T(128)} %copy-done.12, f32[16,8,32,128]{3,2,1,0:T(8,128)} %bitcast.141, bf16[]{:T(256)} %constant.93.clone.1), kind=kCustom, calls=%fused_computation.38 | custom fusion | bytes 4194816 | tf_op jit(solution)/shard_map/scatter | solution.py:115
  144.9 6.2 %all-to-all-start.1 = ((bf16[16,16,4096]{2,1,0:T(8,128)(2,1)}), bf16[16,16,4096]{2,1,0:T(8,128)(2,1)}, u32[]{:S(2)}, u32[]{:S(2)}) async-start(bf16[16,16,4096]{2,1,0:T(8,128)(2,1)} %bitcast.7), calls=%async_computation.1 | async-start | bytes 4194304 | tf_op jit(solution)/shard_map/all_to_all | solution.py:120
  151.3 0.8 convert_reduce_fusion.1
  152.1 40.0 %all-to-all-done.1 = bf16[16,16,4096]{2,1,0:T(8,128)(2,1)} async-done(((bf16[16,16,4096]{2,1,0:T(8,128)(2,1)}), bf16[16,16,4096]{2,1,0:T(8,128)(2,1)}, u32[]{:S(2)}, u32[]{:S(2)}) %all-to-all-start.1) | async-done | bytes 2097184 | tf_op jit(solution)/shard_map/all_to_all | solution.py:120
  192.1 2.0 fusion.27
  194.8 28.4 %all-gather = bf16[16,4,4096]{2,1,0:T(4,128)(2,1)S(1)} all-gather(bf16[1,4,4096]{2,1,0:T(4,128)(2,1)S(1)} %bitcast.145), channel_id=1, replica_groups=mesh['groups'=2,'band'=16] {'band'}, dimensions={0}, use_global_device_ids=true | all-gather | bytes 557056 | tf_op jit(solution)/shard_map/all_gather | solution.py:152
  223.4 1.5 fusion.28
  224.8 1.7 copy.65
  (189 shorter events, 43.7 us)
Async XLA Ops:
  1.4 3.2 %copy-start.7 = (s32[128]{0:T(128)}, s32[128]{0:T(128)S(1)}, u32[]{:S(2)}) copy-start(s32[128]{0:T(128)S(1)} %reshape_squeeze.7) | copy-start | bytes 1540
  4.2 0.5 copy-start.10
  4.7 11.1 %copy-start.12 = (s32[128]{0:T(128)}, s32[128]{0:T(128)S(1)}, u32[]{:S(2)}) copy-start(s32[128]{0:T(128)S(1)} %fusion.46) | copy-start | bytes 1540
  6.4 138.5 %all-to-all-start = ((bf16[16,16,4]{1,2,0:T(4,128)(2,1)}), bf16[16,16,4]{1,2,0:T(4,128)(2,1)}, u32[]{:S(2)}, u32[]{:S(2)}) async-start(bf16[16,16,4]{1,2,0:T(4,128)(2,1)} %copy.53), calls=%async_computation | async-start | bytes 32768 | tf_op jit(solution)/shard_map/all_to_all | solution.py:134
  51.4 2.4 %copy-start.1 = (f32[27,11]{0,1:T(8,128)S(1)}, f32[27,11]{0,1:T(8,128)}, u32[]{:S(2)}) copy-start(f32[27,11]{0,1:T(8,128)} %constant.97.clone..sunk.3) | copy-start | bytes 3568
  53.8 1.2 copy-start.2
  53.8 1.2 copy-start.5
  62.6 1.0 copy-start.4
  62.6 1.8 copy-start.3
  62.6 1.8 copy-start.6
  64.4 1.2 copy-start.2
  64.4 1.2 copy-start.5
  73.3 1.0 copy-start.4
  73.3 1.8 copy-start.3
  73.3 1.8 copy-start.6
  75.1 1.2 copy-start.2
  75.1 1.2 copy-start.5
  84.0 1.0 copy-start.4
  84.0 1.8 copy-start.3
  84.0 1.8 copy-start.6
  85.8 1.2 copy-start.2
  85.8 1.2 copy-start.5
  94.7 1.0 copy-start.4
  94.7 1.8 copy-start.3
  94.7 1.8 copy-start.6
  96.5 1.2 copy-start.2
  96.5 1.2 copy-start.5
  105.3 1.0 copy-start.4
  105.3 1.8 copy-start.3
  105.4 1.8 copy-start.6
  107.1 1.2 copy-start.2
  107.1 1.2 copy-start.5
  116.0 1.0 copy-start.4
  116.0 1.8 copy-start.3
  116.0 1.8 copy-start.6
  117.8 1.2 copy-start.2
  117.8 1.2 copy-start.5
  126.7 1.0 copy-start.4
  126.7 1.8 copy-start.3
  126.7 1.8 copy-start.6
  128.5 1.2 copy-start.2
  128.5 1.2 copy-start.5
  137.4 1.0 copy-start.4
  137.4 1.8 copy-start.3
  137.4 1.8 copy-start.6
  144.9 6.2 %copy-start.9 = (f32[1,8]{1,0:T(1,128)S(1)}, f32[1,8]{1,0:T(1,128)}, u32[]{:S(2)}) copy-start(f32[1,8]{1,0:T(1,128)} %param.13) | copy-start | bytes 100
  144.9 6.3 %copy-start.8 = (s32[128]{0:T(128)S(1)}, s32[128]{0:T(128)}, u32[]{:S(2)}) copy-start(s32[128]{0:T(128)} %copy-done.7) | copy-start | bytes 1540
  144.9 6.3 %copy-start.11 = (s32[128]{0:T(128)S(1)}, s32[128]{0:T(128)}, u32[]{:S(2)}) copy-start(s32[128]{0:T(128)} %copy-done.10) | copy-start | bytes 1540
  144.9 47.2 %all-to-all-start.1 = ((bf16[16,16,4096]{2,1,0:T(8,128)(2,1)}), bf16[16,16,4096]{2,1,0:T(8,128)(2,1)}, u32[]{:S(2)}, u32[]{:S(2)}) async-start(bf16[16,16,4096]{2,1,0:T(8,128)(2,1)} %bitcast.7), calls=%async_computation.1 | async-start | bytes 4194304 | tf_op jit(solution)/shard_map/all_to_all | solution.py:120
  152.1 71.2 %copy-start = (f32[8,16,32,128]{3,2,1,0:T(8,128)S(1)}, f32[8,16,32,128]{3,2,1,0:T(8,128)}, u32[]{:S(2)}) copy-start(f32[8,16,32,128]{3,2,1,0:T(8,128)} %get-tuple-element.49) | copy-start | bytes 6291460
where the time goes:
time: 228 us; the launch traced here: 227 us
  matrix products  56.5 us (25%)
  other arithmetic  51.1 us (22%)
  waiting for transfers between devices  40 us (18%)
  local copies, waits for them, and re-layouts  35.3 us (15%)
  blocking collectives  28.4 us (12%)
  starting transfers between devices  13.6 us (6%)
    all_to_all x1, waiting for transfers between devices, body(): lax.all_to_all(outgoing.reshape(band_count, capacity, pixel_count), 'band...  40 us
    unnamed x38, other arithmetic  34 us
    dot_general x8, matrix products, one_epoch(): jnp.einsum('bjp,box->jxpo', mixing, column_stack, precision=lax.Precision...  33.7 us
    all_gather x1, blocking collectives, body(): shard_rows = lax.all_gather(templates, 'band', axis=0, tiled=True)  28.4 us
    dot_general x8, matrix products, one_epoch(): jnp.einsum('jpy,tyx->tpjx', row_tables, pixels, preferred_element_type=jn...  11.7 us
    reshape x8, local copies, waits for them, and re-layouts, one_epoch(): flat = rowed.reshape(per_epoch, tile_rows, row_count * tile_side)  7.69 us
    dot_general x8, matrix products, one_epoch(): jnp.einsum('tpk,kq->tpq', flat, mixer, preferred_element_type=jnp.float32)  7.57 us
    all_to_all x1, starting transfers between devices, body(): lax.all_to_all(out_weight.reshape(band_count, capacity, PD), 'band', spli...  7.46 us
  transfers between devices with their start and end apart: 2, of which 1 were waited for; matrix products, arithmetic and copies ran while one was open for 58% of the time, Pallas kernels for 0%

commit v1 on v0

v1 whole, which is shorter than its diff:
```python
import functools

import jax
import jax.numpy as jnp
import numpy as np
from jax import lax
from jax.experimental import pallas as pl
from jax.experimental.pallas import tpu as pltpu
from jax.sharding import PartitionSpec as P

PD = 4
HALF = 9
P_SIZE = 3

sigmas = (0.75, 1.5, 3.0)
degrees = (4, 2, 2)

BF16 = jnp.bfloat16
F32 = jnp.float32
EXTRA = 16


def kernel_matrices(tile_side):
    place = np.arange(tile_side)
    apart = place[:, None] - place[None, :]
    offset = apart.astype(np.float32)
    inside = (np.abs(apart) <= HALF).astype(np.float32)
    taps = np.arange(-HALF, HALF + 1).astype(np.float32)
    tables = []
    for width_sigma, degree in zip(sigmas, degrees):
        scale = np.float32(2.0 * width_sigma * width_sigma)
        total = np.sum(np.exp(-taps * taps / scale), dtype=np.float32)
        envelope = np.exp(-offset * offset / scale) * inside / total
        for power in range(degree + 1):
            tables.append((envelope * (offset / np.float32(width_sigma)) ** power).astype(np.float32))
    return np.stack(tables)


def basis_pairs():
    kernel_list = []
    base_index = 0
    for degree in degrees:
        for column_power in range(degree + 1):
            for row_power in range(degree + 1 - column_power):
                kernel_list.append((base_index + row_power, base_index + column_power))
        base_index = base_index + degree + 1
    return kernel_list


def stage_factors(band_count):
    factors = []
    rest = band_count
    if rest >= 2:
        factors.append(2)
        rest //= 2
    inner = 1
    while 4 * inner * inner <= rest:
        inner *= 2
    for factor in (inner, rest // inner):
        if factor > 1:
            factors.append(factor)
    return factors


def place_of(distance, factors):
    total = int(np.prod(factors))
    place = 0
    for factor in factors:
        total //= factor
        place = place + (distance % factor) * total
        distance = distance // factor
    return place


def smooth_kernel(
    me_ref, coef_ref, weight_ref, valid_ref, owner_ref, local_ref,
    image_ref, column_ref, row_ref, patch_row_ref, weight_row_ref,
    smooth_ref, *rest, factors, band_count, row_count,
):
    message_refs = rest[: factors[0]]
    mixer_ref, flat_ref, total_ref = rest[factors[0]:]
    epoch = pl.program_id(0)
    per_epoch, tile_rows, tile_side = image_ref.shape[1:]
    pairs = basis_pairs()

    @pl.when(epoch == 0)
    def _():
        total_ref[...] = jnp.zeros_like(total_ref)

    band_rows = 16
    for top in range(0, tile_side, band_rows):
        columns = [column_ref[c, top:top + band_rows, :] for c in range(row_count)]
        for r in range(row_count):
            used = [(b, pair[1]) for b, pair in enumerate(pairs) if pair[0] == r]
            for m in range(P_SIZE):
                value = None
                for b, c in used:
                    term = coef_ref[epoch, b * P_SIZE + m] * columns[c]
                    value = term if value is None else value + term
                mixer_ref[r * tile_side + top:r * tile_side + top + band_rows,
                          m * tile_side:(m + 1) * tile_side] = value.astype(BF16)

    for t in range(0, per_epoch, 2):
        pixels = jnp.concatenate([image_ref[0, t].astype(BF16), image_ref[0, t + 1].astype(BF16)], axis=1)
        rowed = jnp.dot(row_ref[...], pixels, preferred_element_type=F32).astype(BF16)
        for s in range(2):
            for r in range(row_count):
                flat_ref[(t + s) * tile_rows:(t + s + 1) * tile_rows,
                         r * tile_side:(r + 1) * tile_side] = (
                    rowed[r * tile_rows:(r + 1) * tile_rows, s * tile_side:(s + 1) * tile_side])

    spatial = jnp.dot(flat_ref[...], mixer_ref[...], preferred_element_type=F32)
    column = lax.broadcasted_iota(jnp.int32, (tile_rows, tile_side), 1).astype(F32)
    row = lax.broadcasted_iota(jnp.int32, (tile_rows, tile_side), 0).astype(F32)
    down = 2.0 * (row + 0.5) / tile_rows - 1.0
    weight = jnp.full((tile_rows, tile_side), weight_ref[0, epoch] * valid_ref[0, epoch].astype(F32), F32)
    weight = weight.astype(BF16).astype(F32)
    for t in range(per_epoch):
        across = 2.0 * (column + (t * tile_side + 0.5)) / (per_epoch * tile_side) - 1.0
        part = spatial[t * tile_rows:(t + 1) * tile_rows]
        value = (part[:, :tile_side] + across * part[:, tile_side:2 * tile_side]
                 + down * part[:, 2 * tile_side:])
        smooth_ref[0, t] = value
        place = place_of(owner_ref[epoch, t] ^ me_ref[0], factors) * PD + local_ref[epoch, t]
        total_ref[place] = total_ref[place] + weight * value.astype(BF16).astype(F32)

    @pl.when(epoch == pl.num_programs(0) - 1)
    def _():
        per_group = band_count // factors[0]
        lane_patch = patch_row_ref[...]
        lane_weight = weight_row_ref[...]
        line = lax.broadcasted_iota(jnp.int32, (EXTRA, lane_patch.shape[1]), 0)
        for g in range(factors[0]):
            @pl.loop(0, per_group)
            def _(i):
                block = g * per_group + i
                for q in range(PD):
                    message_refs[g][i, q * tile_rows:(q + 1) * tile_rows, :] = total_ref[block * PD + q].astype(BF16)
                named = (line < PD) & (lane_patch == block * PD + line)
                marks = jnp.where(named, lane_weight, 0.0)
                folded = marks[:, :tile_side]
                for k in range(1, marks.shape[1] // tile_side):
                    folded = folded + marks[:, k * tile_side:(k + 1) * tile_side]
                message_refs[g][i, PD * tile_rows:, :] = folded.astype(BF16)


def smooth(me, coeffs, weights, valid_epoch, owners, locals_, images, patch_row, weight_row, factors, band_count):
    _, epochs, per_epoch, tile_rows, tile_side = images.shape
    columns = np.ascontiguousarray(kernel_matrices(tile_side).transpose(0, 2, 1))
    row_count = columns.shape[0]
    rows = jnp.asarray(kernel_matrices(tile_rows).reshape(row_count * tile_rows, tile_rows), BF16)
    block_rows = PD * tile_rows + EXTRA
    per_group = band_count // factors[0]
    smem = pl.BlockSpec(memory_space=pltpu.SMEM)
    tile_block = pl.BlockSpec((1, per_epoch, tile_rows, tile_side), lambda e: (e, 0, 0, 0))

    def whole(shape):
        return pl.BlockSpec(shape, lambda e: (0,) * len(shape), pipeline_mode=pl.Buffered(1))

    message = jax.ShapeDtypeStruct((per_group, block_rows, tile_side), BF16)
    return pl.pallas_call(
        functools.partial(smooth_kernel, factors=factors, band_count=band_count, row_count=row_count),
        grid=(epochs,),
        in_specs=[smem] * 6 + [
            tile_block, whole(columns.shape), whole(rows.shape), whole(patch_row.shape), whole(weight_row.shape),
        ],
        out_specs=[tile_block] + [pl.BlockSpec(message.shape, lambda e: (0, 0, 0))] * factors[0],
        out_shape=[jax.ShapeDtypeStruct(images.shape[1:], F32)] + [message] * factors[0],
        scratch_shapes=[
            pltpu.VMEM((row_count * tile_side, P_SIZE * tile_side), BF16),
            pltpu.VMEM((per_epoch * tile_rows, row_count * tile_side), BF16),
            pltpu.VMEM((band_count * PD, tile_rows, tile_side), F32),
        ],
        compiler_params=pltpu.CompilerParams(
            dimension_semantics=("arbitrary",), vmem_limit_bytes=40 * 1024 * 1024),
        name="smooth",
    )(me, coeffs, weights, valid_epoch, owners, locals_, images[0], jnp.asarray(columns), rows, patch_row, weight_row)


def add_kernel(*refs, count, groups):
    parts, outs = refs[:count], refs[count:]
    per_group = outs[0].shape[0]
    for g in range(groups):
        @pl.loop(0, per_group)
        def _(i):
            total = parts[0][g * per_group + i].astype(F32)
            for part in parts[1:]:
                total = total + part[g * per_group + i].astype(F32)
            outs[g][i] = total.astype(BF16)


def add_and_split(parts, groups):
    blocks, block_rows, lanes = parts[0].shape
    out = jax.ShapeDtypeStruct((blocks // groups, block_rows, lanes), BF16)
    return pl.pallas_call(
        functools.partial(add_kernel, count=len(parts), groups=groups),
        out_shape=[out] * groups, name="add_and_split",
    )(*parts)


def finish_kernel(*refs, tile_rows):
    parts, out_ref = refs[:-1], refs[-1]
    total = parts[0][0].astype(F32)
    for part in parts[1:]:
        total = total + part[0].astype(F32)
    for q in range(PD):
        mass = jnp.sum(total[PD * tile_rows + q:PD * tile_rows + q + 1, :], axis=1, keepdims=True)
        out_ref[q] = (total[q * tile_rows:(q + 1) * tile_rows] / (1.0 + mass)).astype(BF16)


def finish(parts, tile_rows):
    lanes = parts[0].shape[2]
    return pl.pallas_call(
        functools.partial(finish_kernel, tile_rows=tile_rows),
        out_shape=jax.ShapeDtypeStruct((PD, tile_rows, lanes), BF16), name="finish",
    )(*parts)


def difference_kernel(me_ref, scale_ref, owner_ref, local_ref, table_ref, smooth_ref, out_ref, *, factors):
    epoch = pl.program_id(0)
    scale = scale_ref[0, epoch]
    for t in range(smooth_ref.shape[1]):
        place = place_of(owner_ref[epoch, t] ^ me_ref[0], factors) * PD + local_ref[epoch, t]
        out_ref[0, t] = smooth_ref[0, t] - scale * table_ref[place].astype(F32)


def subtract(me, scales, owners, locals_, table, smoothed, factors):
    epochs, per_epoch, tile_rows, tile_side = smoothed.shape
    smem = pl.BlockSpec(memory_space=pltpu.SMEM)
    tile_block = pl.BlockSpec((1, per_epoch, tile_rows, tile_side), lambda e: (e, 0, 0, 0))
    return pl.pallas_call(
        functools.partial(difference_kernel, factors=factors),
        grid=(epochs,),
        in_specs=[smem] * 4 + [
            pl.BlockSpec(table.shape, lambda e: (0, 0, 0), pipeline_mode=pl.Buffered(1)), tile_block],
        out_specs=tile_block,
        out_shape=jax.ShapeDtypeStruct(smoothed.shape, F32),
        compiler_params=pltpu.CompilerParams(dimension_semantics=("arbitrary",)),
        name="subtract",
    )(me, scales, owners, locals_, table, smoothed)


def body(images, coeffs, weights, scales, valid_epoch, patch_owner, patch_local):
    band_count = lax.axis_size("band")
    _, epochs, per_epoch, tile_rows, tile_side = images.shape
    tile_count = epochs * per_epoch
    factors = stage_factors(band_count)
    me = lax.axis_index("band").astype(jnp.int32).reshape(1)
    owners = patch_owner.reshape(epochs, per_epoch)
    locals_ = patch_local.reshape(epochs, per_epoch)
    flat_coeffs = coeffs.reshape(epochs, -1)
    patch_row = (place_of(owners ^ me[0], factors) * PD + locals_).reshape(1, tile_count)
    weight_row = jnp.broadcast_to(
        (weights[0] * valid_epoch[0].astype(F32)).astype(BF16).astype(F32)[:, None], (epochs, per_epoch)
    ).reshape(1, tile_count)

    smoothed, *blocks = smooth(
        me, flat_coeffs, weights, valid_epoch, owners, locals_, images, patch_row, weight_row, factors, band_count)

    def exchange(value, step):
        return lax.ppermute(value, "band", [(d, d ^ step) for d in range(band_count)])

    stride = 1
    strides = []
    for k, factor in enumerate(factors):
        strides.append(stride)
        parts = [blocks[0]] + [exchange(blocks[j], j * stride) for j in range(1, factor)]
        stride *= factor
        if k + 1 < len(factors):
            blocks = add_and_split(parts, factors[k + 1])
    templates = finish(parts, tile_rows)

    table = templates
    for factor, stride in zip(reversed(factors), reversed(strides)):
        table = jnp.concatenate([table] + [exchange(table, j * stride) for j in range(1, factor)], axis=0)

    difference = subtract(me, scales, owners, locals_, table, smoothed, factors)
    return difference[None], templates


def solution(mesh):
    return jax.shard_map(
        body,
        mesh=mesh,
        in_specs=(
            P(("groups", "band"), None, None, None, None),
            P(("groups", "band"), None, None, None),
            P(("groups", "band"), None),
            P(("groups", "band"), None),
            P(("groups", "band"), None),
            P(("groups", "band"), None, None, None),
            P(("groups", "band"), None, None),
        ),
        out_specs=(
            P(("groups", "band"), None, None, None, None),
            P(("groups", "band"), None, None),
        ),
        check_vma=False,
    )
```

time: 228 us -> 74.6 us (0.33)
  matrix products: 56.5 us -> 0 us
  other arithmetic: 51.1 us -> 2.19 us
  blocking collectives: 28.4 us -> 0 us
  Pallas kernels: 0 us -> 25.4 us
  waiting for transfers between devices: 40 us -> 17.8 us
  local copies, waits for them, and re-layouts: 35.3 us -> 14 us
    dot_general x26 -> x0, matrix products: 56.5 us -> none  [the longest x8 33.7 us: one_epoch(): jnp.einsum('bjp,box->jxpo', mixing, column_stack, precision=lax.Precision...]
    all_to_all x2 -> x0, waiting for transfers between devices: 40 us -> none  [the longest x1 40 us: body(): lax.all_to_all(outgoing.reshape(band_count, capacity, pixel_count), 'band...]
    unnamed x38 -> x0, other arithmetic: 34 us -> none
    all_gather x1 -> x0, blocking collectives: 28.4 us -> none  [body(): shard_rows = lax.all_gather(templates, 'band', axis=0, tiled=True)]
    pallas_call x0 -> x5, Pallas kernels: none -> 25.4 us  [the longest x1 13.6 us: smooth(): pl.pallas_call(functools.partial(smooth_kernel, factors=factors, band_cou...]
    ppermute x0 -> x10, waiting for transfers between devices: none -> 17.8 us  [exchange(): lax.ppermute(value, 'band', [(d, d ^ step) for d in range(band_count)])]
    ppermute x0 -> x10, starting transfers between devices: none -> 13.8 us  [exchange(): lax.ppermute(value, 'band', [(d, d ^ step) for d in range(band_count)])]
    all_to_all x2 -> x0, starting transfers between devices: 13.6 us -> none  [the longest x1 7.46 us: body(): lax.all_to_all(out_weight.reshape(band_count, capacity, PD), 'band', spli...]
  transfers between devices with their start and end apart: 2 -> 10, of which waited for: 1 -> 8; matrix products, arithmetic and copies ran while one was open for 58% -> 1% of each run, Pallas kernels for 0% -> 0%
where the time goes in v1:
time: 74.6 us; the launch traced here: 73.8 us
  Pallas kernels  25.4 us (34%)
  waiting for transfers between devices  17.8 us (24%)
  local copies, waits for them, and re-layouts  14 us (19%)
  starting transfers between devices  13.8 us (18%)
  other arithmetic  2.19 us (3%)
    ppermute x10, waiting for transfers between devices, exchange(): lax.ppermute(value, 'band', [(d, d ^ step) for d in range(band_count)])  17.8 us
    ppermute x10, starting transfers between devices, exchange(): lax.ppermute(value, 'band', [(d, d ^ step) for d in range(band_count)])  13.8 us
    pallas_call x1, Pallas kernels, smooth(): pl.pallas_call(functools.partial(smooth_kernel, factors=factors, band_cou...  13.6 us
    unnamed x35, local copies, waits for them, and re-layouts  12.8 us
    pallas_call x1, Pallas kernels, subtract(): pl.pallas_call(functools.partial(difference_kernel, factors=factors), gri...  6.73 us
    pallas_call x2, Pallas kernels, add_and_split(): pl.pallas_call(functools.partial(add_kernel, count=len(parts), groups=gro...  3.52 us
    pallas_call x1, Pallas kernels, finish(): pl.pallas_call(functools.partial(finish_kernel, tile_rows=tile_rows), out...  1.53 us
  transfers between devices with their start and end apart: 10, of which 8 were waited for; matrix products, arithmetic and copies ran while one was open for 1% of the time, Pallas kernels for 0%

profile of v1, /device:TPU:0, one launch (start us, length us, event | category | flops | bytes accessed | tf_op | source)
XLA Modules:
  0.0 73.8 jit_solution(14341017368442699518)
XLA Ops:
  0.6 0.8 %reshape.241 = s32[1,128]{1,0:T(1,128)S(1)} reshape(s32[1,8,16]{2,1,0:T(8,128)} %param.15) | data formatting | bytes 1024 | tf_op jit(solution)/shard_map/reshape | solution.py:250
  1.4 0.7 bitcast_convert_fusion
  2.1 0.1 broadcast_in_dim.4
  2.2 0.1 reshape.242.weight_row_ref
  2.2 0.7 xor_reduce_fusion
  2.9 0.1 xor.18
  3.0 0.8 %copy.12 = f32[1,8,27,3]{1,3,2,0:T(4,128)S(1)} copy(f32[1,8,27,3]{2,1,3,0:T(8,128)} %param.10) | data formatting | bytes 5184 | tf_op args[1]
  3.9 0.1 copy.13.coef_ref
  4.0 0.0 copy-start
  4.0 1.6 %copy-done = f32[1,8,16,32,128]{4,3,2,1,0:T(8,128)S(1)} copy-done((f32[1,8,16,32,128]{4,3,2,1,0:T(8,128)S(1)}, f32[1,8,16,32,128]{4,3,2,1,0:T(8,128)}, u32[]{:S(2)}) %copy-start) | copy-done | bytes 2097176
  5.6 0.0 copy-start.2
  5.6 1.1 %copy-done.2 = f32[11,128,128]{2,1,0:T(8,128)S(1)} copy-done((f32[11,128,128]{2,1,0:T(8,128)S(1)}, f32[11,128,128]{2,1,0:T(8,128)}, u32[]{:S(2)}) %copy-start.2) | copy-done | bytes 720920
  6.7 0.0 copy-start.4
  6.7 0.9 %copy-done.4 = bf16[352,32]{1,0:T(8,128)(2,1)S(1)} copy-done((bf16[352,32]{1,0:T(8,128)(2,1)S(1)}, bf16[352,32]{1,0:T(8,128)(2,1)}, u32[]{:S(2)}) %copy-start.4) | copy-done | bytes 22552
  7.6 0.0 copy-start.5
  7.6 0.7 copy-done.5
  8.3 0.0 copy-start.6
  8.3 0.7 copy-done.6
  8.9 0.0 copy-start.7
  8.9 0.7 copy-done.7
  9.6 0.0 copy-start.8
  9.6 0.7 copy-done.8
  10.2 13.6 %smooth.1 = (f32[8,16,32,128]{3,2,1,0:T(8,128)S(1)}, bf16[8,144,128]{2,1,0:T(8,128)(2,1)S(1)}, bf16[8,144,128]{2,1,0:T(8,128)(2,1)S(1)}) custom-call(s32[1]{0:T(128)} %bitcast.me_ref, f32[8,81]{1,0:T(8,128)S(1)} %copy.13.coef_ref, f32[1,8]{1,0:T(1,128)S(1)} %copy-done.7, s32[1,8]{1,0:T(1,128)S(1)} %copy-done.8, s32[8,16]{1,0:T(8,128)S(1)} %bitcast.12, ...), custom_call_target="tpu_custom_call" | custom-call | tf_op jit(solution)/shard_map/smooth/pallas_call | solution.py:161
  23.8 0.0 copy-start.1
  23.8 1.3 %copy-done.1 = f32[8,16,32,128]{3,2,1,0:T(8,128)} copy-done((f32[8,16,32,128]{3,2,1,0:T(8,128)}, f32[8,16,32,128]{3,2,1,0:T(8,128)S(1)}, u32[]{:S(2)}) %copy-start.1) | copy-done | bytes 2097176
  25.2 0.0 copy-start.3
  25.2 0.7 copy-done.3
  25.9 0.5 collective-permute-start
  26.4 1.2 %collective-permute-done.refs_1_ = bf16[8,144,128]{2,1,0:T(8,128)(2,1)S(1)} collective-permute-done((bf16[8,144,128]{2,1,0:T(8,128)(2,1)S(1)}, bf16[8,144,128]{2,1,0:T(8,128)(2,1)S(1)}, u32[]{:S(2)}, u32[]{:S(2)}) %collective-permute-start) | collective-permute-done | bytes 294944 | tf_op jit(solution)/shard_map/ppermute | solution.py:261
  27.6 0.7 copy-done.10
  28.3 1.9 %add_and_split.2 = (bf16[4,144,128]{2,1,0:T(8,128)(2,1)}, bf16[4,144,128]{2,1,0:T(8,128)(2,1)}) custom-call(bf16[8,144,128]{2,1,0:T(8,128)(2,1)} %copy-done.3, bf16[8,144,128]{2,1,0:T(8,128)(2,1)} %copy-done.10), custom_call_target="tpu_custom_call" | custom-call | tf_op jit(solution)/shard_map/add_and_split/pallas_call | solution.py:195
  30.2 2.9 %collective-permute-start.1 = (bf16[4,144,128]{2,1,0:T(8,128)(2,1)}, bf16[4,144,128]{2,1,0:T(8,128)(2,1)S(1)}, u32[]{:S(2)}, u32[]{:S(2)}) collective-permute-start(bf16[4,144,128]{2,1,0:T(8,128)(2,1)} %get-tuple-element.14), channel_id=1, source_target_pairs={{0,2},{1,3},{2,0},{3,1},{4,6},{5,7},{6,4},{7,5},{8,10},{9,11},{10,... | collective-permute-start | bytes 442376 | tf_op jit(solution)/shard_map/ppermute | solution.py:261
  33.1 4.4 %collective-permute-done.1.refs_1_ = bf16[4,144,128]{2,1,0:T(8,128)(2,1)S(1)} collective-permute-done((bf16[4,144,128]{2,1,0:T(8,128)(2,1)}, bf16[4,144,128]{2,1,0:T(8,128)(2,1)S(1)}, u32[]{:S(2)}, u32[]{:S(2)}) %collective-permute-start.1) | collective-permute-done | bytes 147488 | tf_op jit(solution)/shard_map/ppermute | solution.py:261
  37.4 0.0 copy-start.11
  37.4 0.7 copy-done.11
  38.1 1.6 %add_and_split.3 = (bf16[1,144,128]{2,1,0:T(8,128)(2,1)}, bf16[1,144,128]{2,1,0:T(8,128)(2,1)}, bf16[1,144,128]{2,1,0:T(8,128)(2,1)}, bf16[1,144,128]{2,1,0:T(8,128)(2,1)}) custom-call(bf16[4,144,128]{2,1,0:T(8,128)(2,1)} %get-tuple-element.13.refs_0_, bf16[4,144,128]{2,1,0:T(8,128)(2,1)} %copy-done.11), custom_call_target="tpu_custom_call" | custom-call | tf_op jit(solution)/shard_map/add_and_split/pallas_call | solution.py:195
  39.7 1.8 %collective-permute-start.2 = (bf16[1,144,128]{2,1,0:T(8,128)(2,1)}, bf16[1,144,128]{2,1,0:T(8,128)(2,1)S(1)}, u32[]{:S(2)}, u32[]{:S(2)}) collective-permute-start(bf16[1,144,128]{2,1,0:T(8,128)(2,1)} %get-tuple-element.16), channel_id=1, source_target_pairs={{0,4},{1,5},{2,6},{3,7},{4,0},{5,1},{6,2},{7,3},{8,12},{9,13},{10,... | collective-permute-start | bytes 110600 | tf_op jit(solution)/shard_map/ppermute | solution.py:261
  41.5 2.6 %collective-permute-start.3 = (bf16[1,144,128]{2,1,0:T(8,128)(2,1)}, bf16[1,144,128]{2,1,0:T(8,128)(2,1)S(1)}, u32[]{:S(2)}, u32[]{:S(2)}) collective-permute-start(bf16[1,144,128]{2,1,0:T(8,128)(2,1)} %get-tuple-element.17), channel_id=1, source_target_pairs={{0,8},{1,9},{2,10},{3,11},{4,12},{5,13},{6,14},{7,15},{8,0},{9,1},... | collective-permute-start | bytes 110600 | tf_op jit(solution)/shard_map/ppermute | solution.py:261
  44.1 0.0 collective-permute-start.4
  44.1 0.0 collective-permute-done.2.refs_1_
  44.1 0.0 copy-start.12
  44.1 2.8 %collective-permute-done.3.refs_2_ = bf16[1,144,128]{2,1,0:T(8,128)(2,1)S(1)} collective-permute-done((bf16[1,144,128]{2,1,0:T(8,128)(2,1)}, bf16[1,144,128]{2,1,0:T(8,128)(2,1)S(1)}, u32[]{:S(2)}, u32[]{:S(2)}) %collective-permute-start.3) | collective-permute-done | bytes 36896 | tf_op jit(solution)/shard_map/ppermute | solution.py:261
  46.9 0.0 copy-start.13
  46.9 3.2 %collective-permute-done.4.refs_3_ = bf16[1,144,128]{2,1,0:T(8,128)(2,1)S(1)} collective-permute-done((bf16[1,144,128]{2,1,0:T(8,128)(2,1)}, bf16[1,144,128]{2,1,0:T(8,128)(2,1)S(1)}, u32[]{:S(2)}, u32[]{:S(2)}) %collective-permute-start.4) | collective-permute-done | bytes 36896 | tf_op jit(solution)/shard_map/ppermute | solution.py:261
  50.1 0.0 copy-done.12
  50.1 0.0 copy-done.13
  50.1 0.6 copy-done.14
  50.7 1.5 %finish.1 = bf16[4,32,128]{2,1,0:T(8,128)(2,1)} custom-call(bf16[1,144,128]{2,1,0:T(8,128)(2,1)} %get-tuple-element.15.refs_0_, bf16[1,144,128]{2,1,0:T(8,128)(2,1)} %copy-done.12, bf16[1,144,128]{2,1,0:T(8,128)(2,1)} %copy-done.13, bf16[1,144,128]{2,1,0:T(8,128)(2,1)} %copy-done.14), custom_call_target="tpu_custom_call" | custom-call | tf_op jit(solution)/shard_map/finish/pallas_call | solution.py:213
  52.2 0.4 collective-permute-start.7
  52.6 0.0 collective-permute-start.6
  52.6 4.0 %collective-permute-start.5 = (bf16[4,32,128]{2,1,0:T(8,128)(2,1)}, bf16[4,32,128]{2,1,0:T(8,128)(2,1)S(1)}, u32[]{:S(2)}, u32[]{:S(2)}) collective-permute-start(bf16[4,32,128]{2,1,0:T(8,128)(2,1)} %finish.1), channel_id=1, source_target_pairs={{0,4},{1,5},{2,6},{3,7},{4,0},{5,1},{6,2},{7,3},{8,12},{9,13},{10,... | collective-permute-start | bytes 98312 | tf_op jit(solution)/shard_map/ppermute | solution.py:261
  56.6 0.8 %constant_dynamic-update-slice_fusion.4 = (bf16[32,32,128]{2,1,0:T(8,128)(2,1)S(1)}, bf16[64,32,128]{2,1,0:T(8,128)(2,1)S(1)}) fusion(bf16[4,32,128]{2,1,0:T(8,128)(2,1)} %finish.1), kind=kLoop, calls=%fused_computation.5 | loop fusion | bytes 98304
  57.4 0.7 collective-permute-done.7
  58.1 0.0 collective-permute-done.6
  58.1 0.6 collective-permute-done.5
  58.7 0.8 %pad_maximum_fusion = bf16[16,32,128]{2,1,0:T(8,128)(2,1)S(1)} fusion(bf16[4,32,128]{2,1,0:T(8,128)(2,1)S(1)} %collective-permute-done.7, bf16[4,32,128]{2,1,0:T(8,128)(2,1)S(1)} %collective-permute-done.6, bf16[4,32,128]{2,1,0:T(8,128)(2,1)S(1)} %collective-permute-done.5, bf16[4,32,128]{2,1,0:T(8,128)(2,1)} %finish.1), kind=kLoop, calls=%fused_computation | loop fusion | flops 196608 | bytes 262144 | tf_op jit(solution)/shard_map/concatenate | solution.py:275
  59.5 1.6 %collective-permute-start.8 = (bf16[16,32,128]{2,1,0:T(8,128)(2,1)S(1)}, bf16[16,32,128]{2,1,0:T(8,128)(2,1)S(1)}, u32[]{:S(2)}, u32[]{:S(2)}) collective-permute-start(bf16[16,32,128]{2,1,0:T(8,128)(2,1)S(1)} %pad_maximum_fusion), channel_id=1, source_target_pairs={{0,2},{1,3},{2,0},{3,1},{4,6},{5,7},{6,4},{7,5},{8,10},{9,11},{10,... | collective-permute-start | bytes 393224 | tf_op jit(solution)/shard_map/ppermute | solution.py:261
  61.2 3.4 %collective-permute-done.8 = bf16[16,32,128]{2,1,0:T(8,128)(2,1)S(1)} collective-permute-done((bf16[16,32,128]{2,1,0:T(8,128)(2,1)S(1)}, bf16[16,32,128]{2,1,0:T(8,128)(2,1)S(1)}, u32[]{:S(2)}, u32[]{:S(2)}) %collective-permute-start.8) | collective-permute-done | bytes 131104 | tf_op jit(solution)/shard_map/ppermute | solution.py:261
  64.6 0.1 constant_dynamic-update-slice_fusion
  64.6 0.1 collective-permute-start.9
  64.7 1.5 %collective-permute-done.9 = bf16[32,32,128]{2,1,0:T(8,128)(2,1)S(1)} collective-permute-done((bf16[32,32,128]{2,1,0:T(8,128)(2,1)S(1)}, bf16[32,32,128]{2,1,0:T(8,128)(2,1)S(1)}, u32[]{:S(2)}, u32[]{:S(2)}) %collective-permute-start.9) | collective-permute-done | bytes 262176 | tf_op jit(solution)/shard_map/ppermute | solution.py:261
  66.3 0.0 copy-start.9
  66.3 0.8 %copy-done.9 = bf16[64,32,128]{2,1,0:T(8,128)(2,1)} copy-done((bf16[64,32,128]{2,1,0:T(8,128)(2,1)}, bf16[64,32,128]{2,1,0:T(8,128)(2,1)S(1)}, u32[]{:S(2)}) %copy-start.9) | copy-done | bytes 524312
  67.1 6.7 %subtract.1 = f32[8,16,32,128]{3,2,1,0:T(8,128)} custom-call(s32[1]{0:T(128)} %bitcast.me_ref, f32[1,8]{1,0:T(1,128)} %scale_ref.1, s32[8,16]{1,0:T(8,128)} %bitcast.11, s32[8,16]{1,0:T(8,128)} %bitcast.13, bf16[64,32,128]{2,1,0:T(8,128)(2,1)} %copy-done.9, f32[8,16,32,128]{3,2,1,0:T(8,128)} %copy-done.1), custom_call_target="tpu_custom_call" | custom-call | tf_op jit(solution)/shard_map/subtract/pallas_call | solution.py:231
  (8 shorter events, 0.2 us)
Async XLA Ops:
  4.0 1.6 %copy-start = (f32[1,8,16,32,128]{4,3,2,1,0:T(8,128)S(1)}, f32[1,8,16,32,128]{4,3,2,1,0:T(8,128)}, u32[]{:S(2)}) copy-start(f32[1,8,16,32,128]{4,3,2,1,0:T(8,128)} %param.9) | copy-start | bytes 6291460
  5.6 1.1 %copy-start.2 = (f32[11,128,128]{2,1,0:T(8,128)S(1)}, f32[11,128,128]{2,1,0:T(8,128)}, u32[]{:S(2)}) copy-start(f32[11,128,128]{2,1,0:T(8,128)} %constant.61.clone.column_ref) | copy-start | bytes 2162692
  6.7 0.9 %copy-start.4 = (bf16[352,32]{1,0:T(8,128)(2,1)S(1)}, bf16[352,32]{1,0:T(8,128)(2,1)}, u32[]{:S(2)}) copy-start(bf16[352,32]{1,0:T(8,128)(2,1)} %constant.60.clone.row_ref) | copy-start | bytes 67588
  7.6 0.7 copy-start.5
  8.3 0.7 copy-start.6
  8.9 0.7 copy-start.7
  9.6 0.7 copy-start.8
  23.8 1.4 %copy-start.1 = (f32[8,16,32,128]{3,2,1,0:T(8,128)}, f32[8,16,32,128]{3,2,1,0:T(8,128)S(1)}, u32[]{:S(2)}) copy-start(f32[8,16,32,128]{3,2,1,0:T(8,128)S(1)} %get-tuple-element.19.smooth_ref) | copy-start | bytes 6291460
  25.2 0.7 copy-start.3
  25.9 1.7 %collective-permute-start = (bf16[8,144,128]{2,1,0:T(8,128)(2,1)S(1)}, bf16[8,144,128]{2,1,0:T(8,128)(2,1)S(1)}, u32[]{:S(2)}, u32[]{:S(2)}) collective-permute-start(bf16[8,144,128]{2,1,0:T(8,128)(2,1)S(1)} %get-tuple-element.12), channel_id=1, source_target_pairs={{0,1},{1,0},{2,3},{3,2},{4,5},{5,4},{6,7},{7,6},{8,9},{9,8},{10,11... | collective-permute-start | bytes 884744 | tf_op jit(solution)/shard_map/ppermute | solution.py:261
  27.6 0.7 copy-start.10
  30.2 7.2 %collective-permute-start.1 = (bf16[4,144,128]{2,1,0:T(8,128)(2,1)}, bf16[4,144,128]{2,1,0:T(8,128)(2,1)S(1)}, u32[]{:S(2)}, u32[]{:S(2)}) collective-permute-start(bf16[4,144,128]{2,1,0:T(8,128)(2,1)} %get-tuple-element.14), channel_id=1, source_target_pairs={{0,2},{1,3},{2,0},{3,1},{4,6},{5,7},{6,4},{7,5},{8,10},{9,11},{10,... | collective-permute-start | bytes 442376 | tf_op jit(solution)/shard_map/ppermute | solution.py:261
  37.4 0.7 copy-start.11
  39.7 4.4 %collective-permute-start.2 = (bf16[1,144,128]{2,1,0:T(8,128)(2,1)}, bf16[1,144,128]{2,1,0:T(8,128)(2,1)S(1)}, u32[]{:S(2)}, u32[]{:S(2)}) collective-permute-start(bf16[1,144,128]{2,1,0:T(8,128)(2,1)} %get-tuple-element.16), channel_id=1, source_target_pairs={{0,4},{1,5},{2,6},{3,7},{4,0},{5,1},{6,2},{7,3},{8,12},{9,13},{10,... | collective-permute-start | bytes 110600 | tf_op jit(solution)/shard_map/ppermute | solution.py:261
  41.5 5.4 %collective-permute-start.3 = (bf16[1,144,128]{2,1,0:T(8,128)(2,1)}, bf16[1,144,128]{2,1,0:T(8,128)(2,1)S(1)}, u32[]{:S(2)}, u32[]{:S(2)}) collective-permute-start(bf16[1,144,128]{2,1,0:T(8,128)(2,1)} %get-tuple-element.17), channel_id=1, source_target_pairs={{0,8},{1,9},{2,10},{3,11},{4,12},{5,13},{6,14},{7,15},{8,0},{9,1},... | collective-permute-start | bytes 110600 | tf_op jit(solution)/shard_map/ppermute | solution.py:261
  44.1 6.0 %collective-permute-start.4 = (bf16[1,144,128]{2,1,0:T(8,128)(2,1)}, bf16[1,144,128]{2,1,0:T(8,128)(2,1)S(1)}, u32[]{:S(2)}, u32[]{:S(2)}) collective-permute-start(bf16[1,144,128]{2,1,0:T(8,128)(2,1)} %get-tuple-element.18), channel_id=1, source_target_pairs={{0,12},{1,13},{2,14},{3,15},{4,8},{5,9},{6,10},{7,11},{8,4},{9,5},... | collective-permute-start | bytes 110600 | tf_op jit(solution)/shard_map/ppermute | solution.py:261
  44.1 6.0 %copy-start.12 = (bf16[1,144,128]{2,1,0:T(8,128)(2,1)}, bf16[1,144,128]{2,1,0:T(8,128)(2,1)S(1)}, u32[]{:S(2)}) copy-start(bf16[1,144,128]{2,1,0:T(8,128)(2,1)S(1)} %collective-permute-done.2.refs_1_) | copy-start | bytes 110596
  46.9 3.2 %copy-start.13 = (bf16[1,144,128]{2,1,0:T(8,128)(2,1)}, bf16[1,144,128]{2,1,0:T(8,128)(2,1)S(1)}, u32[]{:S(2)}) copy-start(bf16[1,144,128]{2,1,0:T(8,128)(2,1)S(1)} %collective-permute-done.3.refs_2_) | copy-start | bytes 110596
  50.1 0.6 copy-start.14
  52.2 5.9 %collective-permute-start.7 = (bf16[4,32,128]{2,1,0:T(8,128)(2,1)}, bf16[4,32,128]{2,1,0:T(8,128)(2,1)S(1)}, u32[]{:S(2)}, u32[]{:S(2)}) collective-permute-start(bf16[4,32,128]{2,1,0:T(8,128)(2,1)} %finish.1), channel_id=1, source_target_pairs={{0,12},{1,13},{2,14},{3,15},{4,8},{5,9},{6,10},{7,11},{8,4},{9,5},... | collective-permute-start | bytes 98312 | tf_op jit(solution)/shard_map/ppermute | solution.py:261
  52.6 5.5 %collective-permute-start.6 = (bf16[4,32,128]{2,1,0:T(8,128)(2,1)}, bf16[4,32,128]{2,1,0:T(8,128)(2,1)S(1)}, u32[]{:S(2)}, u32[]{:S(2)}) collective-permute-start(bf16[4,32,128]{2,1,0:T(8,128)(2,1)} %finish.1), channel_id=1, source_target_pairs={{0,8},{1,9},{2,10},{3,11},{4,12},{5,13},{6,14},{7,15},{8,0},{9,1},... | collective-permute-start | bytes 98312 | tf_op jit(solution)/shard_map/ppermute | solution.py:261
  52.6 6.1 %collective-permute-start.5 = (bf16[4,32,128]{2,1,0:T(8,128)(2,1)}, bf16[4,32,128]{2,1,0:T(8,128)(2,1)S(1)}, u32[]{:S(2)}, u32[]{:S(2)}) collective-permute-start(bf16[4,32,128]{2,1,0:T(8,128)(2,1)} %finish.1), channel_id=1, source_target_pairs={{0,4},{1,5},{2,6},{3,7},{4,0},{5,1},{6,2},{7,3},{8,12},{9,13},{10,... | collective-permute-start | bytes 98312 | tf_op jit(solution)/shard_map/ppermute | solution.py:261
  59.5 5.0 %collective-permute-start.8 = (bf16[16,32,128]{2,1,0:T(8,128)(2,1)S(1)}, bf16[16,32,128]{2,1,0:T(8,128)(2,1)S(1)}, u32[]{:S(2)}, u32[]{:S(2)}) collective-permute-start(bf16[16,32,128]{2,1,0:T(8,128)(2,1)S(1)} %pad_maximum_fusion), channel_id=1, source_target_pairs={{0,2},{1,3},{2,0},{3,1},{4,6},{5,7},{6,4},{7,5},{8,10},{9,11},{10,... | collective-permute-start | bytes 393224 | tf_op jit(solution)/shard_map/ppermute | solution.py:261
  64.6 1.6 %collective-permute-start.9 = (bf16[32,32,128]{2,1,0:T(8,128)(2,1)S(1)}, bf16[32,32,128]{2,1,0:T(8,128)(2,1)S(1)}, u32[]{:S(2)}, u32[]{:S(2)}) collective-permute-start(bf16[32,32,128]{2,1,0:T(8,128)(2,1)S(1)} %get-tuple-element.20), channel_id=1, source_target_pairs={{0,1},{1,0},{2,3},{3,2},{4,5},{5,4},{6,7},{7,6},{8,9},{9,8},{10,11... | collective-permute-start | bytes 786440 | tf_op jit(solution)/shard_map/ppermute | solution.py:261
  66.3 0.8 %copy-start.9 = (bf16[64,32,128]{2,1,0:T(8,128)(2,1)}, bf16[64,32,128]{2,1,0:T(8,128)(2,1)S(1)}, u32[]{:S(2)}) copy-start(bf16[64,32,128]{2,1,0:T(8,128)(2,1)S(1)} %constant_dynamic-update-slice_fusion.5.table_ref) | copy-start | bytes 1572868

commit v2 on v1

--- a/solution.py
+++ b/solution.py
@@ -67,14 +67,13 @@
     place = 0
     for factor in factors:
         total //= factor
-        place = place + (distance % factor) * total
-        distance = distance // factor
+        place = place + (distance & (factor - 1)) * total
+        distance = distance >> (factor.bit_length() - 1)
     return place
 
 
 def smooth_kernel(
-    me_ref, coef_ref, weight_ref, valid_ref, owner_ref, local_ref,
-    image_ref, column_ref, row_ref, patch_row_ref, weight_row_ref,
+    me_ref, coef_ref, weight_ref, valid_ref, owner_ref, local_ref, image_ref, column_ref, row_ref,
     smooth_ref, *rest, factors, band_count, row_count,
 ):
     message_refs = rest[: factors[0]]
@@ -95,7 +94,7 @@
             for m in range(P_SIZE):
                 value = None
                 for b, c in used:
-                    term = coef_ref[epoch, b * P_SIZE + m] * columns[c]
+                    term = coef_ref[m, epoch, b] * columns[c]
                     value = term if value is None else value + term
                 mixer_ref[r * tile_side + top:r * tile_side + top + band_rows,
                           m * tile_side:(m + 1) * tile_side] = value.astype(BF16)
@@ -113,45 +112,48 @@
     column = lax.broadcasted_iota(jnp.int32, (tile_rows, tile_side), 1).astype(F32)
     row = lax.broadcasted_iota(jnp.int32, (tile_rows, tile_side), 0).astype(F32)
     down = 2.0 * (row + 0.5) / tile_rows - 1.0
-    weight = jnp.full((tile_rows, tile_side), weight_ref[0, epoch] * valid_ref[0, epoch].astype(F32), F32)
+    lane = lax.broadcasted_iota(jnp.int32, (8, tile_side), 1)
+    weight = jnp.full((8, tile_side), weight_ref[0, epoch] * valid_ref[0, epoch].astype(F32), F32)
     weight = weight.astype(BF16).astype(F32)
+    weights = jnp.concatenate([weight] * (tile_rows // 8), axis=0)
     for t in range(per_epoch):
         across = 2.0 * (column + (t * tile_side + 0.5)) / (per_epoch * tile_side) - 1.0
         part = spatial[t * tile_rows:(t + 1) * tile_rows]
         value = (part[:, :tile_side] + across * part[:, tile_side:2 * tile_side]
                  + down * part[:, 2 * tile_side:])
-        smooth_ref[0, t] = value
+        smooth_ref[epoch, t] = value
         place = place_of(owner_ref[epoch, t] ^ me_ref[0], factors) * PD + local_ref[epoch, t]
-        total_ref[place] = total_ref[place] + weight * value.astype(BF16).astype(F32)
+        total_ref[place, :tile_rows] = total_ref[place, :tile_rows] + weights * value.astype(BF16).astype(F32)
+        total_ref[place, tile_rows:] = total_ref[place, tile_rows:] + jnp.where(lane == t % tile_side, weight, 0.0)
 
     @pl.when(epoch == pl.num_programs(0) - 1)
     def _():
         per_group = band_count // factors[0]
-        lane_patch = patch_row_ref[...]
-        lane_weight = weight_row_ref[...]
-        line = lax.broadcasted_iota(jnp.int32, (EXTRA, lane_patch.shape[1]), 0)
+        line = lax.broadcasted_iota(jnp.int32, (8, tile_side), 0)
         for g in range(factors[0]):
             @pl.loop(0, per_group)
             def _(i):
-                block = g * per_group + i
+                block = (g * per_group + i) * PD
+                marks = jnp.zeros((8, tile_side), F32)
                 for q in range(PD):
-                    message_refs[g][i, q * tile_rows:(q + 1) * tile_rows, :] = total_ref[block * PD + q].astype(BF16)
-                named = (line < PD) & (lane_patch == block * PD + line)
-                marks = jnp.where(named, lane_weight, 0.0)
-                folded = marks[:, :tile_side]
-                for k in range(1, marks.shape[1] // tile_side):
-                    folded = folded + marks[:, k * tile_side:(k + 1) * tile_side]
-                message_refs[g][i, PD * tile_rows:, :] = folded.astype(BF16)
-
-
-def smooth(me, coeffs, weights, valid_epoch, owners, locals_, images, patch_row, weight_row, factors, band_count):
-    _, epochs, per_epoch, tile_rows, tile_side = images.shape
+                    message_refs[g][i, q * tile_rows:(q + 1) * tile_rows, :] = (
+                        total_ref[block + q, :tile_rows].astype(BF16))
+                    marks = jnp.where(line == q, total_ref[block + q, tile_rows:], marks)
+                message_refs[g][i, PD * tile_rows:, :] = (
+                    jnp.concatenate([marks, jnp.zeros((EXTRA - 8, tile_side), F32)], axis=0).astype(BF16))
+
+
+VMEM = pl.BlockSpec(memory_space=pltpu.VMEM)
+SMEM = pl.BlockSpec(memory_space=pltpu.SMEM)
+
+
+def smooth(me, coeffs, weights, valid_epoch, owners, locals_, images, factors, band_count):
+    epochs, per_epoch, tile_rows, tile_side = images.shape
     columns = np.ascontiguousarray(kernel_matrices(tile_side).transpose(0, 2, 1))
     row_count = columns.shape[0]
     rows = jnp.asarray(kernel_matrices(tile_rows).reshape(row_count * tile_rows, tile_rows), BF16)
     block_rows = PD * tile_rows + EXTRA
     per_group = band_count // factors[0]
-    smem = pl.BlockSpec(memory_space=pltpu.SMEM)
     tile_block = pl.BlockSpec((1, per_epoch, tile_rows, tile_side), lambda e: (e, 0, 0, 0))
 
     def whole(shape):
@@ -161,28 +163,26 @@
     return pl.pallas_call(
         functools.partial(smooth_kernel, factors=factors, band_count=band_count, row_count=row_count),
         grid=(epochs,),
-        in_specs=[smem] * 6 + [
-            tile_block, whole(columns.shape), whole(rows.shape), whole(patch_row.shape), whole(weight_row.shape),
-        ],
-        out_specs=[tile_block] + [pl.BlockSpec(message.shape, lambda e: (0, 0, 0))] * factors[0],
-        out_shape=[jax.ShapeDtypeStruct(images.shape[1:], F32)] + [message] * factors[0],
+        in_specs=[SMEM] * 6 + [tile_block, whole(columns.shape), whole(rows.shape)],
+        out_specs=[VMEM] * (1 + factors[0]),
+        out_shape=[jax.ShapeDtypeStruct(images.shape, F32)] + [message] * factors[0],
         scratch_shapes=[
             pltpu.VMEM((row_count * tile_side, P_SIZE * tile_side), BF16),
             pltpu.VMEM((per_epoch * tile_rows, row_count * tile_side), BF16),
-            pltpu.VMEM((band_count * PD, tile_rows, tile_side), F32),
+            pltpu.VMEM((band_count * PD, tile_rows + 8, tile_side), F32),
         ],
         compiler_params=pltpu.CompilerParams(
-            dimension_semantics=("arbitrary",), vmem_limit_bytes=40 * 1024 * 1024),
+            dimension_semantics=("arbitrary",), vmem_limit_bytes=VMEM_SMOOTH),
         name="smooth",
-    )(me, coeffs, weights, valid_epoch, owners, locals_, images[0], jnp.asarray(columns), rows, patch_row, weight_row)
+    )(me, *[pltpu.with_memory_space_constraint(value, pltpu.HBM) for value in (
+        coeffs, weights, valid_epoch, owners, locals_, images, jnp.asarray(columns), rows)])
 
 
 def add_kernel(*refs, count, groups):
     parts, outs = refs[:count], refs[count:]
     per_group = outs[0].shape[0]
     for g in range(groups):
-        @pl.loop(0, per_group)
-        def _(i):
+        for i in range(per_group):
             total = parts[0][g * per_group + i].astype(F32)
             for part in parts[1:]:
                 total = total + part[g * per_group + i].astype(F32)
@@ -194,7 +194,9 @@
     out = jax.ShapeDtypeStruct((blocks // groups, block_rows, lanes), BF16)
     return pl.pallas_call(
         functools.partial(add_kernel, count=len(parts), groups=groups),
+        in_specs=[VMEM] * len(parts), out_specs=[VMEM] * groups,
         out_shape=[out] * groups, name="add_and_split",
+        compiler_params=pltpu.CompilerParams(vmem_limit_bytes=VMEM_SMALL),
     )(*parts)
 
 
@@ -212,50 +214,61 @@
     lanes = parts[0].shape[2]
     return pl.pallas_call(
         functools.partial(finish_kernel, tile_rows=tile_rows),
+        in_specs=[VMEM] * len(parts), out_specs=VMEM,
         out_shape=jax.ShapeDtypeStruct((PD, tile_rows, lanes), BF16), name="finish",
+        compiler_params=pltpu.CompilerParams(vmem_limit_bytes=VMEM_SMALL),
     )(*parts)
 
 
-def difference_kernel(me_ref, scale_ref, owner_ref, local_ref, table_ref, smooth_ref, out_ref, *, factors):
+def difference_kernel(me_ref, scale_ref, owner_ref, local_ref, smooth_ref, *rest, factors, count):
+    pieces, (out_ref, table_ref) = rest[:count], rest[count:]
     epoch = pl.program_id(0)
+
+    @pl.when(epoch == 0)
+    def _():
+        start = 0
+        for piece in pieces:
+            table_ref[start:start + piece.shape[0]] = piece[...]
+            start += piece.shape[0]
+
     scale = scale_ref[0, epoch]
     for t in range(smooth_ref.shape[1]):
         place = place_of(owner_ref[epoch, t] ^ me_ref[0], factors) * PD + local_ref[epoch, t]
-        out_ref[0, t] = smooth_ref[0, t] - scale * table_ref[place].astype(F32)
-
-
-def subtract(me, scales, owners, locals_, table, smoothed, factors):
+        out_ref[0, t] = smooth_ref[epoch, t] - scale * table_ref[place].astype(F32)
+
+
+def subtract(me, scales, owners, locals_, pieces, smoothed, factors):
     epochs, per_epoch, tile_rows, tile_side = smoothed.shape
-    smem = pl.BlockSpec(memory_space=pltpu.SMEM)
     tile_block = pl.BlockSpec((1, per_epoch, tile_rows, tile_side), lambda e: (e, 0, 0, 0))
+    patches = sum(piece.shape[0] for piece in pieces)
     return pl.pallas_call(
-        functools.partial(difference_kernel, factors=factors),
+        functools.partial(difference_kernel, factors=factors, count=len(pieces)),
         grid=(epochs,),
-        in_specs=[smem] * 4 + [
-            pl.BlockSpec(table.shape, lambda e: (0, 0, 0), pipeline_mode=pl.Buffered(1)), tile_block],
+        in_specs=[SMEM] * 4 + [VMEM] * (1 + len(pieces)),
         out_specs=tile_block,
         out_shape=jax.ShapeDtypeStruct(smoothed.shape, F32),
-        compiler_params=pltpu.CompilerParams(dimension_semantics=("arbitrary",)),
+        scratch_shapes=[pltpu.VMEM((patches, tile_rows, tile_side), BF16)],
+        compiler_params=pltpu.CompilerParams(
+            dimension_semantics=("arbitrary",), vmem_limit_bytes=VMEM_SUBTRACT),
         name="subtract",
-    )(me, scales, owners, locals_, table, smoothed)
+    )(me, scales, owners, locals_, smoothed, *pieces)
+
+
+VMEM_SMOOTH = 48 * 1024 * 1024
+VMEM_SMALL = 16 * 1024 * 1024
+VMEM_SUBTRACT = 40 * 1024 * 1024
 
 
 def body(images, coeffs, weights, scales, valid_epoch, patch_owner, patch_local):
     band_count = lax.axis_size("band")
     _, epochs, per_epoch, tile_rows, tile_side = images.shape
-    tile_count = epochs * per_epoch
     factors = stage_factors(band_count)
     me = lax.axis_index("band").astype(jnp.int32).reshape(1)
     owners = patch_owner.reshape(epochs, per_epoch)
     locals_ = patch_local.reshape(epochs, per_epoch)
-    flat_coeffs = coeffs.reshape(epochs, -1)
-    patch_row = (place_of(owners ^ me[0], factors) * PD + locals_).reshape(1, tile_count)
-    weight_row = jnp.broadcast_to(
-        (weights[0] * valid_epoch[0].astype(F32)).astype(BF16).astype(F32)[:, None], (epochs, per_epoch)
-    ).reshape(1, tile_count)
 
     smoothed, *blocks = smooth(
-        me, flat_coeffs, weights, valid_epoch, owners, locals_, images, patch_row, weight_row, factors, band_count)
+        me, coeffs[0].transpose(2, 0, 1), weights, valid_epoch, owners, locals_, images[0], factors, band_count)
 
     def exchange(value, step):
         return lax.ppermute(value, "band", [(d, d ^ step) for d in range(band_count)])
@@ -270,11 +283,13 @@
             blocks = add_and_split(parts, factors[k + 1])
     templates = finish(parts, tile_rows)
 
-    table = templates
+    pieces = [templates]
     for factor, stride in zip(reversed(factors), reversed(strides)):
-        table = jnp.concatenate([table] + [exchange(table, j * stride) for j in range(1, factor)], axis=0)
-
-    difference = subtract(me, scales, owners, locals_, table, smoothed, factors)
+        if stride > 1 and len(pieces) > 1:
+            pieces = [jnp.concatenate(pieces, axis=0)]
+        pieces = pieces + [exchange(piece, j * stride) for j in range(1, factor) for piece in pieces]
+
+    difference = subtract(me, scales, owners, locals_, pieces, smoothed, factors)
     return difference[None], templates
 
 

time: 74.6 us -> 52.7 us (0.71)
  local copies, waits for them, and re-layouts: 14 us -> 0.01 us
  Pallas kernels: 25.4 us -> 19 us
  other arithmetic: 2.19 us -> 0.78 us
    unnamed x35 -> x6, local copies, waits for them, and re-layouts: 12.8 us -> 0.01 us
    pallas_call x2, Pallas kernels: 8.26 us -> 4.74 us  [the longest x1 4.03 us: subtract(): pl.pallas_call(functools.partial(difference_kernel, factors=factors, coun...]
    pallas_call x2, Pallas kernels: 3.52 us -> 0.11 us  [add_and_split(): pl.pallas_call(functools.partial(add_kernel, count=len(parts), groups=gro...]
    reshape x4 -> x0, local copies, waits for them, and re-layouts: 0.94 us -> none  [the longest x1 0.77 us: body(): locals_ = patch_local.reshape(epochs, per_epoch)]
    ppermute x10 -> x11, waiting for transfers between devices: 17.8 us -> 18 us  [exchange(): lax.ppermute(value, 'band', [(d, d ^ step) for d in range(band_count)])]
    ppermute x10 -> x11, starting transfers between devices: 13.8 us -> 13.9 us  [exchange(): lax.ppermute(value, 'band', [(d, d ^ step) for d in range(band_count)])]
  transfers between devices with their start and end apart: 10 -> 11, of which waited for: 8 -> 8; matrix products, arithmetic and copies ran while one was open for 1% -> 0% of each run, Pallas kernels for 0% -> 0%
where the time goes in v2:
time: 52.7 us; the launch traced here: 52.4 us
  Pallas kernels  19 us (36%)
  waiting for transfers between devices  18 us (34%)
  starting transfers between devices  13.9 us (26%)
  other arithmetic  0.78 us (1%)
  between operations  0.69 us (1%)
    ppermute x11, waiting for transfers between devices, exchange(): lax.ppermute(value, 'band', [(d, d ^ step) for d in range(band_count)])  18 us
    pallas_call x1, Pallas kernels, smooth(): pl.pallas_call(functools.partial(smooth_kernel, factors=factors, band_cou...  14.1 us
    ppermute x11, starting transfers between devices, exchange(): lax.ppermute(value, 'band', [(d, d ^ step) for d in range(band_count)])  13.9 us
    pallas_call x1, Pallas kernels, subtract(): pl.pallas_call(functools.partial(difference_kernel, factors=factors, coun...  4.03 us
  transfers between devices with their start and end apart: 11, of which 8 were waited for; matrix products, arithmetic and copies ran while one was open for 0% of the time, Pallas kernels for 0%

profile of v2, /device:TPU:0, one launch (start us, length us, event | category | flops | bytes accessed | tf_op | source)
XLA Modules:
  0.0 52.4 jit_solution(17100584942089000800)
XLA Ops:
  0.6 0.0 copy-start
  0.6 0.0 copy-start.1
  0.7 0.0 copy-start.2
  0.7 14.1 %smooth.1 = (f32[8,16,32,128]{3,2,1,0:T(8,128)S(1)}, bf16[8,144,128]{2,1,0:T(8,128)(2,1)S(1)}, bf16[8,144,128]{2,1,0:T(8,128)(2,1)S(1)}) custom-call(s32[1]{0:T(128)} %bitcast.me_ref, f32[3,8,27]{2,1,0:T(8,128)} %bitcast.14, f32[1,8]{1,0:T(1,128)} %weight_ref.1, s32[1,8]{1,0:T(1,128)} %valid_ref.1, s32[8,16]{1,0:T(8,128)} %bitcast.8, s32[8,16]{1,0:T(8,128)} %bitcast.10, ...), custom_call_target="tpu_custom_call" | custom-call | tf_op jit(solution)/shard_map/smooth/pallas_call | solution.py:163
  14.8 0.6 %collective-permute-start = (bf16[8,144,128]{2,1,0:T(8,128)(2,1)S(1)}, bf16[8,144,128]{2,1,0:T(8,128)(2,1)S(1)}, u32[]{:S(2)}, u32[]{:S(2)}) collective-permute-start(bf16[8,144,128]{2,1,0:T(8,128)(2,1)S(1)} %get-tuple-element.13), channel_id=1, source_target_pairs={{0,1},{1,0},{2,3},{3,2},{4,5},{5,4},{6,7},{7,6},{8,9},{9,8},{10,11... | collective-permute-start | bytes 884744 | tf_op jit(solution)/shard_map/ppermute | solution.py:274
  15.4 1.2 %collective-permute-done.refs_1_ = bf16[8,144,128]{2,1,0:T(8,128)(2,1)S(1)} collective-permute-done((bf16[8,144,128]{2,1,0:T(8,128)(2,1)S(1)}, bf16[8,144,128]{2,1,0:T(8,128)(2,1)S(1)}, u32[]{:S(2)}, u32[]{:S(2)}) %collective-permute-start) | collective-permute-done | bytes 294944 | tf_op jit(solution)/shard_map/ppermute | solution.py:274
  16.6 0.1 add_and_split.2
  16.7 2.9 %collective-permute-start.1 = (bf16[4,144,128]{2,1,0:T(8,128)(2,1)S(1)}, bf16[4,144,128]{2,1,0:T(8,128)(2,1)S(1)}, u32[]{:S(2)}, u32[]{:S(2)}) collective-permute-start(bf16[4,144,128]{2,1,0:T(8,128)(2,1)S(1)} %get-tuple-element.15), channel_id=1, source_target_pairs={{0,2},{1,3},{2,0},{3,1},{4,6},{5,7},{6,4},{7,5},{8,10},{9,11},{10,... | collective-permute-start | bytes 442376 | tf_op jit(solution)/shard_map/ppermute | solution.py:274
  19.6 4.1 %collective-permute-done.1.refs_1_ = bf16[4,144,128]{2,1,0:T(8,128)(2,1)S(1)} collective-permute-done((bf16[4,144,128]{2,1,0:T(8,128)(2,1)S(1)}, bf16[4,144,128]{2,1,0:T(8,128)(2,1)S(1)}, u32[]{:S(2)}, u32[]{:S(2)}) %collective-permute-start.1) | collective-permute-done | bytes 147488 | tf_op jit(solution)/shard_map/ppermute | solution.py:274
  23.8 1.9 %collective-permute-start.2 = (bf16[1,144,128]{2,1,0:T(8,128)(2,1)S(1)}, bf16[1,144,128]{2,1,0:T(8,128)(2,1)S(1)}, u32[]{:S(2)}, u32[]{:S(2)}) collective-permute-start(bf16[1,144,128]{2,1,0:T(8,128)(2,1)S(1)} %get-tuple-element.17), channel_id=1, source_target_pairs={{0,4},{1,5},{2,6},{3,7},{4,0},{5,1},{6,2},{7,3},{8,12},{9,13},{10,... | collective-permute-start | bytes 110600 | tf_op jit(solution)/shard_map/ppermute | solution.py:274
  25.6 2.6 %collective-permute-start.3 = (bf16[1,144,128]{2,1,0:T(8,128)(2,1)S(1)}, bf16[1,144,128]{2,1,0:T(8,128)(2,1)S(1)}, u32[]{:S(2)}, u32[]{:S(2)}) collective-permute-start(bf16[1,144,128]{2,1,0:T(8,128)(2,1)S(1)} %get-tuple-element.18), channel_id=1, source_target_pairs={{0,8},{1,9},{2,10},{3,11},{4,12},{5,13},{6,14},{7,15},{8,0},{9,1},... | collective-permute-start | bytes 110600 | tf_op jit(solution)/shard_map/ppermute | solution.py:274
  28.2 0.0 collective-permute-start.4
  28.3 0.0 collective-permute-done.2.refs_1_
  28.3 2.6 %collective-permute-done.3.refs_2_ = bf16[1,144,128]{2,1,0:T(8,128)(2,1)S(1)} collective-permute-done((bf16[1,144,128]{2,1,0:T(8,128)(2,1)S(1)}, bf16[1,144,128]{2,1,0:T(8,128)(2,1)S(1)}, u32[]{:S(2)}, u32[]{:S(2)}) %collective-permute-start.3) | collective-permute-done | bytes 36896 | tf_op jit(solution)/shard_map/ppermute | solution.py:274
  30.9 3.1 %collective-permute-done.4.refs_3_ = bf16[1,144,128]{2,1,0:T(8,128)(2,1)S(1)} collective-permute-done((bf16[1,144,128]{2,1,0:T(8,128)(2,1)S(1)}, bf16[1,144,128]{2,1,0:T(8,128)(2,1)S(1)}, u32[]{:S(2)}, u32[]{:S(2)}) %collective-permute-start.4) | collective-permute-done | bytes 36896 | tf_op jit(solution)/shard_map/ppermute | solution.py:274
  34.0 0.7 %finish.1 = bf16[4,32,128]{2,1,0:T(8,128)(2,1)} custom-call(bf16[1,144,128]{2,1,0:T(8,128)(2,1)S(1)} %get-tuple-element.16.refs_0_, bf16[1,144,128]{2,1,0:T(8,128)(2,1)S(1)} %collective-permute-done.2.refs_1_, bf16[1,144,128]{2,1,0:T(8,128)(2,1)S(1)} %collective-permute-done.3.refs_2_, bf16[1,144,128]{2,1,0:T(8,128)(2,1)S(1)} %collective-permute-done.4.refs_3_), custom_call_target="tpu_custom_call" | custom-call | tf_op jit(solution)/shard_map/finish/pallas_call | solution.py:215
  34.7 0.4 collective-permute-start.7
  35.1 0.0 collective-permute-start.6
  35.1 4.0 %collective-permute-start.5 = (bf16[4,32,128]{2,1,0:T(8,128)(2,1)}, bf16[4,32,128]{2,1,0:T(8,128)(2,1)S(1)}, u32[]{:S(2)}, u32[]{:S(2)}) collective-permute-start(bf16[4,32,128]{2,1,0:T(8,128)(2,1)} %finish.1), channel_id=1, source_target_pairs={{0,4},{1,5},{2,6},{3,7},{4,0},{5,1},{6,2},{7,3},{8,12},{9,13},{10,... | collective-permute-start | bytes 98312 | tf_op jit(solution)/shard_map/ppermute | solution.py:274
  39.1 1.5 %collective-permute-done.7 = bf16[4,32,128]{2,1,0:T(8,128)(2,1)S(1)} collective-permute-done((bf16[4,32,128]{2,1,0:T(8,128)(2,1)}, bf16[4,32,128]{2,1,0:T(8,128)(2,1)S(1)}, u32[]{:S(2)}, u32[]{:S(2)}) %collective-permute-start.7) | collective-permute-done | bytes 32800 | tf_op jit(solution)/shard_map/ppermute | solution.py:274
  40.6 0.0 collective-permute-done.6
  40.6 0.6 %collective-permute-done.5 = bf16[4,32,128]{2,1,0:T(8,128)(2,1)S(1)} collective-permute-done((bf16[4,32,128]{2,1,0:T(8,128)(2,1)}, bf16[4,32,128]{2,1,0:T(8,128)(2,1)S(1)}, u32[]{:S(2)}, u32[]{:S(2)}) %collective-permute-start.5) | collective-permute-done | bytes 32800 | tf_op jit(solution)/shard_map/ppermute | solution.py:274
  41.2 0.8 %pad_maximum_fusion.rest_0_ = bf16[16,32,128]{2,1,0:T(8,128)(2,1)S(1)} fusion(bf16[4,32,128]{2,1,0:T(8,128)(2,1)S(1)} %collective-permute-done.7, bf16[4,32,128]{2,1,0:T(8,128)(2,1)S(1)} %collective-permute-done.6, bf16[4,32,128]{2,1,0:T(8,128)(2,1)S(1)} %collective-permute-done.5, bf16[4,32,128]{2,1,0:T(8,128)(2,1)} %finish.1), kind=kLoop, calls=%fused_computation | loop fusion | flops 196608 | bytes 262144 | tf_op jit(solution)/shard_map/concatenate | solution.py:289
  42.0 1.6 %collective-permute-start.8 = (bf16[16,32,128]{2,1,0:T(8,128)(2,1)S(1)}, bf16[16,32,128]{2,1,0:T(8,128)(2,1)S(1)}, u32[]{:S(2)}, u32[]{:S(2)}) collective-permute-start(bf16[16,32,128]{2,1,0:T(8,128)(2,1)S(1)} %pad_maximum_fusion.rest_0_), channel_id=1, source_target_pairs={{0,2},{1,3},{2,0},{3,1},{4,6},{5,7},{6,4},{7,5},{8,10},{9,11},{10,... | collective-permute-start | bytes 393224 | tf_op jit(solution)/shard_map/ppermute | solution.py:274
  43.6 0.0 collective-permute-start.9
  43.6 3.5 %collective-permute-done.8.rest_1_ = bf16[16,32,128]{2,1,0:T(8,128)(2,1)S(1)} collective-permute-done((bf16[16,32,128]{2,1,0:T(8,128)(2,1)S(1)}, bf16[16,32,128]{2,1,0:T(8,128)(2,1)S(1)}, u32[]{:S(2)}, u32[]{:S(2)}) %collective-permute-start.8) | collective-permute-done | bytes 131104 | tf_op jit(solution)/shard_map/ppermute | solution.py:274
  47.1 0.0 collective-permute-start.10
  47.1 0.0 collective-permute-done.9.rest_2_
  47.1 1.3 %collective-permute-done.10.rest_3_ = bf16[16,32,128]{2,1,0:T(8,128)(2,1)S(1)} collective-permute-done((bf16[16,32,128]{2,1,0:T(8,128)(2,1)S(1)}, bf16[16,32,128]{2,1,0:T(8,128)(2,1)S(1)}, u32[]{:S(2)}, u32[]{:S(2)}) %collective-permute-start.10) | collective-permute-done | bytes 131104 | tf_op jit(solution)/shard_map/ppermute | solution.py:274
  48.4 0.0 copy-done
  48.4 0.0 copy-done.1
  48.4 0.0 copy-done.2
  48.4 4.0 %subtract.1 = f32[8,16,32,128]{3,2,1,0:T(8,128)} custom-call(s32[1]{0:T(128)} %bitcast.me_ref, f32[1,8]{1,0:T(1,128)S(1)} %copy-done.2, s32[8,16]{1,0:T(8,128)S(1)} %bitcast.9, s32[8,16]{1,0:T(8,128)S(1)} %bitcast.11, f32[8,16,32,128]{3,2,1,0:T(8,128)S(1)} %get-tuple-element.11.smooth_ref, bf16[16,32,128]{2,1,0:T(8,128)(2,1)S(1)} %pad_maximum_fusion.rest_0_, ...), custom_call_target="tpu_custom_call" | custom-call | tf_op jit(solution)/shard_map/subtract/pallas_call | solution.py:244
  (1 shorter events, 0.0 us)
Async XLA Ops:
  0.6 47.8 %copy-start = (s32[1,8,16,1]{2,3,1,0:T(1,128)S(1)}, s32[1,8,16,1]{2,3,1,0:T(1,128)}, u32[]{:S(2)}) copy-start(s32[1,8,16,1]{2,3,1,0:T(1,128)} %param.14) | copy-start | bytes 1540
  0.6 47.8 %copy-start.1 = (s32[1,8,16]{2,1,0:T(8,128)S(1)}, s32[1,8,16]{2,1,0:T(8,128)}, u32[]{:S(2)}) copy-start(s32[1,8,16]{2,1,0:T(8,128)} %param.15) | copy-start | bytes 1540
  0.7 47.8 %copy-start.2 = (f32[1,8]{1,0:T(1,128)S(1)}, f32[1,8]{1,0:T(1,128)}, u32[]{:S(2)}) copy-start(f32[1,8]{1,0:T(1,128)} %scale_ref.1) | copy-start | bytes 100
  14.8 1.8 %collective-permute-start = (bf16[8,144,128]{2,1,0:T(8,128)(2,1)S(1)}, bf16[8,144,128]{2,1,0:T(8,128)(2,1)S(1)}, u32[]{:S(2)}, u32[]{:S(2)}) collective-permute-start(bf16[8,144,128]{2,1,0:T(8,128)(2,1)S(1)} %get-tuple-element.13), channel_id=1, source_target_pairs={{0,1},{1,0},{2,3},{3,2},{4,5},{5,4},{6,7},{7,6},{8,9},{9,8},{10,11... | collective-permute-start | bytes 884744 | tf_op jit(solution)/shard_map/ppermute | solution.py:274
  16.7 7.1 %collective-permute-start.1 = (bf16[4,144,128]{2,1,0:T(8,128)(2,1)S(1)}, bf16[4,144,128]{2,1,0:T(8,128)(2,1)S(1)}, u32[]{:S(2)}, u32[]{:S(2)}) collective-permute-start(bf16[4,144,128]{2,1,0:T(8,128)(2,1)S(1)} %get-tuple-element.15), channel_id=1, source_target_pairs={{0,2},{1,3},{2,0},{3,1},{4,6},{5,7},{6,4},{7,5},{8,10},{9,11},{10,... | collective-permute-start | bytes 442376 | tf_op jit(solution)/shard_map/ppermute | solution.py:274
  23.8 4.5 %collective-permute-start.2 = (bf16[1,144,128]{2,1,0:T(8,128)(2,1)S(1)}, bf16[1,144,128]{2,1,0:T(8,128)(2,1)S(1)}, u32[]{:S(2)}, u32[]{:S(2)}) collective-permute-start(bf16[1,144,128]{2,1,0:T(8,128)(2,1)S(1)} %get-tuple-element.17), channel_id=1, source_target_pairs={{0,4},{1,5},{2,6},{3,7},{4,0},{5,1},{6,2},{7,3},{8,12},{9,13},{10,... | collective-permute-start | bytes 110600 | tf_op jit(solution)/shard_map/ppermute | solution.py:274
  25.6 5.2 %collective-permute-start.3 = (bf16[1,144,128]{2,1,0:T(8,128)(2,1)S(1)}, bf16[1,144,128]{2,1,0:T(8,128)(2,1)S(1)}, u32[]{:S(2)}, u32[]{:S(2)}) collective-permute-start(bf16[1,144,128]{2,1,0:T(8,128)(2,1)S(1)} %get-tuple-element.18), channel_id=1, source_target_pairs={{0,8},{1,9},{2,10},{3,11},{4,12},{5,13},{6,14},{7,15},{8,0},{9,1},... | collective-permute-start | bytes 110600 | tf_op jit(solution)/shard_map/ppermute | solution.py:274
  28.2 5.8 %collective-permute-start.4 = (bf16[1,144,128]{2,1,0:T(8,128)(2,1)S(1)}, bf16[1,144,128]{2,1,0:T(8,128)(2,1)S(1)}, u32[]{:S(2)}, u32[]{:S(2)}) collective-permute-start(bf16[1,144,128]{2,1,0:T(8,128)(2,1)S(1)} %get-tuple-element.19), channel_id=1, source_target_pairs={{0,12},{1,13},{2,14},{3,15},{4,8},{5,9},{6,10},{7,11},{8,4},{9,5},... | collective-permute-start | bytes 110600 | tf_op jit(solution)/shard_map/ppermute | solution.py:274
  34.7 5.9 %collective-permute-start.7 = (bf16[4,32,128]{2,1,0:T(8,128)(2,1)}, bf16[4,32,128]{2,1,0:T(8,128)(2,1)S(1)}, u32[]{:S(2)}, u32[]{:S(2)}) collective-permute-start(bf16[4,32,128]{2,1,0:T(8,128)(2,1)} %finish.1), channel_id=1, source_target_pairs={{0,12},{1,13},{2,14},{3,15},{4,8},{5,9},{6,10},{7,11},{8,4},{9,5},... | collective-permute-start | bytes 98312 | tf_op jit(solution)/shard_map/ppermute | solution.py:274
  35.1 5.5 %collective-permute-start.6 = (bf16[4,32,128]{2,1,0:T(8,128)(2,1)}, bf16[4,32,128]{2,1,0:T(8,128)(2,1)S(1)}, u32[]{:S(2)}, u32[]{:S(2)}) collective-permute-start(bf16[4,32,128]{2,1,0:T(8,128)(2,1)} %finish.1), channel_id=1, source_target_pairs={{0,8},{1,9},{2,10},{3,11},{4,12},{5,13},{6,14},{7,15},{8,0},{9,1},... | collective-permute-start | bytes 98312 | tf_op jit(solution)/shard_map/ppermute | solution.py:274
  35.1 6.1 %collective-permute-start.5 = (bf16[4,32,128]{2,1,0:T(8,128)(2,1)}, bf16[4,32,128]{2,1,0:T(8,128)(2,1)S(1)}, u32[]{:S(2)}, u32[]{:S(2)}) collective-permute-start(bf16[4,32,128]{2,1,0:T(8,128)(2,1)} %finish.1), channel_id=1, source_target_pairs={{0,4},{1,5},{2,6},{3,7},{4,0},{5,1},{6,2},{7,3},{8,12},{9,13},{10,... | collective-permute-start | bytes 98312 | tf_op jit(solution)/shard_map/ppermute | solution.py:274
  42.0 5.0 %collective-permute-start.8 = (bf16[16,32,128]{2,1,0:T(8,128)(2,1)S(1)}, bf16[16,32,128]{2,1,0:T(8,128)(2,1)S(1)}, u32[]{:S(2)}, u32[]{:S(2)}) collective-permute-start(bf16[16,32,128]{2,1,0:T(8,128)(2,1)S(1)} %pad_maximum_fusion.rest_0_), channel_id=1, source_target_pairs={{0,2},{1,3},{2,0},{3,1},{4,6},{5,7},{6,4},{7,5},{8,10},{9,11},{10,... | collective-permute-start | bytes 393224 | tf_op jit(solution)/shard_map/ppermute | solution.py:274
  43.6 3.5 %collective-permute-start.9 = (bf16[16,32,128]{2,1,0:T(8,128)(2,1)S(1)}, bf16[16,32,128]{2,1,0:T(8,128)(2,1)S(1)}, u32[]{:S(2)}, u32[]{:S(2)}) collective-permute-start(bf16[16,32,128]{2,1,0:T(8,128)(2,1)S(1)} %pad_maximum_fusion.rest_0_), channel_id=1, source_target_pairs={{0,1},{1,0},{2,3},{3,2},{4,5},{5,4},{6,7},{7,6},{8,9},{9,8},{10,11... | collective-permute-start | bytes 393224 | tf_op jit(solution)/shard_map/ppermute | solution.py:274
  47.1 1.3 %collective-permute-start.10 = (bf16[16,32,128]{2,1,0:T(8,128)(2,1)S(1)}, bf16[16,32,128]{2,1,0:T(8,128)(2,1)S(1)}, u32[]{:S(2)}, u32[]{:S(2)}) collective-permute-start(bf16[16,32,128]{2,1,0:T(8,128)(2,1)S(1)} %collective-permute-done.8.rest_1_), channel_id=1, source_target_pairs={{0,1},{1,0},{2,3},{3,2},{4,5},{5,4},{6,7},{7,6},{8,9},{9,8},{10,11... | collective-permute-start | bytes 393224 | tf_op jit(solution)/shard_map/ppermute | solution.py:274

commit v3 on v2

--- a/solution.py
+++ b/solution.py
@@ -77,54 +77,60 @@
     smooth_ref, *rest, factors, band_count, row_count,
 ):
     message_refs = rest[: factors[0]]
-    mixer_ref, flat_ref, total_ref = rest[factors[0]:]
+    mixer_ref, column_pass_ref, total_ref = rest[factors[0]:]
     epoch = pl.program_id(0)
     per_epoch, tile_rows, tile_side = image_ref.shape[1:]
+    per_lanes = tile_side // tile_rows
     pairs = basis_pairs()
 
     @pl.when(epoch == 0)
     def _():
         total_ref[...] = jnp.zeros_like(total_ref)
 
-    band_rows = 16
-    for top in range(0, tile_side, band_rows):
-        columns = [column_ref[c, top:top + band_rows, :] for c in range(row_count)]
-        for r in range(row_count):
-            used = [(b, pair[1]) for b, pair in enumerate(pairs) if pair[0] == r]
-            for m in range(P_SIZE):
-                value = None
-                for b, c in used:
-                    term = coef_ref[m, epoch, b] * columns[c]
-                    value = term if value is None else value + term
-                mixer_ref[r * tile_side + top:r * tile_side + top + band_rows,
-                          m * tile_side:(m + 1) * tile_side] = value.astype(BF16)
-
-    for t in range(0, per_epoch, 2):
-        pixels = jnp.concatenate([image_ref[0, t].astype(BF16), image_ref[0, t + 1].astype(BF16)], axis=1)
-        rowed = jnp.dot(row_ref[...], pixels, preferred_element_type=F32).astype(BF16)
-        for s in range(2):
-            for r in range(row_count):
-                flat_ref[(t + s) * tile_rows:(t + s + 1) * tile_rows,
-                         r * tile_side:(r + 1) * tile_side] = (
-                    rowed[r * tile_rows:(r + 1) * tile_rows, s * tile_side:(s + 1) * tile_side])
-
-    spatial = jnp.dot(flat_ref[...], mixer_ref[...], preferred_element_type=F32)
-    column = lax.broadcasted_iota(jnp.int32, (tile_rows, tile_side), 1).astype(F32)
     row = lax.broadcasted_iota(jnp.int32, (tile_rows, tile_side), 0).astype(F32)
     down = 2.0 * (row + 0.5) / tile_rows - 1.0
+    for block in range(mixer_ref.shape[0]):
+        used = [b for b, pair in enumerate(pairs) if pair[1] // per_lanes == block]
+        sums = []
+        for m in range(P_SIZE):
+            value = None
+            for b in used:
+                term = coef_ref[m, epoch, b] * row_ref[b]
+                value = term if value is None else value + term
+            sums.append(value)
+        mixer_ref[block, :tile_rows] = (sums[0] + down * sums[2]).astype(BF16)
+        mixer_ref[block, tile_rows:] = sums[1].astype(BF16)
+
+    pixels = image_ref[0].reshape(per_epoch * tile_rows, tile_side).astype(BF16)
+    for c in range(0, row_count, 2):
+        wide = min(2, row_count - c)
+        passed = jnp.dot(
+            pixels, column_ref[:, c * tile_side:(c + wide) * tile_side], preferred_element_type=F32).astype(BF16)
+        for s in range(wide):
+            for t in range(per_epoch):
+                column_pass_ref[t, (c + s) * tile_rows:(c + s + 1) * tile_rows] = (
+                    passed[t * tile_rows:(t + 1) * tile_rows, s * tile_side:(s + 1) * tile_side])
+
+    depth = row_count * tile_rows
+    mixer = jnp.concatenate([mixer_ref[block] for block in range(mixer_ref.shape[0])], axis=1)[:, :depth]
+    column = lax.broadcasted_iota(jnp.int32, (tile_rows, tile_side), 1).astype(F32)
     lane = lax.broadcasted_iota(jnp.int32, (8, tile_side), 1)
     weight = jnp.full((8, tile_side), weight_ref[0, epoch] * valid_ref[0, epoch].astype(F32), F32)
     weight = weight.astype(BF16).astype(F32)
     weights = jnp.concatenate([weight] * (tile_rows // 8), axis=0)
-    for t in range(per_epoch):
-        across = 2.0 * (column + (t * tile_side + 0.5)) / (per_epoch * tile_side) - 1.0
-        part = spatial[t * tile_rows:(t + 1) * tile_rows]
-        value = (part[:, :tile_side] + across * part[:, tile_side:2 * tile_side]
-                 + down * part[:, 2 * tile_side:])
-        smooth_ref[epoch, t] = value
-        place = place_of(owner_ref[epoch, t] ^ me_ref[0], factors) * PD + local_ref[epoch, t]
-        total_ref[place, :tile_rows] = total_ref[place, :tile_rows] + weights * value.astype(BF16).astype(F32)
-        total_ref[place, tile_rows:] = total_ref[place, tile_rows:] + jnp.where(lane == t % tile_side, weight, 0.0)
+    for first in range(0, per_epoch, 2):
+        both = jnp.concatenate([column_pass_ref[first], column_pass_ref[first + 1]], axis=1)
+        spatial = jnp.dot(mixer, both, preferred_element_type=F32)
+        for s in range(2):
+            t = first + s
+            across = 2.0 * (column + (t * tile_side + 0.5)) / (per_epoch * tile_side) - 1.0
+            part = spatial[:, s * tile_side:(s + 1) * tile_side]
+            value = part[:tile_rows] + across * part[tile_rows:]
+            smooth_ref[epoch, t] = value
+            place = place_of(owner_ref[epoch, t] ^ me_ref[0], factors) * PD + local_ref[epoch, t]
+            total_ref[place, :tile_rows] = total_ref[place, :tile_rows] + weights * value.astype(BF16).astype(F32)
+            total_ref[place, tile_rows:] = (
+                total_ref[place, tile_rows:] + jnp.where(lane == t % tile_side, weight, 0.0))
 
     @pl.when(epoch == pl.num_programs(0) - 1)
     def _():
@@ -149,9 +155,16 @@
 
 def smooth(me, coeffs, weights, valid_epoch, owners, locals_, images, factors, band_count):
     epochs, per_epoch, tile_rows, tile_side = images.shape
-    columns = np.ascontiguousarray(kernel_matrices(tile_side).transpose(0, 2, 1))
+    columns = kernel_matrices(tile_side)
     row_count = columns.shape[0]
-    rows = jnp.asarray(kernel_matrices(tile_rows).reshape(row_count * tile_rows, tile_rows), BF16)
+    columns = jnp.asarray(columns.transpose(2, 0, 1).reshape(tile_side, row_count * tile_side), BF16)
+    per_lanes = tile_side // tile_rows
+    row_matrices = np.asarray(kernel_matrices(tile_rows), dtype=BF16).astype(np.float32)
+    pairs = basis_pairs()
+    rows = np.zeros((len(pairs), tile_rows, tile_side), np.float32)
+    for b, (row, column) in enumerate(pairs):
+        start = column % per_lanes * tile_rows
+        rows[b, :, start:start + tile_rows] = row_matrices[row]
     block_rows = PD * tile_rows + EXTRA
     per_group = band_count // factors[0]
     tile_block = pl.BlockSpec((1, per_epoch, tile_rows, tile_side), lambda e: (e, 0, 0, 0))
@@ -167,15 +180,15 @@
         out_specs=[VMEM] * (1 + factors[0]),
         out_shape=[jax.ShapeDtypeStruct(images.shape, F32)] + [message] * factors[0],
         scratch_shapes=[
-            pltpu.VMEM((row_count * tile_side, P_SIZE * tile_side), BF16),
-            pltpu.VMEM((per_epoch * tile_rows, row_count * tile_side), BF16),
+            pltpu.VMEM((-(-row_count // per_lanes), 2 * tile_rows, tile_side), BF16),
+            pltpu.VMEM((per_epoch, row_count * tile_rows, tile_side), BF16),
             pltpu.VMEM((band_count * PD, tile_rows + 8, tile_side), F32),
         ],
         compiler_params=pltpu.CompilerParams(
             dimension_semantics=("arbitrary",), vmem_limit_bytes=VMEM_SMOOTH),
         name="smooth",
     )(me, *[pltpu.with_memory_space_constraint(value, pltpu.HBM) for value in (
-        coeffs, weights, valid_epoch, owners, locals_, images, jnp.asarray(columns), rows)])
+        coeffs, weights, valid_epoch, owners, locals_, images, columns, jnp.asarray(rows))])
 
 
 def add_kernel(*refs, count, groups):

time: 52.7 us -> 47.5 us (0.901)
  Pallas kernels: 19 us -> 13.8 us
    pallas_call x1, Pallas kernels: 14.1 us -> 8.9 us  [smooth(): pl.pallas_call(functools.partial(smooth_kernel, factors=factors, band_cou...]
where the time goes in v3:
time: 47.5 us; the launch traced here: 47.2 us
  waiting for transfers between devices  18 us (38%)
  starting transfers between devices  13.9 us (29%)
  Pallas kernels  13.8 us (29%)
  other arithmetic  0.78 us (2%)
  between operations  0.69 us (1%)
    ppermute x11, waiting for transfers between devices, exchange(): lax.ppermute(value, 'band', [(d, d ^ step) for d in range(band_count)])  18 us
    ppermute x11, starting transfers between devices, exchange(): lax.ppermute(value, 'band', [(d, d ^ step) for d in range(band_count)])  13.9 us
    pallas_call x1, Pallas kernels, smooth(): pl.pallas_call(functools.partial(smooth_kernel, factors=factors, band_cou...  8.9 us
    pallas_call x1, Pallas kernels, subtract(): pl.pallas_call(functools.partial(difference_kernel, factors=factors, coun...  4.03 us
  transfers between devices with their start and end apart: 11, of which 8 were waited for; matrix products, arithmetic and copies ran while one was open for 0% of the time, Pallas kernels for 0%

profile of v3, /device:TPU:0, one launch (start us, length us, event | category | flops | bytes accessed | tf_op | source)
XLA Modules:
  0.0 47.2 jit_solution(8402684366084289668)
XLA Ops:
  0.6 0.0 copy-start
  0.6 0.0 copy-start.1
  0.7 0.0 copy-start.2
  0.7 8.9 %smooth.1 = (f32[8,16,32,128]{3,2,1,0:T(8,128)S(1)}, bf16[8,144,128]{2,1,0:T(8,128)(2,1)S(1)}, bf16[8,144,128]{2,1,0:T(8,128)(2,1)S(1)}) custom-call(s32[1]{0:T(128)} %bitcast.me_ref, f32[3,8,27]{2,1,0:T(8,128)} %bitcast.14, f32[1,8]{1,0:T(1,128)} %weight_ref.1, s32[1,8]{1,0:T(1,128)} %valid_ref.1, s32[8,16]{1,0:T(8,128)} %bitcast.8, s32[8,16]{1,0:T(8,128)} %bitcast.10, ...), custom_call_target="tpu_custom_call" | custom-call | tf_op jit(solution)/shard_map/smooth/pallas_call | solution.py:176
  9.6 0.6 %collective-permute-start = (bf16[8,144,128]{2,1,0:T(8,128)(2,1)S(1)}, bf16[8,144,128]{2,1,0:T(8,128)(2,1)S(1)}, u32[]{:S(2)}, u32[]{:S(2)}) collective-permute-start(bf16[8,144,128]{2,1,0:T(8,128)(2,1)S(1)} %get-tuple-element.13), channel_id=1, source_target_pairs={{0,1},{1,0},{2,3},{3,2},{4,5},{5,4},{6,7},{7,6},{8,9},{9,8},{10,11... | collective-permute-start | bytes 884744 | tf_op jit(solution)/shard_map/ppermute | solution.py:287
  10.1 1.2 %collective-permute-done.refs_1_ = bf16[8,144,128]{2,1,0:T(8,128)(2,1)S(1)} collective-permute-done((bf16[8,144,128]{2,1,0:T(8,128)(2,1)S(1)}, bf16[8,144,128]{2,1,0:T(8,128)(2,1)S(1)}, u32[]{:S(2)}, u32[]{:S(2)}) %collective-permute-start) | collective-permute-done | bytes 294944 | tf_op jit(solution)/shard_map/ppermute | solution.py:287
  11.3 0.1 add_and_split.2
  11.4 3.0 %collective-permute-start.1 = (bf16[4,144,128]{2,1,0:T(8,128)(2,1)S(1)}, bf16[4,144,128]{2,1,0:T(8,128)(2,1)S(1)}, u32[]{:S(2)}, u32[]{:S(2)}) collective-permute-start(bf16[4,144,128]{2,1,0:T(8,128)(2,1)S(1)} %get-tuple-element.15), channel_id=1, source_target_pairs={{0,2},{1,3},{2,0},{3,1},{4,6},{5,7},{6,4},{7,5},{8,10},{9,11},{10,... | collective-permute-start | bytes 442376 | tf_op jit(solution)/shard_map/ppermute | solution.py:287
  14.4 4.1 %collective-permute-done.1.refs_1_ = bf16[4,144,128]{2,1,0:T(8,128)(2,1)S(1)} collective-permute-done((bf16[4,144,128]{2,1,0:T(8,128)(2,1)S(1)}, bf16[4,144,128]{2,1,0:T(8,128)(2,1)S(1)}, u32[]{:S(2)}, u32[]{:S(2)}) %collective-permute-start.1) | collective-permute-done | bytes 147488 | tf_op jit(solution)/shard_map/ppermute | solution.py:287
  18.6 1.9 %collective-permute-start.2 = (bf16[1,144,128]{2,1,0:T(8,128)(2,1)S(1)}, bf16[1,144,128]{2,1,0:T(8,128)(2,1)S(1)}, u32[]{:S(2)}, u32[]{:S(2)}) collective-permute-start(bf16[1,144,128]{2,1,0:T(8,128)(2,1)S(1)} %get-tuple-element.17), channel_id=1, source_target_pairs={{0,4},{1,5},{2,6},{3,7},{4,0},{5,1},{6,2},{7,3},{8,12},{9,13},{10,... | collective-permute-start | bytes 110600 | tf_op jit(solution)/shard_map/ppermute | solution.py:287
  20.4 2.6 %collective-permute-start.3 = (bf16[1,144,128]{2,1,0:T(8,128)(2,1)S(1)}, bf16[1,144,128]{2,1,0:T(8,128)(2,1)S(1)}, u32[]{:S(2)}, u32[]{:S(2)}) collective-permute-start(bf16[1,144,128]{2,1,0:T(8,128)(2,1)S(1)} %get-tuple-element.18), channel_id=1, source_target_pairs={{0,8},{1,9},{2,10},{3,11},{4,12},{5,13},{6,14},{7,15},{8,0},{9,1},... | collective-permute-start | bytes 110600 | tf_op jit(solution)/shard_map/ppermute | solution.py:287
  23.0 0.0 collective-permute-start.4
  23.0 0.0 collective-permute-done.2.refs_1_
  23.0 2.6 %collective-permute-done.3.refs_2_ = bf16[1,144,128]{2,1,0:T(8,128)(2,1)S(1)} collective-permute-done((bf16[1,144,128]{2,1,0:T(8,128)(2,1)S(1)}, bf16[1,144,128]{2,1,0:T(8,128)(2,1)S(1)}, u32[]{:S(2)}, u32[]{:S(2)}) %collective-permute-start.3) | collective-permute-done | bytes 36896 | tf_op jit(solution)/shard_map/ppermute | solution.py:287
  25.6 3.1 %collective-permute-done.4.refs_3_ = bf16[1,144,128]{2,1,0:T(8,128)(2,1)S(1)} collective-permute-done((bf16[1,144,128]{2,1,0:T(8,128)(2,1)S(1)}, bf16[1,144,128]{2,1,0:T(8,128)(2,1)S(1)}, u32[]{:S(2)}, u32[]{:S(2)}) %collective-permute-start.4) | collective-permute-done | bytes 36896 | tf_op jit(solution)/shard_map/ppermute | solution.py:287
  28.8 0.7 %finish.1 = bf16[4,32,128]{2,1,0:T(8,128)(2,1)} custom-call(bf16[1,144,128]{2,1,0:T(8,128)(2,1)S(1)} %get-tuple-element.16.refs_0_, bf16[1,144,128]{2,1,0:T(8,128)(2,1)S(1)} %collective-permute-done.2.refs_1_, bf16[1,144,128]{2,1,0:T(8,128)(2,1)S(1)} %collective-permute-done.3.refs_2_, bf16[1,144,128]{2,1,0:T(8,128)(2,1)S(1)} %collective-permute-done.4.refs_3_), custom_call_target="tpu_custom_call" | custom-call | tf_op jit(solution)/shard_map/finish/pallas_call | solution.py:228
  29.5 0.4 collective-permute-start.7
  29.9 0.0 collective-permute-start.6
  29.9 4.0 %collective-permute-start.5 = (bf16[4,32,128]{2,1,0:T(8,128)(2,1)}, bf16[4,32,128]{2,1,0:T(8,128)(2,1)S(1)}, u32[]{:S(2)}, u32[]{:S(2)}) collective-permute-start(bf16[4,32,128]{2,1,0:T(8,128)(2,1)} %finish.1), channel_id=1, source_target_pairs={{0,4},{1,5},{2,6},{3,7},{4,0},{5,1},{6,2},{7,3},{8,12},{9,13},{10,... | collective-permute-start | bytes 98312 | tf_op jit(solution)/shard_map/ppermute | solution.py:287
  33.9 1.5 %collective-permute-done.7 = bf16[4,32,128]{2,1,0:T(8,128)(2,1)S(1)} collective-permute-done((bf16[4,32,128]{2,1,0:T(8,128)(2,1)}, bf16[4,32,128]{2,1,0:T(8,128)(2,1)S(1)}, u32[]{:S(2)}, u32[]{:S(2)}) %collective-permute-start.7) | collective-permute-done | bytes 32800 | tf_op jit(solution)/shard_map/ppermute | solution.py:287
  35.4 0.0 collective-permute-done.6
  35.4 0.6 %collective-permute-done.5 = bf16[4,32,128]{2,1,0:T(8,128)(2,1)S(1)} collective-permute-done((bf16[4,32,128]{2,1,0:T(8,128)(2,1)}, bf16[4,32,128]{2,1,0:T(8,128)(2,1)S(1)}, u32[]{:S(2)}, u32[]{:S(2)}) %collective-permute-start.5) | collective-permute-done | bytes 32800 | tf_op jit(solution)/shard_map/ppermute | solution.py:287
  36.0 0.8 %pad_maximum_fusion.rest_0_ = bf16[16,32,128]{2,1,0:T(8,128)(2,1)S(1)} fusion(bf16[4,32,128]{2,1,0:T(8,128)(2,1)S(1)} %collective-permute-done.7, bf16[4,32,128]{2,1,0:T(8,128)(2,1)S(1)} %collective-permute-done.6, bf16[4,32,128]{2,1,0:T(8,128)(2,1)S(1)} %collective-permute-done.5, bf16[4,32,128]{2,1,0:T(8,128)(2,1)} %finish.1), kind=kLoop, calls=%fused_computation | loop fusion | flops 196608 | bytes 262144 | tf_op jit(solution)/shard_map/concatenate | solution.py:302
  36.8 1.6 %collective-permute-start.8 = (bf16[16,32,128]{2,1,0:T(8,128)(2,1)S(1)}, bf16[16,32,128]{2,1,0:T(8,128)(2,1)S(1)}, u32[]{:S(2)}, u32[]{:S(2)}) collective-permute-start(bf16[16,32,128]{2,1,0:T(8,128)(2,1)S(1)} %pad_maximum_fusion.rest_0_), channel_id=1, source_target_pairs={{0,2},{1,3},{2,0},{3,1},{4,6},{5,7},{6,4},{7,5},{8,10},{9,11},{10,... | collective-permute-start | bytes 393224 | tf_op jit(solution)/shard_map/ppermute | solution.py:287
  38.4 0.0 collective-permute-start.9
  38.4 3.4 %collective-permute-done.8.rest_1_ = bf16[16,32,128]{2,1,0:T(8,128)(2,1)S(1)} collective-permute-done((bf16[16,32,128]{2,1,0:T(8,128)(2,1)S(1)}, bf16[16,32,128]{2,1,0:T(8,128)(2,1)S(1)}, u32[]{:S(2)}, u32[]{:S(2)}) %collective-permute-start.8) | collective-permute-done | bytes 131104 | tf_op jit(solution)/shard_map/ppermute | solution.py:287
  41.8 0.0 collective-permute-start.10
  41.8 0.0 collective-permute-done.9.rest_2_
  41.8 1.3 %collective-permute-done.10.rest_3_ = bf16[16,32,128]{2,1,0:T(8,128)(2,1)S(1)} collective-permute-done((bf16[16,32,128]{2,1,0:T(8,128)(2,1)S(1)}, bf16[16,32,128]{2,1,0:T(8,128)(2,1)S(1)}, u32[]{:S(2)}, u32[]{:S(2)}) %collective-permute-start.10) | collective-permute-done | bytes 131104 | tf_op jit(solution)/shard_map/ppermute | solution.py:287
  43.2 0.0 copy-done
  43.2 0.0 copy-done.1
  43.2 0.0 copy-done.2
  43.2 4.0 %subtract.1 = f32[8,16,32,128]{3,2,1,0:T(8,128)} custom-call(s32[1]{0:T(128)} %bitcast.me_ref, f32[1,8]{1,0:T(1,128)S(1)} %copy-done.2, s32[8,16]{1,0:T(8,128)S(1)} %bitcast.9, s32[8,16]{1,0:T(8,128)S(1)} %bitcast.11, f32[8,16,32,128]{3,2,1,0:T(8,128)S(1)} %get-tuple-element.11.smooth_ref, bf16[16,32,128]{2,1,0:T(8,128)(2,1)S(1)} %pad_maximum_fusion.rest_0_, ...), custom_call_target="tpu_custom_call" | custom-call | tf_op jit(solution)/shard_map/subtract/pallas_call | solution.py:257
  (1 shorter events, 0.0 us)
Async XLA Ops:
  0.6 42.5 %copy-start = (s32[1,8,16,1]{2,3,1,0:T(1,128)S(1)}, s32[1,8,16,1]{2,3,1,0:T(1,128)}, u32[]{:S(2)}) copy-start(s32[1,8,16,1]{2,3,1,0:T(1,128)} %param.14) | copy-start | bytes 1540
  0.6 42.5 %copy-start.1 = (s32[1,8,16]{2,1,0:T(8,128)S(1)}, s32[1,8,16]{2,1,0:T(8,128)}, u32[]{:S(2)}) copy-start(s32[1,8,16]{2,1,0:T(8,128)} %param.15) | copy-start | bytes 1540
  0.7 42.5 %copy-start.2 = (f32[1,8]{1,0:T(1,128)S(1)}, f32[1,8]{1,0:T(1,128)}, u32[]{:S(2)}) copy-start(f32[1,8]{1,0:T(1,128)} %scale_ref.1) | copy-start | bytes 100
  9.6 1.8 %collective-permute-start = (bf16[8,144,128]{2,1,0:T(8,128)(2,1)S(1)}, bf16[8,144,128]{2,1,0:T(8,128)(2,1)S(1)}, u32[]{:S(2)}, u32[]{:S(2)}) collective-permute-start(bf16[8,144,128]{2,1,0:T(8,128)(2,1)S(1)} %get-tuple-element.13), channel_id=1, source_target_pairs={{0,1},{1,0},{2,3},{3,2},{4,5},{5,4},{6,7},{7,6},{8,9},{9,8},{10,11... | collective-permute-start | bytes 884744 | tf_op jit(solution)/shard_map/ppermute | solution.py:287
  11.4 7.1 %collective-permute-start.1 = (bf16[4,144,128]{2,1,0:T(8,128)(2,1)S(1)}, bf16[4,144,128]{2,1,0:T(8,128)(2,1)S(1)}, u32[]{:S(2)}, u32[]{:S(2)}) collective-permute-start(bf16[4,144,128]{2,1,0:T(8,128)(2,1)S(1)} %get-tuple-element.15), channel_id=1, source_target_pairs={{0,2},{1,3},{2,0},{3,1},{4,6},{5,7},{6,4},{7,5},{8,10},{9,11},{10,... | collective-permute-start | bytes 442376 | tf_op jit(solution)/shard_map/ppermute | solution.py:287
  18.6 4.5 %collective-permute-start.2 = (bf16[1,144,128]{2,1,0:T(8,128)(2,1)S(1)}, bf16[1,144,128]{2,1,0:T(8,128)(2,1)S(1)}, u32[]{:S(2)}, u32[]{:S(2)}) collective-permute-start(bf16[1,144,128]{2,1,0:T(8,128)(2,1)S(1)} %get-tuple-element.17), channel_id=1, source_target_pairs={{0,4},{1,5},{2,6},{3,7},{4,0},{5,1},{6,2},{7,3},{8,12},{9,13},{10,... | collective-permute-start | bytes 110600 | tf_op jit(solution)/shard_map/ppermute | solution.py:287
  20.4 5.2 %collective-permute-start.3 = (bf16[1,144,128]{2,1,0:T(8,128)(2,1)S(1)}, bf16[1,144,128]{2,1,0:T(8,128)(2,1)S(1)}, u32[]{:S(2)}, u32[]{:S(2)}) collective-permute-start(bf16[1,144,128]{2,1,0:T(8,128)(2,1)S(1)} %get-tuple-element.18), channel_id=1, source_target_pairs={{0,8},{1,9},{2,10},{3,11},{4,12},{5,13},{6,14},{7,15},{8,0},{9,1},... | collective-permute-start | bytes 110600 | tf_op jit(solution)/shard_map/ppermute | solution.py:287
  23.0 5.8 %collective-permute-start.4 = (bf16[1,144,128]{2,1,0:T(8,128)(2,1)S(1)}, bf16[1,144,128]{2,1,0:T(8,128)(2,1)S(1)}, u32[]{:S(2)}, u32[]{:S(2)}) collective-permute-start(bf16[1,144,128]{2,1,0:T(8,128)(2,1)S(1)} %get-tuple-element.19), channel_id=1, source_target_pairs={{0,12},{1,13},{2,14},{3,15},{4,8},{5,9},{6,10},{7,11},{8,4},{9,5},... | collective-permute-start | bytes 110600 | tf_op jit(solution)/shard_map/ppermute | solution.py:287
  29.5 5.9 %collective-permute-start.7 = (bf16[4,32,128]{2,1,0:T(8,128)(2,1)}, bf16[4,32,128]{2,1,0:T(8,128)(2,1)S(1)}, u32[]{:S(2)}, u32[]{:S(2)}) collective-permute-start(bf16[4,32,128]{2,1,0:T(8,128)(2,1)} %finish.1), channel_id=1, source_target_pairs={{0,12},{1,13},{2,14},{3,15},{4,8},{5,9},{6,10},{7,11},{8,4},{9,5},... | collective-permute-start | bytes 98312 | tf_op jit(solution)/shard_map/ppermute | solution.py:287
  29.9 5.5 %collective-permute-start.6 = (bf16[4,32,128]{2,1,0:T(8,128)(2,1)}, bf16[4,32,128]{2,1,0:T(8,128)(2,1)S(1)}, u32[]{:S(2)}, u32[]{:S(2)}) collective-permute-start(bf16[4,32,128]{2,1,0:T(8,128)(2,1)} %finish.1), channel_id=1, source_target_pairs={{0,8},{1,9},{2,10},{3,11},{4,12},{5,13},{6,14},{7,15},{8,0},{9,1},... | collective-permute-start | bytes 98312 | tf_op jit(solution)/shard_map/ppermute | solution.py:287
  29.9 6.1 %collective-permute-start.5 = (bf16[4,32,128]{2,1,0:T(8,128)(2,1)}, bf16[4,32,128]{2,1,0:T(8,128)(2,1)S(1)}, u32[]{:S(2)}, u32[]{:S(2)}) collective-permute-start(bf16[4,32,128]{2,1,0:T(8,128)(2,1)} %finish.1), channel_id=1, source_target_pairs={{0,4},{1,5},{2,6},{3,7},{4,0},{5,1},{6,2},{7,3},{8,12},{9,13},{10,... | collective-permute-start | bytes 98312 | tf_op jit(solution)/shard_map/ppermute | solution.py:287
  36.8 5.0 %collective-permute-start.8 = (bf16[16,32,128]{2,1,0:T(8,128)(2,1)S(1)}, bf16[16,32,128]{2,1,0:T(8,128)(2,1)S(1)}, u32[]{:S(2)}, u32[]{:S(2)}) collective-permute-start(bf16[16,32,128]{2,1,0:T(8,128)(2,1)S(1)} %pad_maximum_fusion.rest_0_), channel_id=1, source_target_pairs={{0,2},{1,3},{2,0},{3,1},{4,6},{5,7},{6,4},{7,5},{8,10},{9,11},{10,... | collective-permute-start | bytes 393224 | tf_op jit(solution)/shard_map/ppermute | solution.py:287
  38.4 3.5 %collective-permute-start.9 = (bf16[16,32,128]{2,1,0:T(8,128)(2,1)S(1)}, bf16[16,32,128]{2,1,0:T(8,128)(2,1)S(1)}, u32[]{:S(2)}, u32[]{:S(2)}) collective-permute-start(bf16[16,32,128]{2,1,0:T(8,128)(2,1)S(1)} %pad_maximum_fusion.rest_0_), channel_id=1, source_target_pairs={{0,1},{1,0},{2,3},{3,2},{4,5},{5,4},{6,7},{7,6},{8,9},{9,8},{10,11... | collective-permute-start | bytes 393224 | tf_op jit(solution)/shard_map/ppermute | solution.py:287
  41.8 1.3 %collective-permute-start.10 = (bf16[16,32,128]{2,1,0:T(8,128)(2,1)S(1)}, bf16[16,32,128]{2,1,0:T(8,128)(2,1)S(1)}, u32[]{:S(2)}, u32[]{:S(2)}) collective-permute-start(bf16[16,32,128]{2,1,0:T(8,128)(2,1)S(1)} %collective-permute-done.8.rest_1_), channel_id=1, source_target_pairs={{0,1},{1,0},{2,3},{3,2},{4,5},{5,4},{6,7},{7,6},{8,9},{9,8},{10,11... | collective-permute-start | bytes 393224 | tf_op jit(solution)/shard_map/ppermute | solution.py:287

commit v4 on v3

v4 whole, which is shorter than its diff:
```python
import functools

import jax
import jax.numpy as jnp
import numpy as np
from jax import lax
from jax.experimental import pallas as pl
from jax.experimental.pallas import tpu as pltpu
from jax.sharding import PartitionSpec as P

PD = 4
HALF = 9
P_SIZE = 3

sigmas = (0.75, 1.5, 3.0)
degrees = (4, 2, 2)

BF16 = jnp.bfloat16
F32 = jnp.float32
EXTRA = 8


def kernel_matrices(tile_side):
    place = np.arange(tile_side)
    apart = place[:, None] - place[None, :]
    offset = apart.astype(np.float32)
    inside = (np.abs(apart) <= HALF).astype(np.float32)
    taps = np.arange(-HALF, HALF + 1).astype(np.float32)
    tables = []
    for width_sigma, degree in zip(sigmas, degrees):
        scale = np.float32(2.0 * width_sigma * width_sigma)
        total = np.sum(np.exp(-taps * taps / scale), dtype=np.float32)
        envelope = np.exp(-offset * offset / scale) * inside / total
        for power in range(degree + 1):
            tables.append((envelope * (offset / np.float32(width_sigma)) ** power).astype(np.float32))
    return np.stack(tables)


def basis_pairs():
    kernel_list = []
    base_index = 0
    for degree in degrees:
        for column_power in range(degree + 1):
            for row_power in range(degree + 1 - column_power):
                kernel_list.append((base_index + row_power, base_index + column_power))
        base_index = base_index + degree + 1
    return kernel_list


def reduce_stages(band_count):
    return gather_stages(band_count)


def gather_stages(band_count):
    rest = band_count // 2
    inner = 1
    while 4 * inner * inner <= rest:
        inner *= 2
    return [factor for factor in (2, inner, rest // inner) if factor > 1]


def place_of(distance, factors):
    total = int(np.prod(factors))
    place = 0
    for factor in factors:
        total //= factor
        place = place + (distance & (factor - 1)) * total
        distance = distance >> (factor.bit_length() - 1)
    return place


def smooth_kernel(
    me_ref, weight_ref, valid_ref, owner_ref, local_ref, coef_ref, image_ref, column_ref, row_ref, spread_ref,
    smooth_ref, *rest, factors, band_count, row_count, layers,
):
    message_refs = rest[:-(2 * TOGETHER + 2)]
    total_ref, factor_ref = rest[-(2 * TOGETHER + 2):-2 * TOGETHER]
    mixer_refs, column_pass_refs = rest[-2 * TOGETHER:-TOGETHER], rest[-TOGETHER:]
    step = pl.program_id(0)
    together, per_epoch, tile_rows, tile_side = image_ref.shape
    epochs = smooth_ref.shape[0]
    depth = row_count * tile_rows

    @pl.when(step == 0)
    def _():
        total_ref[...] = jnp.zeros_like(total_ref)
        coefs = coef_ref[...].reshape(P_SIZE * epochs, coef_ref.shape[2])
        for k in range(len(layers)):
            factor_ref[k] = jnp.dot(
                coefs, spread_ref[k], precision=lax.Precision.HIGHEST, preferred_element_type=F32)

    row = lax.broadcasted_iota(jnp.int32, (tile_rows, tile_side), 0).astype(F32)
    column = lax.broadcasted_iota(jnp.int32, (tile_rows, tile_side), 1).astype(F32)
    lane = lax.broadcasted_iota(jnp.int32, (8, tile_side), 1)
    down = 2.0 * (row + 0.5) / tile_rows - 1.0

    for sub in range(together):
        epoch = step * together + sub
        mixer_ref, column_pass_ref = mixer_refs[sub], column_pass_refs[sub]

        for block in range(mixer_ref.shape[0]):
            sums = []
            for m in range(P_SIZE):
                value = None
                for k, owner in enumerate(layers):
                    if owner == block:
                        factor = factor_ref[k, pl.ds(m * epochs + epoch, 1), :]
                        term = factor * row_ref[k]
                        value = term if value is None else value + term
                sums.append(value)
            mixer_ref[block, :tile_rows] = (sums[0] + down * sums[2]).astype(BF16)
            mixer_ref[block, tile_rows:] = sums[1].astype(BF16)

        pixels = image_ref[sub].reshape(per_epoch * tile_rows, tile_side).astype(BF16)
        for c in range(0, row_count, 2):
            wide = min(2, row_count - c)
            passed = jnp.dot(
                pixels, column_ref[:, c * tile_side:(c + wide) * tile_side], preferred_element_type=F32).astype(BF16)
            for s in range(wide):
                for t in range(per_epoch):
                    column_pass_ref[t, (c + s) * tile_rows:(c + s + 1) * tile_rows] = (
                        passed[t * tile_rows:(t + 1) * tile_rows, s * tile_side:(s + 1) * tile_side])

    for sub in range(together):
        epoch = step * together + sub
        mixer_ref, column_pass_ref = mixer_refs[sub], column_pass_refs[sub]
        mixer = jnp.concatenate([mixer_ref[block] for block in range(mixer_ref.shape[0])], axis=1)[:, :depth]
        weight = jnp.full((8, tile_side), weight_ref[0, epoch] * valid_ref[0, epoch].astype(F32), F32)
        weight = weight.astype(BF16).astype(F32)
        weights = jnp.concatenate([weight] * (tile_rows // 8), axis=0)
        for first in range(0, per_epoch, 2):
            both = jnp.concatenate([column_pass_ref[first], column_pass_ref[first + 1]], axis=1)
            spatial = jnp.dot(mixer, both, preferred_element_type=F32)
            for s in range(2):
                t = first + s
                across = 2.0 * (column + (t * tile_side + 0.5)) / (per_epoch * tile_side) - 1.0
                part = spatial[:, s * tile_side:(s + 1) * tile_side]
                value = part[:tile_rows] + across * part[tile_rows:]
                smooth_ref[epoch, t] = value
                place = place_of(owner_ref[epoch, t] ^ me_ref[0], factors) * PD + local_ref[epoch, t]
                total_ref[place, :tile_rows] = (
                    total_ref[place, :tile_rows] + weights * value.astype(BF16).astype(F32))
                total_ref[place, tile_rows:] = (
                    total_ref[place, tile_rows:] + jnp.where(lane == t % tile_side, weight, 0.0))

    @pl.when(step == pl.num_programs(0) - 1)
    def _():
        groups = factors[0]
        per_group = band_count // groups
        line = lax.broadcasted_iota(jnp.int32, (8, tile_side), 0)
        part_rows = tile_rows // CHAINS
        for g in range(groups):
            @pl.loop(0, per_group)
            def _(i):
                block = (g * per_group + i) * PD
                marks = jnp.zeros((8, tile_side), F32)
                for q in range(PD):
                    for h in range(CHAINS):
                        message_refs[h * groups + g][i, q * part_rows:(q + 1) * part_rows, :] = (
                            total_ref[block + q, h * part_rows:(h + 1) * part_rows].astype(BF16))
                    marks = jnp.where(line == q, total_ref[block + q, tile_rows:], marks)
                message_refs[g][i, PD * part_rows:, :] = marks.astype(BF16)


VMEM = pl.BlockSpec(memory_space=pltpu.VMEM)
SMEM = pl.BlockSpec(memory_space=pltpu.SMEM)


def smooth(me, coeffs, weights, valid_epoch, owners, locals_, images, factors, band_count):
    epochs, per_epoch, tile_rows, tile_side = images.shape
    columns = kernel_matrices(tile_side)
    row_count = columns.shape[0]
    columns = jnp.asarray(columns.transpose(2, 0, 1).reshape(tile_side, row_count * tile_side), BF16)
    per_lanes = tile_side // tile_rows
    row_matrices = np.asarray(kernel_matrices(tile_rows), dtype=BF16).astype(np.float32)
    pairs = basis_pairs()
    layers, rows, spread = [], [], []
    for block in range(-(-row_count // per_lanes)):
        held = [[b for b, pair in enumerate(pairs) if pair[1] == block * per_lanes + i] for i in range(per_lanes)]
        for depth in range(max(map(len, held))):
            layers.append(block)
            rows.append(np.zeros((tile_rows, tile_side), np.float32))
            spread.append(np.zeros((len(pairs), tile_side), np.float32))
            for i, bases in enumerate(held):
                if depth < len(bases):
                    lanes = slice(i * tile_rows, (i + 1) * tile_rows)
                    rows[-1][:, lanes] = row_matrices[pairs[bases[depth]][0]]
                    spread[-1][bases[depth], lanes] = 1.0
    rows, spread = np.stack(rows), np.stack(spread)
    part_rows = PD * tile_rows // CHAINS
    per_group = band_count // factors[0]
    tile_block = pl.BlockSpec((TOGETHER, per_epoch, tile_rows, tile_side), lambda e: (e, 0, 0, 0))

    def whole(shape):
        return pl.BlockSpec(shape, lambda e: (0,) * len(shape), pipeline_mode=pl.Buffered(1))

    messages = [
        jax.ShapeDtypeStruct((per_group, part_rows + (EXTRA if h == 0 else 0), tile_side), BF16)
        for h in range(CHAINS) for _ in range(factors[0])]
    return pl.pallas_call(
        functools.partial(smooth_kernel, factors=factors, band_count=band_count, row_count=row_count,
            layers=layers),
        grid=(epochs // TOGETHER,),
        in_specs=[SMEM] * 5 + [
            whole(coeffs.shape), tile_block, whole(columns.shape), whole(rows.shape), whole(spread.shape)],
        out_specs=[VMEM] * (1 + len(messages)),
        out_shape=[jax.ShapeDtypeStruct(images.shape, F32)] + messages,
        scratch_shapes=[
            pltpu.VMEM((band_count * PD, tile_rows + 8, tile_side), F32),
            pltpu.VMEM((len(layers), P_SIZE * epochs, tile_side), F32),
        ] + [
            pltpu.VMEM((-(-row_count // per_lanes), 2 * tile_rows, tile_side), BF16),
        ] * TOGETHER + [
            pltpu.VMEM((per_epoch, row_count * tile_rows, tile_side), BF16),
        ] * TOGETHER,
        compiler_params=pltpu.CompilerParams(
            dimension_semantics=("arbitrary",), vmem_limit_bytes=VMEM_SMOOTH),
        name="smooth",
    )(me, *[pltpu.with_memory_space_constraint(value, pltpu.HBM) for value in (
        weights, valid_epoch, owners, locals_, coeffs, images, columns, jnp.asarray(rows), jnp.asarray(spread))])


def add_kernel(*refs, count, groups):
    parts, outs = refs[:count], refs[count:]
    per_group = outs[0].shape[0]
    for g in range(groups):
        for i in range(per_group):
            total = parts[0][g * per_group + i].astype(F32)
            for part in parts[1:]:
                total = total + part[g * per_group + i].astype(F32)
            outs[g][i] = total.astype(BF16)


def add_and_split(parts, groups):
    blocks, block_rows, lanes = parts[0].shape
    out = jax.ShapeDtypeStruct((blocks // groups, block_rows, lanes), BF16)
    return pl.pallas_call(
        functools.partial(add_kernel, count=len(parts), groups=groups),
        in_specs=[VMEM] * len(parts), out_specs=[VMEM] * groups,
        out_shape=[out] * groups, name="add_and_split",
        compiler_params=pltpu.CompilerParams(vmem_limit_bytes=VMEM_SMALL),
    )(*parts)


def finish_kernel(*refs, part_rows):
    *parts, out_ref = refs
    each = len(parts) // CHAINS
    inverse = None
    for h in range(CHAINS):
        total = parts[h * each][0].astype(F32)
        for part in parts[h * each + 1:(h + 1) * each]:
            total = total + part[0].astype(F32)
        if h == 0:
            marks = total[PD * part_rows:, :]
            inverse = jnp.broadcast_to(1.0 / (1.0 + jnp.sum(marks, axis=1, keepdims=True)), marks.shape)
        for q in range(PD):
            out_ref[q, h * part_rows:(h + 1) * part_rows] = (
                total[q * part_rows:(q + 1) * part_rows] * inverse[q:q + 1]).astype(BF16)


def finish(parts, tile_rows):
    return pl.pallas_call(
        functools.partial(finish_kernel, part_rows=tile_rows // CHAINS),
        in_specs=[VMEM] * len(parts), out_specs=VMEM,
        out_shape=jax.ShapeDtypeStruct((PD, tile_rows, parts[0].shape[2]), BF16), name="finish",
        compiler_params=pltpu.CompilerParams(vmem_limit_bytes=VMEM_SMALL),
    )(*parts)


def join_kernel(*refs):
    start = 0
    for piece in refs[:-1]:
        refs[-1][start:start + piece.shape[0]] = piece[...]
        start += piece.shape[0]


def join(pieces):
    total = sum(piece.shape[0] for piece in pieces)
    return pl.pallas_call(
        join_kernel, in_specs=[VMEM] * len(pieces), out_specs=VMEM,
        out_shape=jax.ShapeDtypeStruct((total, *pieces[0].shape[1:]), BF16), name="join",
        compiler_params=pltpu.CompilerParams(vmem_limit_bytes=VMEM_SMALL),
    )(*pieces)


def difference_kernel(me_ref, scale_ref, owner_ref, local_ref, smooth_ref, *rest, factors, count):
    pieces, (out_ref, template_ref, table_ref, ready_ref, sems) = rest[:count], rest[count:]
    epochs, per_epoch = smooth_ref.shape[:2]
    start = 0
    for piece in pieces:
        table_ref[start:start + piece.shape[0]] = piece[...]
        start += piece.shape[0]

    def copy(e):
        return pltpu.make_async_copy(ready_ref.at[e], out_ref.at[e], sems.at[e])

    for e in range(epochs):
        scale = scale_ref[0, e]
        for t in range(per_epoch):
            place = place_of(owner_ref[e, t] ^ me_ref[0], factors) * PD + local_ref[e, t]
            ready_ref[e, t] = smooth_ref[e, t] - scale * table_ref[place].astype(F32)
        if e > 0:
            copy(e - 1).start()
    template_ref[...] = table_ref[:PD]
    copy(epochs - 1).start()
    for e in range(epochs):
        copy(e).wait()


def subtract(me, scales, owners, locals_, pieces, smoothed, factors):
    tile_rows, tile_side = smoothed.shape[2:]
    own = (PD, tile_rows, tile_side)
    return pl.pallas_call(
        functools.partial(difference_kernel, factors=factors, count=len(pieces)),
        in_specs=[SMEM] * 4 + [VMEM] * (1 + len(pieces)),
        out_specs=[pl.BlockSpec(memory_space=pltpu.HBM), VMEM],
        out_shape=[jax.ShapeDtypeStruct(smoothed.shape, F32), jax.ShapeDtypeStruct(own, BF16)],
        scratch_shapes=[
            pltpu.VMEM((PD * int(np.prod(factors)), tile_rows, tile_side), BF16),
            pltpu.VMEM(smoothed.shape, F32),
            pltpu.SemaphoreType.DMA((smoothed.shape[0],)),
        ],
        compiler_params=pltpu.CompilerParams(vmem_limit_bytes=VMEM_SUBTRACT),
        name="subtract",
    )(me, scales, owners, locals_, smoothed, *pieces)


TOGETHER = 2
CHAINS = 1
VMEM_SMOOTH = 48 * 1024 * 1024
VMEM_SMALL = 16 * 1024 * 1024
VMEM_SUBTRACT = 40 * 1024 * 1024


def body(images, coeffs, weights, scales, valid_epoch, patch_owner, patch_local):
    band_count = lax.axis_size("band")
    _, epochs, per_epoch, tile_rows, tile_side = images.shape
    down, up = reduce_stages(band_count), gather_stages(band_count)
    me = lax.axis_index("band").astype(jnp.int32).reshape(1)
    owners = patch_owner.reshape(epochs, per_epoch)
    locals_ = patch_local.reshape(epochs, per_epoch)

    smoothed, *messages = smooth(
        me, coeffs[0].transpose(2, 0, 1), weights, valid_epoch, owners, locals_, images[0], down, band_count)

    def exchange(value, step):
        return lax.ppermute(value, "band", [(d, d ^ step) for d in range(band_count)])

    chains = [messages[h * down[0]:(h + 1) * down[0]] for h in range(CHAINS)]
    stride = 1
    for k, factor in enumerate(down):
        for h in range(CHAINS):
            blocks = chains[h]
            parts = [blocks[0]] + [exchange(blocks[j], j * stride) for j in range(1, factor)]
            chains[h] = add_and_split(parts, down[k + 1]) if k + 1 < len(down) else parts
        stride *= factor

    pieces = [finish([part for chain in chains for part in chain], tile_rows)]
    stride = band_count
    for factor in reversed(up):
        stride //= factor
        if len(pieces) > 2:
            pieces = [join(pieces)]
        pieces = pieces + [exchange(piece, j * stride) for j in range(1, factor) for piece in pieces]

    difference, templates = subtract(me, scales, owners, locals_, pieces, smoothed, up)
    return difference[None], templates


def solution(mesh):
    return jax.shard_map(
        body,
        mesh=mesh,
        in_specs=(
            P(("groups", "band"), None, None, None, None),
            P(("groups", "band"), None, None, None),
            P(("groups", "band"), None),
            P(("groups", "band"), None),
            P(("groups", "band"), None),
            P(("groups", "band"), None, None, None),
            P(("groups", "band"), None, None),
        ),
        out_specs=(
            P(("groups", "band"), None, None, None, None),
            P(("groups", "band"), None, None),
        ),
        check_vma=False,
    )
```

time: 47.5 us -> 43.2 us (0.909)
  Pallas kernels: 13.8 us -> 10.8 us
  other arithmetic: 0.78 us -> 0 us
    pallas_call x1, Pallas kernels: 4.03 us -> 2.81 us  [subtract(): pl.pallas_call(functools.partial(difference_kernel, factors=factors, coun...]
    pallas_call x1, Pallas kernels: 8.9 us -> 7.79 us  [smooth(): pl.pallas_call(functools.partial(smooth_kernel, factors=factors, band_cou...]
    concatenate x1 -> x0, other arithmetic: 0.78 us -> none  [body(): pieces = [jnp.concatenate(pieces, axis=0)]]
    pallas_call x1 -> x2, Pallas kernels: 0.71 us -> 0.11 us  [the longest x1 0.1 us: finish(): pl.pallas_call(functools.partial(finish_kernel, part_rows=tile_rows // CH...]
where the time goes in v4:
time: 43.2 us; the launch traced here: 43.1 us
  waiting for transfers between devices  17.6 us (41%)
  starting transfers between devices  14 us (32%)
  Pallas kernels  10.8 us (25%)
  between operations  0.69 us (2%)
    ppermute x11, waiting for transfers between devices, exchange(): lax.ppermute(value, 'band', [(d, d ^ step) for d in range(band_count)])  17.6 us
    ppermute x11, starting transfers between devices, exchange(): lax.ppermute(value, 'band', [(d, d ^ step) for d in range(band_count)])  14 us
    pallas_call x1, Pallas kernels, smooth(): pl.pallas_call(functools.partial(smooth_kernel, factors=factors, band_cou...  7.79 us
    pallas_call x1, Pallas kernels, subtract(): pl.pallas_call(functools.partial(difference_kernel, factors=factors, coun...  2.81 us
  transfers between devices with their start and end apart: 11, of which 8 were waited for; matrix products, arithmetic and copies ran while one was open for 0% of the time, Pallas kernels for 0%

profile of v4, /device:TPU:0, one launch (start us, length us, event | category | flops | bytes accessed | tf_op | source)
XLA Modules:
  0.0 43.1 jit_solution(3308702855746412487)
XLA Ops:
  0.6 0.0 copy-start.1
  0.6 0.0 copy-start
  0.7 0.0 copy-start.2
  0.7 7.8 %smooth.1 = (f32[8,16,32,128]{3,2,1,0:T(8,128)S(1)}, bf16[8,136,128]{2,1,0:T(8,128)(2,1)S(1)}, bf16[8,136,128]{2,1,0:T(8,128)(2,1)S(1)}) custom-call(s32[1]{0:T(128)} %bitcast.me_ref, f32[1,8]{1,0:T(1,128)} %weight_ref.1, s32[1,8]{1,0:T(1,128)} %valid_ref.1, s32[8,16]{1,0:T(8,128)} %bitcast.8, s32[8,16]{1,0:T(8,128)} %bitcast.10, f32[3,8,27]{2,1,0:T(8,128)} %bitcast.13, ...), custom_call_target="tpu_custom_call" | custom-call | tf_op jit(solution)/shard_map/smooth/pallas_call | solution.py:200
  8.5 0.6 %collective-permute-start = (bf16[8,136,128]{2,1,0:T(8,128)(2,1)S(1)}, bf16[8,136,128]{2,1,0:T(8,128)(2,1)S(1)}, u32[]{:S(2)}, u32[]{:S(2)}) collective-permute-start(bf16[8,136,128]{2,1,0:T(8,128)(2,1)S(1)} %get-tuple-element.15), channel_id=1, source_target_pairs={{0,1},{1,0},{2,3},{3,2},{4,5},{5,4},{6,7},{7,6},{8,9},{9,8},{10,11... | collective-permute-start | bytes 835592 | tf_op jit(solution)/shard_map/ppermute | solution.py:347
  9.0 1.2 %collective-permute-done.refs_1_ = bf16[8,136,128]{2,1,0:T(8,128)(2,1)S(1)} collective-permute-done((bf16[8,136,128]{2,1,0:T(8,128)(2,1)S(1)}, bf16[8,136,128]{2,1,0:T(8,128)(2,1)S(1)}, u32[]{:S(2)}, u32[]{:S(2)}) %collective-permute-start) | collective-permute-done | bytes 278560 | tf_op jit(solution)/shard_map/ppermute | solution.py:347
  10.2 0.1 add_and_split.2
  10.3 3.0 %collective-permute-start.1 = (bf16[4,136,128]{2,1,0:T(8,128)(2,1)S(1)}, bf16[4,136,128]{2,1,0:T(8,128)(2,1)S(1)}, u32[]{:S(2)}, u32[]{:S(2)}) collective-permute-start(bf16[4,136,128]{2,1,0:T(8,128)(2,1)S(1)} %get-tuple-element.17), channel_id=1, source_target_pairs={{0,2},{1,3},{2,0},{3,1},{4,6},{5,7},{6,4},{7,5},{8,10},{9,11},{10,... | collective-permute-start | bytes 417800 | tf_op jit(solution)/shard_map/ppermute | solution.py:347
  13.3 4.0 %collective-permute-done.1.refs_1_ = bf16[4,136,128]{2,1,0:T(8,128)(2,1)S(1)} collective-permute-done((bf16[4,136,128]{2,1,0:T(8,128)(2,1)S(1)}, bf16[4,136,128]{2,1,0:T(8,128)(2,1)S(1)}, u32[]{:S(2)}, u32[]{:S(2)}) %collective-permute-start.1) | collective-permute-done | bytes 139296 | tf_op jit(solution)/shard_map/ppermute | solution.py:347
  17.3 1.8 %collective-permute-start.2 = (bf16[1,136,128]{2,1,0:T(8,128)(2,1)S(1)}, bf16[1,136,128]{2,1,0:T(8,128)(2,1)S(1)}, u32[]{:S(2)}, u32[]{:S(2)}) collective-permute-start(bf16[1,136,128]{2,1,0:T(8,128)(2,1)S(1)} %get-tuple-element.19), channel_id=1, source_target_pairs={{0,4},{1,5},{2,6},{3,7},{4,0},{5,1},{6,2},{7,3},{8,12},{9,13},{10,... | collective-permute-start | bytes 104456 | tf_op jit(solution)/shard_map/ppermute | solution.py:347
  19.1 2.6 %collective-permute-start.3 = (bf16[1,136,128]{2,1,0:T(8,128)(2,1)S(1)}, bf16[1,136,128]{2,1,0:T(8,128)(2,1)S(1)}, u32[]{:S(2)}, u32[]{:S(2)}) collective-permute-start(bf16[1,136,128]{2,1,0:T(8,128)(2,1)S(1)} %get-tuple-element.20), channel_id=1, source_target_pairs={{0,8},{1,9},{2,10},{3,11},{4,12},{5,13},{6,14},{7,15},{8,0},{9,1},... | collective-permute-start | bytes 104456 | tf_op jit(solution)/shard_map/ppermute | solution.py:347
  21.7 0.0 collective-permute-start.4
  21.7 0.0 collective-permute-done.2.refs_1_
  21.7 2.5 %collective-permute-done.3.refs_2_ = bf16[1,136,128]{2,1,0:T(8,128)(2,1)S(1)} collective-permute-done((bf16[1,136,128]{2,1,0:T(8,128)(2,1)S(1)}, bf16[1,136,128]{2,1,0:T(8,128)(2,1)S(1)}, u32[]{:S(2)}, u32[]{:S(2)}) %collective-permute-start.3) | collective-permute-done | bytes 34848 | tf_op jit(solution)/shard_map/ppermute | solution.py:347
  24.2 3.2 %collective-permute-done.4.refs_3_ = bf16[1,136,128]{2,1,0:T(8,128)(2,1)S(1)} collective-permute-done((bf16[1,136,128]{2,1,0:T(8,128)(2,1)S(1)}, bf16[1,136,128]{2,1,0:T(8,128)(2,1)S(1)}, u32[]{:S(2)}, u32[]{:S(2)}) %collective-permute-start.4) | collective-permute-done | bytes 34848 | tf_op jit(solution)/shard_map/ppermute | solution.py:347
  27.4 0.1 finish.1.refs_0_
  27.5 0.4 collective-permute-start.7
  27.9 0.0 collective-permute-start.6
  27.9 4.0 %collective-permute-start.5 = (bf16[4,32,128]{2,1,0:T(8,128)(2,1)S(1)}, bf16[4,32,128]{2,1,0:T(8,128)(2,1)S(1)}, u32[]{:S(2)}, u32[]{:S(2)}) collective-permute-start(bf16[4,32,128]{2,1,0:T(8,128)(2,1)S(1)} %finish.1.refs_0_), channel_id=1, source_target_pairs={{0,4},{1,5},{2,6},{3,7},{4,0},{5,1},{6,2},{7,3},{8,12},{9,13},{10,... | collective-permute-start | bytes 98312 | tf_op jit(solution)/shard_map/ppermute | solution.py:347
  31.9 1.3 %collective-permute-done.7.refs_3_ = bf16[4,32,128]{2,1,0:T(8,128)(2,1)S(1)} collective-permute-done((bf16[4,32,128]{2,1,0:T(8,128)(2,1)S(1)}, bf16[4,32,128]{2,1,0:T(8,128)(2,1)S(1)}, u32[]{:S(2)}, u32[]{:S(2)}) %collective-permute-start.7) | collective-permute-done | bytes 32800 | tf_op jit(solution)/shard_map/ppermute | solution.py:347
  33.3 0.0 collective-permute-done.6.refs_2_
  33.3 0.6 %collective-permute-done.5.refs_1_ = bf16[4,32,128]{2,1,0:T(8,128)(2,1)S(1)} collective-permute-done((bf16[4,32,128]{2,1,0:T(8,128)(2,1)S(1)}, bf16[4,32,128]{2,1,0:T(8,128)(2,1)S(1)}, u32[]{:S(2)}, u32[]{:S(2)}) %collective-permute-start.5) | collective-permute-done | bytes 32800 | tf_op jit(solution)/shard_map/ppermute | solution.py:347
  33.8 1.6 %collective-permute-start.8 = (bf16[16,32,128]{2,1,0:T(8,128)(2,1)S(1)}, bf16[16,32,128]{2,1,0:T(8,128)(2,1)S(1)}, u32[]{:S(2)}, u32[]{:S(2)}) collective-permute-start(bf16[16,32,128]{2,1,0:T(8,128)(2,1)S(1)} %join.1.rest_0_), channel_id=1, source_target_pairs={{0,2},{1,3},{2,0},{3,1},{4,6},{5,7},{6,4},{7,5},{8,10},{9,11},{10,... | collective-permute-start | bytes 393224 | tf_op jit(solution)/shard_map/ppermute | solution.py:347
  35.4 0.0 collective-permute-start.9
  35.4 3.5 %collective-permute-done.8.rest_1_ = bf16[16,32,128]{2,1,0:T(8,128)(2,1)S(1)} collective-permute-done((bf16[16,32,128]{2,1,0:T(8,128)(2,1)S(1)}, bf16[16,32,128]{2,1,0:T(8,128)(2,1)S(1)}, u32[]{:S(2)}, u32[]{:S(2)}) %collective-permute-start.8) | collective-permute-done | bytes 131104 | tf_op jit(solution)/shard_map/ppermute | solution.py:347
  38.9 0.0 collective-permute-start.10
  38.9 0.0 collective-permute-done.9.rest_2_
  38.9 1.3 %collective-permute-done.10.rest_3_ = bf16[16,32,128]{2,1,0:T(8,128)(2,1)S(1)} collective-permute-done((bf16[16,32,128]{2,1,0:T(8,128)(2,1)S(1)}, bf16[16,32,128]{2,1,0:T(8,128)(2,1)S(1)}, u32[]{:S(2)}, u32[]{:S(2)}) %collective-permute-start.10) | collective-permute-done | bytes 131104 | tf_op jit(solution)/shard_map/ppermute | solution.py:347
  40.2 0.0 copy-done.1
  40.2 0.0 copy-done
  40.2 0.0 copy-done.2
  40.2 2.8 %subtract.1 = (f32[8,16,32,128]{3,2,1,0:T(8,128)}, bf16[4,32,128]{2,1,0:T(8,128)(2,1)}) custom-call(s32[1]{0:T(128)} %bitcast.me_ref, f32[1,8]{1,0:T(1,128)S(1)} %copy-done.2, s32[8,16]{1,0:T(8,128)S(1)} %bitcast.9, s32[8,16]{1,0:T(8,128)S(1)} %bitcast.11, f32[8,16,32,128]{3,2,1,0:T(8,128)S(1)} %get-tuple-element.13.smooth_ref, ...), custom_call_target="tpu_custom_call" | custom-call | tf_op jit(solution)/shard_map/subtract/pallas_call | solution.py:313
  (2 shorter events, 0.0 us)
Async XLA Ops:
  0.6 39.6 %copy-start.1 = (s32[1,8,16]{2,1,0:T(8,128)S(1)}, s32[1,8,16]{2,1,0:T(8,128)}, u32[]{:S(2)}) copy-start(s32[1,8,16]{2,1,0:T(8,128)} %param.16) | copy-start | bytes 1540
  0.6 39.6 %copy-start = (s32[1,8,16,1]{2,3,1,0:T(1,128)S(1)}, s32[1,8,16,1]{2,3,1,0:T(1,128)}, u32[]{:S(2)}) copy-start(s32[1,8,16,1]{2,3,1,0:T(1,128)} %param.15) | copy-start | bytes 1540
  0.7 39.6 %copy-start.2 = (f32[1,8]{1,0:T(1,128)S(1)}, f32[1,8]{1,0:T(1,128)}, u32[]{:S(2)}) copy-start(f32[1,8]{1,0:T(1,128)} %scale_ref.1) | copy-start | bytes 100
  8.5 1.8 %collective-permute-start = (bf16[8,136,128]{2,1,0:T(8,128)(2,1)S(1)}, bf16[8,136,128]{2,1,0:T(8,128)(2,1)S(1)}, u32[]{:S(2)}, u32[]{:S(2)}) collective-permute-start(bf16[8,136,128]{2,1,0:T(8,128)(2,1)S(1)} %get-tuple-element.15), channel_id=1, source_target_pairs={{0,1},{1,0},{2,3},{3,2},{4,5},{5,4},{6,7},{7,6},{8,9},{9,8},{10,11... | collective-permute-start | bytes 835592 | tf_op jit(solution)/shard_map/ppermute | solution.py:347
  10.3 6.9 %collective-permute-start.1 = (bf16[4,136,128]{2,1,0:T(8,128)(2,1)S(1)}, bf16[4,136,128]{2,1,0:T(8,128)(2,1)S(1)}, u32[]{:S(2)}, u32[]{:S(2)}) collective-permute-start(bf16[4,136,128]{2,1,0:T(8,128)(2,1)S(1)} %get-tuple-element.17), channel_id=1, source_target_pairs={{0,2},{1,3},{2,0},{3,1},{4,6},{5,7},{6,4},{7,5},{8,10},{9,11},{10,... | collective-permute-start | bytes 417800 | tf_op jit(solution)/shard_map/ppermute | solution.py:347
  17.3 4.5 %collective-permute-start.2 = (bf16[1,136,128]{2,1,0:T(8,128)(2,1)S(1)}, bf16[1,136,128]{2,1,0:T(8,128)(2,1)S(1)}, u32[]{:S(2)}, u32[]{:S(2)}) collective-permute-start(bf16[1,136,128]{2,1,0:T(8,128)(2,1)S(1)} %get-tuple-element.19), channel_id=1, source_target_pairs={{0,4},{1,5},{2,6},{3,7},{4,0},{5,1},{6,2},{7,3},{8,12},{9,13},{10,... | collective-permute-start | bytes 104456 | tf_op jit(solution)/shard_map/ppermute | solution.py:347
  19.1 5.1 %collective-permute-start.3 = (bf16[1,136,128]{2,1,0:T(8,128)(2,1)S(1)}, bf16[1,136,128]{2,1,0:T(8,128)(2,1)S(1)}, u32[]{:S(2)}, u32[]{:S(2)}) collective-permute-start(bf16[1,136,128]{2,1,0:T(8,128)(2,1)S(1)} %get-tuple-element.20), channel_id=1, source_target_pairs={{0,8},{1,9},{2,10},{3,11},{4,12},{5,13},{6,14},{7,15},{8,0},{9,1},... | collective-permute-start | bytes 104456 | tf_op jit(solution)/shard_map/ppermute | solution.py:347
  21.7 5.7 %collective-permute-start.4 = (bf16[1,136,128]{2,1,0:T(8,128)(2,1)S(1)}, bf16[1,136,128]{2,1,0:T(8,128)(2,1)S(1)}, u32[]{:S(2)}, u32[]{:S(2)}) collective-permute-start(bf16[1,136,128]{2,1,0:T(8,128)(2,1)S(1)} %get-tuple-element.21), channel_id=1, source_target_pairs={{0,12},{1,13},{2,14},{3,15},{4,8},{5,9},{6,10},{7,11},{8,4},{9,5},... | collective-permute-start | bytes 104456 | tf_op jit(solution)/shard_map/ppermute | solution.py:347
  27.5 5.7 %collective-permute-start.7 = (bf16[4,32,128]{2,1,0:T(8,128)(2,1)S(1)}, bf16[4,32,128]{2,1,0:T(8,128)(2,1)S(1)}, u32[]{:S(2)}, u32[]{:S(2)}) collective-permute-start(bf16[4,32,128]{2,1,0:T(8,128)(2,1)S(1)} %finish.1.refs_0_), channel_id=1, source_target_pairs={{0,12},{1,13},{2,14},{3,15},{4,8},{5,9},{6,10},{7,11},{8,4},{9,5},... | collective-permute-start | bytes 98312 | tf_op jit(solution)/shard_map/ppermute | solution.py:347
  27.9 5.3 %collective-permute-start.6 = (bf16[4,32,128]{2,1,0:T(8,128)(2,1)S(1)}, bf16[4,32,128]{2,1,0:T(8,128)(2,1)S(1)}, u32[]{:S(2)}, u32[]{:S(2)}) collective-permute-start(bf16[4,32,128]{2,1,0:T(8,128)(2,1)S(1)} %finish.1.refs_0_), channel_id=1, source_target_pairs={{0,8},{1,9},{2,10},{3,11},{4,12},{5,13},{6,14},{7,15},{8,0},{9,1},... | collective-permute-start | bytes 98312 | tf_op jit(solution)/shard_map/ppermute | solution.py:347
  27.9 5.9 %collective-permute-start.5 = (bf16[4,32,128]{2,1,0:T(8,128)(2,1)S(1)}, bf16[4,32,128]{2,1,0:T(8,128)(2,1)S(1)}, u32[]{:S(2)}, u32[]{:S(2)}) collective-permute-start(bf16[4,32,128]{2,1,0:T(8,128)(2,1)S(1)} %finish.1.refs_0_), channel_id=1, source_target_pairs={{0,4},{1,5},{2,6},{3,7},{4,0},{5,1},{6,2},{7,3},{8,12},{9,13},{10,... | collective-permute-start | bytes 98312 | tf_op jit(solution)/shard_map/ppermute | solution.py:347
  33.8 5.0 %collective-permute-start.8 = (bf16[16,32,128]{2,1,0:T(8,128)(2,1)S(1)}, bf16[16,32,128]{2,1,0:T(8,128)(2,1)S(1)}, u32[]{:S(2)}, u32[]{:S(2)}) collective-permute-start(bf16[16,32,128]{2,1,0:T(8,128)(2,1)S(1)} %join.1.rest_0_), channel_id=1, source_target_pairs={{0,2},{1,3},{2,0},{3,1},{4,6},{5,7},{6,4},{7,5},{8,10},{9,11},{10,... | collective-permute-start | bytes 393224 | tf_op jit(solution)/shard_map/ppermute | solution.py:347
  35.4 3.5 %collective-permute-start.9 = (bf16[16,32,128]{2,1,0:T(8,128)(2,1)S(1)}, bf16[16,32,128]{2,1,0:T(8,128)(2,1)S(1)}, u32[]{:S(2)}, u32[]{:S(2)}) collective-permute-start(bf16[16,32,128]{2,1,0:T(8,128)(2,1)S(1)} %join.1.rest_0_), channel_id=1, source_target_pairs={{0,1},{1,0},{2,3},{3,2},{4,5},{5,4},{6,7},{7,6},{8,9},{9,8},{10,11... | collective-permute-start | bytes 393224 | tf_op jit(solution)/shard_map/ppermute | solution.py:347
  38.9 1.3 %collective-permute-start.10 = (bf16[16,32,128]{2,1,0:T(8,128)(2,1)S(1)}, bf16[16,32,128]{2,1,0:T(8,128)(2,1)S(1)}, u32[]{:S(2)}, u32[]{:S(2)}) collective-permute-start(bf16[16,32,128]{2,1,0:T(8,128)(2,1)S(1)} %collective-permute-done.8.rest_1_), channel_id=1, source_target_pairs={{0,1},{1,0},{2,3},{3,2},{4,5},{5,4},{6,7},{7,6},{8,9},{9,8},{10,11... | collective-permute-start | bytes 393224 | tf_op jit(solution)/shard_map/ppermute | solution.py:347

commit v5 on v4

--- a/solution.py
+++ b/solution.py
@@ -7,6 +7,7 @@
 from jax.experimental import pallas as pl
 from jax.experimental.pallas import tpu as pltpu
 from jax.sharding import PartitionSpec as P
+
 
 PD = 4
 HALF = 9
@@ -70,48 +71,61 @@
 
 
 def smooth_kernel(
-    me_ref, weight_ref, valid_ref, owner_ref, local_ref, coef_ref, image_ref, column_ref, row_ref, spread_ref,
+    me_ref, weight_hbm, valid_hbm, owner_hbm, local_hbm, coef_hbm, spread_hbm, column_hbm, row_hbm, image_hbm,
     smooth_ref, *rest, factors, band_count, row_count, layers,
 ):
-    message_refs = rest[:-(2 * TOGETHER + 2)]
-    total_ref, factor_ref = rest[-(2 * TOGETHER + 2):-2 * TOGETHER]
-    mixer_refs, column_pass_refs = rest[-2 * TOGETHER:-TOGETHER], rest[-TOGETHER:]
-    step = pl.program_id(0)
-    together, per_epoch, tile_rows, tile_side = image_ref.shape
-    epochs = smooth_ref.shape[0]
+    message_refs, rest = rest[:factors[0]], rest[factors[0]:]
+    weight_ref, valid_ref, owner_ref, local_ref, coef_ref, spread_ref, column_ref, row_ref, held_ref = rest[:9]
+    small_sems, image_sems, total_ref, factor_ref = rest[9:13]
+    mixer_refs, column_pass_refs = rest[13:13 + 2 * TOGETHER], rest[13 + 2 * TOGETHER:]
+    epochs, per_epoch, tile_rows, tile_side = smooth_ref.shape
     depth = row_count * tile_rows
 
-    @pl.when(step == 0)
-    def _():
-        total_ref[...] = jnp.zeros_like(total_ref)
-        coefs = coef_ref[...].reshape(P_SIZE * epochs, coef_ref.shape[2])
-        for k in range(len(layers)):
-            factor_ref[k] = jnp.dot(
-                coefs, spread_ref[k], precision=lax.Precision.HIGHEST, preferred_element_type=F32)
+    small = [pltpu.make_async_copy(source, target, small_sems.at[k]) for k, (source, target) in enumerate((
+        (coef_hbm, coef_ref), (spread_hbm, spread_ref), (row_hbm, row_ref), (column_hbm, column_ref),
+        (weight_hbm, weight_ref), (valid_hbm, valid_ref), (owner_hbm, owner_ref), (local_hbm, local_ref)))]
+    images = [
+        pltpu.make_async_copy(image_hbm.at[epoch], held_ref.at[epoch], image_sems.at[epoch])
+        for epoch in range(epochs)]
+    for copy in small[:4] + images[:TOGETHER] + small[4:] + images[TOGETHER:]:
+        copy.start()
+
+    total_ref[...] = jnp.zeros_like(total_ref)
+    small[0].wait()
+    small[1].wait()
+    left = coef_ref[...].reshape(P_SIZE * epochs, coef_ref.shape[2])
+    spread_coefs = None
+    for _ in range(3):
+        piece = left.astype(BF16)
+        left = left - piece.astype(F32)
+        term = jnp.dot(piece, spread_ref[...], preferred_element_type=F32)
+        spread_coefs = term if spread_coefs is None else spread_coefs + term
+    for k in range(len(layers)):
+        factor_ref[k] = spread_coefs[:, k * tile_side:(k + 1) * tile_side]
+    for copy in small[2:]:
+        copy.wait()
 
     row = lax.broadcasted_iota(jnp.int32, (tile_rows, tile_side), 0).astype(F32)
     column = lax.broadcasted_iota(jnp.int32, (tile_rows, tile_side), 1).astype(F32)
     lane = lax.broadcasted_iota(jnp.int32, (8, tile_side), 1)
     down = 2.0 * (row + 0.5) / tile_rows - 1.0
 
-    for sub in range(together):
-        epoch = step * together + sub
-        mixer_ref, column_pass_ref = mixer_refs[sub], column_pass_refs[sub]
-
+    def mixers(epoch, mixer_ref):
         for block in range(mixer_ref.shape[0]):
             sums = []
             for m in range(P_SIZE):
                 value = None
                 for k, owner in enumerate(layers):
                     if owner == block:
-                        factor = factor_ref[k, pl.ds(m * epochs + epoch, 1), :]
+                        factor = factor_ref[k, m * epochs + epoch:m * epochs + epoch + 1, :]
                         term = factor * row_ref[k]
                         value = term if value is None else value + term
                 sums.append(value)
             mixer_ref[block, :tile_rows] = (sums[0] + down * sums[2]).astype(BF16)
             mixer_ref[block, tile_rows:] = sums[1].astype(BF16)
 
-        pixels = image_ref[sub].reshape(per_epoch * tile_rows, tile_side).astype(BF16)
+    def column_pass(epoch, column_pass_ref):
+        pixels = held_ref[epoch].reshape(per_epoch * tile_rows, tile_side).astype(BF16)
         for c in range(0, row_count, 2):
             wide = min(2, row_count - c)
             passed = jnp.dot(
@@ -121,9 +135,7 @@
                     column_pass_ref[t, (c + s) * tile_rows:(c + s + 1) * tile_rows] = (
                         passed[t * tile_rows:(t + 1) * tile_rows, s * tile_side:(s + 1) * tile_side])
 
-    for sub in range(together):
-        epoch = step * together + sub
-        mixer_ref, column_pass_ref = mixer_refs[sub], column_pass_refs[sub]
+    def row_pass(epoch, mixer_ref, column_pass_ref):
         mixer = jnp.concatenate([mixer_ref[block] for block in range(mixer_ref.shape[0])], axis=1)[:, :depth]
         weight = jnp.full((8, tile_side), weight_ref[0, epoch] * valid_ref[0, epoch].astype(F32), F32)
         weight = weight.astype(BF16).astype(F32)
@@ -143,23 +155,31 @@
                 total_ref[place, tile_rows:] = (
                     total_ref[place, tile_rows:] + jnp.where(lane == t % tile_side, weight, 0.0))
 
-    @pl.when(step == pl.num_programs(0) - 1)
-    def _():
-        groups = factors[0]
-        per_group = band_count // groups
-        line = lax.broadcasted_iota(jnp.int32, (8, tile_side), 0)
-        part_rows = tile_rows // CHAINS
-        for g in range(groups):
-            @pl.loop(0, per_group)
-            def _(i):
-                block = (g * per_group + i) * PD
-                marks = jnp.zeros((8, tile_side), F32)
-                for q in range(PD):
-                    for h in range(CHAINS):
-                        message_refs[h * groups + g][i, q * part_rows:(q + 1) * part_rows, :] = (
-                            total_ref[block + q, h * part_rows:(h + 1) * part_rows].astype(BF16))
-                    marks = jnp.where(line == q, total_ref[block + q, tile_rows:], marks)
-                message_refs[g][i, PD * part_rows:, :] = marks.astype(BF16)
+    for step in range(epochs // TOGETHER + 1):
+        now = range(step * TOGETHER, min(epochs, (step + 1) * TOGETHER))
+        for epoch in now:
+            images[epoch].wait()
+        before = range((step - 1) * TOGETHER, step * TOGETHER) if step else ()
+        for k in range(TOGETHER):
+            for epoch in now[k:k + 1]:
+                column_pass(epoch, column_pass_refs[epoch % (2 * TOGETHER)])
+                mixers(epoch, mixer_refs[epoch % (2 * TOGETHER)])
+            for epoch in before[k:k + 1]:
+                slot = epoch % (2 * TOGETHER)
+                row_pass(epoch, mixer_refs[slot], column_pass_refs[slot])
+
+    per_group = band_count // factors[0]
+    line = lax.broadcasted_iota(jnp.int32, (8, tile_side), 0)
+    for g in range(factors[0]):
+        @pl.loop(0, per_group)
+        def _(i):
+            block = (g * per_group + i) * PD
+            marks = jnp.zeros((8, tile_side), F32)
+            for q in range(PD):
+                message_refs[g][i, q * tile_rows:(q + 1) * tile_rows, :] = (
+                    total_ref[block + q, :tile_rows].astype(BF16))
+                marks = jnp.where(line == q, total_ref[block + q, tile_rows:], marks)
+            message_refs[g][i, PD * tile_rows:, :] = marks.astype(BF16)
 
 
 VMEM = pl.BlockSpec(memory_space=pltpu.VMEM)
@@ -186,38 +206,33 @@
                     lanes = slice(i * tile_rows, (i + 1) * tile_rows)
                     rows[-1][:, lanes] = row_matrices[pairs[bases[depth]][0]]
                     spread[-1][bases[depth], lanes] = 1.0
-    rows, spread = np.stack(rows), np.stack(spread)
-    part_rows = PD * tile_rows // CHAINS
+    rows = jnp.asarray(np.stack(rows))
+    spread = jnp.asarray(np.concatenate(spread, axis=1), BF16)
+    block_rows = PD * tile_rows + EXTRA
     per_group = band_count // factors[0]
-    tile_block = pl.BlockSpec((TOGETHER, per_epoch, tile_rows, tile_side), lambda e: (e, 0, 0, 0))
-
-    def whole(shape):
-        return pl.BlockSpec(shape, lambda e: (0,) * len(shape), pipeline_mode=pl.Buffered(1))
-
-    messages = [
-        jax.ShapeDtypeStruct((per_group, part_rows + (EXTRA if h == 0 else 0), tile_side), BF16)
-        for h in range(CHAINS) for _ in range(factors[0])]
+    messages = [jax.ShapeDtypeStruct((per_group, block_rows, tile_side), BF16)] * factors[0]
     return pl.pallas_call(
         functools.partial(smooth_kernel, factors=factors, band_count=band_count, row_count=row_count,
             layers=layers),
-        grid=(epochs // TOGETHER,),
-        in_specs=[SMEM] * 5 + [
-            whole(coeffs.shape), tile_block, whole(columns.shape), whole(rows.shape), whole(spread.shape)],
+        in_specs=[SMEM] + [pl.BlockSpec(memory_space=pltpu.HBM)] * 9,
         out_specs=[VMEM] * (1 + len(messages)),
         out_shape=[jax.ShapeDtypeStruct(images.shape, F32)] + messages,
         scratch_shapes=[
+            *(pltpu.SMEM(value.shape, value.dtype) for value in (weights, valid_epoch, owners, locals_)),
+            *(pltpu.VMEM(value.shape, value.dtype) for value in (coeffs, spread, columns, rows, images)),
+            pltpu.SemaphoreType.DMA((8,)),
+            pltpu.SemaphoreType.DMA((epochs,)),
             pltpu.VMEM((band_count * PD, tile_rows + 8, tile_side), F32),
             pltpu.VMEM((len(layers), P_SIZE * epochs, tile_side), F32),
         ] + [
             pltpu.VMEM((-(-row_count // per_lanes), 2 * tile_rows, tile_side), BF16),
-        ] * TOGETHER + [
+        ] * (2 * TOGETHER) + [
             pltpu.VMEM((per_epoch, row_count * tile_rows, tile_side), BF16),
-        ] * TOGETHER,
-        compiler_params=pltpu.CompilerParams(
-            dimension_semantics=("arbitrary",), vmem_limit_bytes=VMEM_SMOOTH),
+        ] * (2 * TOGETHER),
+        compiler_params=pltpu.CompilerParams(vmem_limit_bytes=VMEM_SMOOTH),
         name="smooth",
     )(me, *[pltpu.with_memory_space_constraint(value, pltpu.HBM) for value in (
-        weights, valid_epoch, owners, locals_, coeffs, images, columns, jnp.asarray(rows), jnp.asarray(spread))])
+        weights, valid_epoch, owners, locals_, coeffs, spread, columns, rows, images)])
 
 
 def add_kernel(*refs, count, groups):
@@ -242,26 +257,21 @@
     )(*parts)
 
 
-def finish_kernel(*refs, part_rows):
+def finish_kernel(*refs):
     *parts, out_ref = refs
-    each = len(parts) // CHAINS
-    inverse = None
-    for h in range(CHAINS):
-        total = parts[h * each][0].astype(F32)
-        for part in parts[h * each + 1:(h + 1) * each]:
-            total = total + part[0].astype(F32)
-        if h == 0:
-            marks = total[PD * part_rows:, :]
-            inverse = jnp.broadcast_to(1.0 / (1.0 + jnp.sum(marks, axis=1, keepdims=True)), marks.shape)
-        for q in range(PD):
-            out_ref[q, h * part_rows:(h + 1) * part_rows] = (
-                total[q * part_rows:(q + 1) * part_rows] * inverse[q:q + 1]).astype(BF16)
+    tile_rows = out_ref.shape[1]
+    total = parts[0][0].astype(F32)
+    for part in parts[1:]:
+        total = total + part[0].astype(F32)
+    marks = total[PD * tile_rows:, :]
+    inverse = jnp.broadcast_to(1.0 / (1.0 + jnp.sum(marks, axis=1, keepdims=True)), marks.shape)
+    for q in range(PD):
+        out_ref[q] = (total[q * tile_rows:(q + 1) * tile_rows] * inverse[q:q + 1]).astype(BF16)
 
 
 def finish(parts, tile_rows):
     return pl.pallas_call(
-        functools.partial(finish_kernel, part_rows=tile_rows // CHAINS),
-        in_specs=[VMEM] * len(parts), out_specs=VMEM,
+        finish_kernel, in_specs=[VMEM] * len(parts), out_specs=VMEM,
         out_shape=jax.ShapeDtypeStruct((PD, tile_rows, parts[0].shape[2]), BF16), name="finish",
         compiler_params=pltpu.CompilerParams(vmem_limit_bytes=VMEM_SMALL),
     )(*parts)
@@ -326,7 +336,6 @@
 
 
 TOGETHER = 2
-CHAINS = 1
 VMEM_SMOOTH = 48 * 1024 * 1024
 VMEM_SMALL = 16 * 1024 * 1024
 VMEM_SUBTRACT = 40 * 1024 * 1024
@@ -334,7 +343,7 @@
 
 def body(images, coeffs, weights, scales, valid_epoch, patch_owner, patch_local):
     band_count = lax.axis_size("band")
-    _, epochs, per_epoch, tile_rows, tile_side = images.shape
+    _, epochs, per_epoch, tile_rows, _ = images.shape
     down, up = reduce_stages(band_count), gather_stages(band_count)
     me = lax.axis_index("band").astype(jnp.int32).reshape(1)
     owners = patch_owner.reshape(epochs, per_epoch)
@@ -346,22 +355,29 @@
     def exchange(value, step):
         return lax.ppermute(value, "band", [(d, d ^ step) for d in range(band_count)])
 
-    chains = [messages[h * down[0]:(h + 1) * down[0]] for h in range(CHAINS)]
-    stride = 1
-    for k, factor in enumerate(down):
-        for h in range(CHAINS):
-            blocks = chains[h]
-            parts = [blocks[0]] + [exchange(blocks[j], j * stride) for j in range(1, factor)]
-            chains[h] = add_and_split(parts, down[k + 1]) if k + 1 < len(down) else parts
-        stride *= factor
-
-    pieces = [finish([part for chain in chains for part in chain], tile_rows)]
-    stride = band_count
-    for factor in reversed(up):
-        stride //= factor
-        if len(pieces) > 2:
-            pieces = [join(pieces)]
-        pieces = pieces + [exchange(piece, j * stride) for j in range(1, factor) for piece in pieces]
+    first, second, third = down
+    half = third // 2
+    parts = [messages[0]] + [exchange(messages[j], j) for j in range(1, first)]
+    split = add_and_split(parts, 2 * second)
+    near, far = split[0::2], split[1::2]
+    far = [far[0]] + [exchange(far[j], j * first) for j in range(1, second)]
+    near = [near[0]] + [exchange(near[j], j * first) for j in range(1, second)]
+    stride = first * second
+    far = add_and_split(far, third - half)
+    arrived = [exchange(far[j - half], j * stride) for j in reversed(range(half, third))]
+    near = add_and_split(near, half)
+    arrived = [near[0]] + [exchange(near[j], j * stride) for j in range(1, half)] + arrived
+
+    pieces = [finish(arrived, tile_rows)]
+    own = pieces[0]
+    distant = [exchange(own, j * stride) for j in reversed(range(half, third))][::-1]
+    close = [own] + [exchange(own, j * stride) for j in range(1, half)]
+    halves = [join(close) if len(close) > 1 else close[0], join(distant) if len(distant) > 1 else distant[0]]
+    pieces = []
+    for piece in halves:
+        pieces.append([piece] + [exchange(piece, j * first) for j in range(1, second)])
+    pieces = [piece for pair in zip(*pieces) for piece in pair]
+    pieces = pieces + [exchange(piece, j) for j in range(1, first) for piece in pieces]
 
     difference, templates = subtract(me, scales, owners, locals_, pieces, smoothed, up)
     return difference[None], templates

time: 43.2 us -> 41.4 us (0.958)
  waiting for transfers between devices: 17.6 us -> 14.3 us
  starting transfers between devices: 14 us -> 15.8 us
    ppermute x11 -> x15, waiting for transfers between devices: 17.6 us -> 14.3 us  [exchange(): lax.ppermute(value, 'band', [(d, d ^ step) for d in range(band_count)])]
    ppermute x11 -> x15, starting transfers between devices: 14 us -> 15.8 us  [exchange(): lax.ppermute(value, 'band', [(d, d ^ step) for d in range(band_count)])]
    pallas_call x1, Pallas kernels: 7.79 us -> 7.35 us  [smooth(): pl.pallas_call(functools.partial(smooth_kernel, factors=factors, band_cou...]
  transfers between devices with their start and end apart: 11 -> 15, of which waited for: 8 -> 9; matrix products, arithmetic and copies ran while one was open for 0% -> 0% of each run, Pallas kernels for 0% -> 0%
where the time goes in v5:
time: 41.4 us; the launch traced here: 41.2 us
  starting transfers between devices  15.8 us (38%)
  waiting for transfers between devices  14.3 us (35%)
  Pallas kernels  10.4 us (25%)
  between operations  0.71 us (2%)
    ppermute x15, starting transfers between devices, exchange(): lax.ppermute(value, 'band', [(d, d ^ step) for d in range(band_count)])  15.8 us
    ppermute x15, waiting for transfers between devices, exchange(): lax.ppermute(value, 'band', [(d, d ^ step) for d in range(band_count)])  14.3 us
    pallas_call x1, Pallas kernels, smooth(): pl.pallas_call(functools.partial(smooth_kernel, factors=factors, band_cou...  7.35 us
    pallas_call x1, Pallas kernels, subtract(): pl.pallas_call(functools.partial(difference_kernel, factors=factors, coun...  2.82 us
  transfers between devices with their start and end apart: 15, of which 9 were waited for; matrix products, arithmetic and copies ran while one was open for 0% of the time, Pallas kernels for 0%

profile of v5, /device:TPU:0, one launch (start us, length us, event | category | flops | bytes accessed | tf_op | source)
XLA Modules:
  0.0 41.2 jit_solution(10279941860301632335)
XLA Ops:
  0.6 0.0 copy-start.1
  0.6 0.0 copy-start
  0.7 0.0 copy-start.2
  0.7 7.3 %smooth.1 = (f32[8,16,32,128]{3,2,1,0:T(8,128)S(1)}, bf16[8,136,128]{2,1,0:T(8,128)(2,1)S(1)}, bf16[8,136,128]{2,1,0:T(8,128)(2,1)S(1)}) custom-call(s32[1]{0:T(128)} %bitcast.me_ref, f32[1,8]{1,0:T(1,128)} %weight_hbm.1, s32[1,8]{1,0:T(1,128)} %valid_hbm.1, s32[8,16]{1,0:T(8,128)} %bitcast.8, s32[8,16]{1,0:T(8,128)} %bitcast.10, f32[3,8,27]{2,1,0:T(8,128)} %bitcast.13, ...), custom_call_target="tpu_custom_call" | custom-call | tf_op jit(solution)/shard_map/smooth/pallas_call | solution.py:214
  8.0 0.6 %collective-permute-start = (bf16[8,136,128]{2,1,0:T(8,128)(2,1)S(1)}, bf16[8,136,128]{2,1,0:T(8,128)(2,1)S(1)}, u32[]{:S(2)}, u32[]{:S(2)}) collective-permute-start(bf16[8,136,128]{2,1,0:T(8,128)(2,1)S(1)} %get-tuple-element.17), channel_id=1, source_target_pairs={{0,1},{1,0},{2,3},{3,2},{4,5},{5,4},{6,7},{7,6},{8,9},{9,8},{10,11... | collective-permute-start | bytes 835592 | tf_op jit(solution)/shard_map/ppermute | solution.py:356
  8.6 1.2 %collective-permute-done.refs_1_ = bf16[8,136,128]{2,1,0:T(8,128)(2,1)S(1)} collective-permute-done((bf16[8,136,128]{2,1,0:T(8,128)(2,1)S(1)}, bf16[8,136,128]{2,1,0:T(8,128)(2,1)S(1)}, u32[]{:S(2)}, u32[]{:S(2)}) %collective-permute-start) | collective-permute-done | bytes 278560 | tf_op jit(solution)/shard_map/ppermute | solution.py:356
  9.8 0.1 add_and_split.3
  9.8 3.0 %collective-permute-start.1 = (bf16[2,136,128]{2,1,0:T(8,128)(2,1)S(1)}, bf16[2,136,128]{2,1,0:T(8,128)(2,1)S(1)}, u32[]{:S(2)}, u32[]{:S(2)}) collective-permute-start(bf16[2,136,128]{2,1,0:T(8,128)(2,1)S(1)} %get-tuple-element.19), channel_id=1, source_target_pairs={{0,2},{1,3},{2,0},{3,1},{4,6},{5,7},{6,4},{7,5},{8,10},{9,11},{10,... | collective-permute-start | bytes 208904 | tf_op jit(solution)/shard_map/ppermute | solution.py:356
  12.8 0.1 collective-permute-start.3
  12.9 2.4 %collective-permute-done.1.refs_1_ = bf16[2,136,128]{2,1,0:T(8,128)(2,1)S(1)} collective-permute-done((bf16[2,136,128]{2,1,0:T(8,128)(2,1)S(1)}, bf16[2,136,128]{2,1,0:T(8,128)(2,1)S(1)}, u32[]{:S(2)}, u32[]{:S(2)}) %collective-permute-start.1) | collective-permute-done | bytes 69664 | tf_op jit(solution)/shard_map/ppermute | solution.py:356
  15.3 2.2 %collective-permute-start.2 = (bf16[1,136,128]{2,1,0:T(8,128)(2,1)S(1)}, bf16[1,136,128]{2,1,0:T(8,128)(2,1)S(1)}, u32[]{:S(2)}, u32[]{:S(2)}) collective-permute-start(bf16[1,136,128]{2,1,0:T(8,128)(2,1)S(1)} %get-tuple-element.21), channel_id=1, source_target_pairs={{0,4},{1,5},{2,6},{3,7},{4,0},{5,1},{6,2},{7,3},{8,12},{9,13},{10,... | collective-permute-start | bytes 104456 | tf_op jit(solution)/shard_map/ppermute | solution.py:356
  17.6 0.0 collective-permute-done.3.refs_1_
  17.6 3.2 %collective-permute-start.4 = (bf16[1,136,128]{2,1,0:T(8,128)(2,1)S(1)}, bf16[1,136,128]{2,1,0:T(8,128)(2,1)S(1)}, u32[]{:S(2)}, u32[]{:S(2)}) collective-permute-start(bf16[1,136,128]{2,1,0:T(8,128)(2,1)S(1)} %get-tuple-element.24), channel_id=1, source_target_pairs={{0,12},{1,13},{2,14},{3,15},{4,8},{5,9},{6,10},{7,11},{8,4},{9,5},... | collective-permute-start | bytes 104456 | tf_op jit(solution)/shard_map/ppermute | solution.py:356
  20.8 0.0 collective-permute-start.5
  20.8 0.0 collective-permute-done.2.refs_1_
  20.8 2.6 %collective-permute-done.4.refs_2_ = bf16[1,136,128]{2,1,0:T(8,128)(2,1)S(1)} collective-permute-done((bf16[1,136,128]{2,1,0:T(8,128)(2,1)S(1)}, bf16[1,136,128]{2,1,0:T(8,128)(2,1)S(1)}, u32[]{:S(2)}, u32[]{:S(2)}) %collective-permute-start.4) | collective-permute-done | bytes 34848 | tf_op jit(solution)/shard_map/ppermute | solution.py:356
  23.4 2.2 %collective-permute-done.5.refs_3_ = bf16[1,136,128]{2,1,0:T(8,128)(2,1)S(1)} collective-permute-done((bf16[1,136,128]{2,1,0:T(8,128)(2,1)S(1)}, bf16[1,136,128]{2,1,0:T(8,128)(2,1)S(1)}, u32[]{:S(2)}, u32[]{:S(2)}) %collective-permute-start.5) | collective-permute-done | bytes 34848 | tf_op jit(solution)/shard_map/ppermute | solution.py:356
  25.6 0.1 finish.1.refs_0_
  25.7 0.0 collective-permute-start.6
  25.8 1.9 %collective-permute-start.8 = (bf16[4,32,128]{2,1,0:T(8,128)(2,1)S(1)}, bf16[4,32,128]{2,1,0:T(8,128)(2,1)S(1)}, u32[]{:S(2)}, u32[]{:S(2)}) collective-permute-start(bf16[4,32,128]{2,1,0:T(8,128)(2,1)S(1)} %finish.1.refs_0_), channel_id=1, source_target_pairs={{0,12},{1,13},{2,14},{3,15},{4,8},{5,9},{6,10},{7,11},{8,4},{9,5},... | collective-permute-start | bytes 98312 | tf_op jit(solution)/shard_map/ppermute | solution.py:356
  27.7 1.6 %collective-permute-start.7 = (bf16[4,32,128]{2,1,0:T(8,128)(2,1)S(1)}, bf16[4,32,128]{2,1,0:T(8,128)(2,1)S(1)}, u32[]{:S(2)}, u32[]{:S(2)}) collective-permute-start(bf16[4,32,128]{2,1,0:T(8,128)(2,1)S(1)} %finish.1.refs_0_), channel_id=1, source_target_pairs={{0,8},{1,9},{2,10},{3,11},{4,12},{5,13},{6,14},{7,15},{8,0},{9,1},... | collective-permute-start | bytes 98312 | tf_op jit(solution)/shard_map/ppermute | solution.py:356
  29.2 0.4 %collective-permute-done.6.refs_1_ = bf16[4,32,128]{2,1,0:T(8,128)(2,1)S(1)} collective-permute-done((bf16[4,32,128]{2,1,0:T(8,128)(2,1)S(1)}, bf16[4,32,128]{2,1,0:T(8,128)(2,1)S(1)}, u32[]{:S(2)}, u32[]{:S(2)}) %collective-permute-start.6) | collective-permute-done | bytes 32800 | tf_op jit(solution)/shard_map/ppermute | solution.py:356
  29.7 1.7 %collective-permute-start.9 = (bf16[8,32,128]{2,1,0:T(8,128)(2,1)S(1)}, bf16[8,32,128]{2,1,0:T(8,128)(2,1)S(1)}, u32[]{:S(2)}, u32[]{:S(2)}) collective-permute-start(bf16[8,32,128]{2,1,0:T(8,128)(2,1)S(1)} %join.2.rest_0_), channel_id=1, source_target_pairs={{0,2},{1,3},{2,0},{3,1},{4,6},{5,7},{6,4},{7,5},{8,10},{9,11},{10,... | collective-permute-start | bytes 196616 | tf_op jit(solution)/shard_map/ppermute | solution.py:356
  31.4 0.2 collective-permute-done.8.refs_1_
  31.5 1.3 %collective-permute-done.7.refs_0_ = bf16[4,32,128]{2,1,0:T(8,128)(2,1)S(1)} collective-permute-done((bf16[4,32,128]{2,1,0:T(8,128)(2,1)S(1)}, bf16[4,32,128]{2,1,0:T(8,128)(2,1)S(1)}, u32[]{:S(2)}, u32[]{:S(2)}) %collective-permute-start.7) | collective-permute-done | bytes 32800 | tf_op jit(solution)/shard_map/ppermute | solution.py:356
  32.9 1.0 %collective-permute-start.10 = (bf16[8,32,128]{2,1,0:T(8,128)(2,1)S(1)}, bf16[8,32,128]{2,1,0:T(8,128)(2,1)S(1)}, u32[]{:S(2)}, u32[]{:S(2)}) collective-permute-start(bf16[8,32,128]{2,1,0:T(8,128)(2,1)S(1)} %join.3.rest_1_), channel_id=1, source_target_pairs={{0,2},{1,3},{2,0},{3,1},{4,6},{5,7},{6,4},{7,5},{8,10},{9,11},{10,... | collective-permute-start | bytes 196616 | tf_op jit(solution)/shard_map/ppermute | solution.py:356
  33.9 0.0 collective-permute-start.11
  33.9 0.5 %collective-permute-start.12 = (bf16[8,32,128]{2,1,0:T(8,128)(2,1)S(1)}, bf16[8,32,128]{2,1,0:T(8,128)(2,1)S(1)}, u32[]{:S(2)}, u32[]{:S(2)}) collective-permute-start(bf16[8,32,128]{2,1,0:T(8,128)(2,1)S(1)} %join.3.rest_1_), channel_id=1, source_target_pairs={{0,1},{1,0},{2,3},{3,2},{4,5},{5,4},{6,7},{7,6},{8,9},{9,8},{10,11... | collective-permute-start | bytes 196616 | tf_op jit(solution)/shard_map/ppermute | solution.py:356
  34.4 0.0 collective-permute-done.9.rest_2_
  34.4 0.0 collective-permute-start.13
  34.4 2.7 %collective-permute-done.10.rest_3_ = bf16[8,32,128]{2,1,0:T(8,128)(2,1)S(1)} collective-permute-done((bf16[8,32,128]{2,1,0:T(8,128)(2,1)S(1)}, bf16[8,32,128]{2,1,0:T(8,128)(2,1)S(1)}, u32[]{:S(2)}, u32[]{:S(2)}) %collective-permute-start.10) | collective-permute-done | bytes 65568 | tf_op jit(solution)/shard_map/ppermute | solution.py:356
  37.1 0.0 collective-permute-start.14
  37.1 0.0 collective-permute-done.11.rest_4_
  37.1 0.0 collective-permute-done.12.rest_5_
  37.1 0.0 collective-permute-done.13.rest_6_
  37.1 1.2 %collective-permute-done.14.rest_7_ = bf16[8,32,128]{2,1,0:T(8,128)(2,1)S(1)} collective-permute-done((bf16[8,32,128]{2,1,0:T(8,128)(2,1)S(1)}, bf16[8,32,128]{2,1,0:T(8,128)(2,1)S(1)}, u32[]{:S(2)}, u32[]{:S(2)}) %collective-permute-start.14) | collective-permute-done | bytes 65568 | tf_op jit(solution)/shard_map/ppermute | solution.py:356
  38.4 0.0 copy-done.1
  38.4 0.0 copy-done
  38.4 0.0 copy-done.2
  38.4 2.8 %subtract.1 = (f32[8,16,32,128]{3,2,1,0:T(8,128)}, bf16[4,32,128]{2,1,0:T(8,128)(2,1)}) custom-call(s32[1]{0:T(128)} %bitcast.me_ref, f32[1,8]{1,0:T(1,128)S(1)} %copy-done.2, s32[8,16]{1,0:T(8,128)S(1)} %bitcast.9, s32[8,16]{1,0:T(8,128)S(1)} %bitcast.11, f32[8,16,32,128]{3,2,1,0:T(8,128)S(1)} %get-tuple-element.15.smooth_ref, ...), custom_call_target="tpu_custom_call" | custom-call | tf_op jit(solution)/shard_map/subtract/pallas_call | solution.py:323
  (4 shorter events, 0.0 us)
Async XLA Ops:
  0.6 37.7 %copy-start.1 = (s32[1,8,16]{2,1,0:T(8,128)S(1)}, s32[1,8,16]{2,1,0:T(8,128)}, u32[]{:S(2)}) copy-start(s32[1,8,16]{2,1,0:T(8,128)} %param.16) | copy-start | bytes 1540
  0.6 37.7 %copy-start = (s32[1,8,16,1]{2,3,1,0:T(1,128)S(1)}, s32[1,8,16,1]{2,3,1,0:T(1,128)}, u32[]{:S(2)}) copy-start(s32[1,8,16,1]{2,3,1,0:T(1,128)} %param.15) | copy-start | bytes 1540
  0.7 37.7 %copy-start.2 = (f32[1,8]{1,0:T(1,128)S(1)}, f32[1,8]{1,0:T(1,128)}, u32[]{:S(2)}) copy-start(f32[1,8]{1,0:T(1,128)} %scale_ref.1) | copy-start | bytes 100
  8.0 1.7 %collective-permute-start = (bf16[8,136,128]{2,1,0:T(8,128)(2,1)S(1)}, bf16[8,136,128]{2,1,0:T(8,128)(2,1)S(1)}, u32[]{:S(2)}, u32[]{:S(2)}) collective-permute-start(bf16[8,136,128]{2,1,0:T(8,128)(2,1)S(1)} %get-tuple-element.17), channel_id=1, source_target_pairs={{0,1},{1,0},{2,3},{3,2},{4,5},{5,4},{6,7},{7,6},{8,9},{9,8},{10,11... | collective-permute-start | bytes 835592 | tf_op jit(solution)/shard_map/ppermute | solution.py:356
  9.8 5.5 %collective-permute-start.1 = (bf16[2,136,128]{2,1,0:T(8,128)(2,1)S(1)}, bf16[2,136,128]{2,1,0:T(8,128)(2,1)S(1)}, u32[]{:S(2)}, u32[]{:S(2)}) collective-permute-start(bf16[2,136,128]{2,1,0:T(8,128)(2,1)S(1)} %get-tuple-element.19), channel_id=1, source_target_pairs={{0,2},{1,3},{2,0},{3,1},{4,6},{5,7},{6,4},{7,5},{8,10},{9,11},{10,... | collective-permute-start | bytes 208904 | tf_op jit(solution)/shard_map/ppermute | solution.py:356
  12.8 4.8 %collective-permute-start.3 = (bf16[2,136,128]{2,1,0:T(8,128)(2,1)S(1)}, bf16[2,136,128]{2,1,0:T(8,128)(2,1)S(1)}, u32[]{:S(2)}, u32[]{:S(2)}) collective-permute-start(bf16[2,136,128]{2,1,0:T(8,128)(2,1)S(1)} %get-tuple-element.23), channel_id=1, source_target_pairs={{0,2},{1,3},{2,0},{3,1},{4,6},{5,7},{6,4},{7,5},{8,10},{9,11},{10,... | collective-permute-start | bytes 208904 | tf_op jit(solution)/shard_map/ppermute | solution.py:356
  15.3 5.5 %collective-permute-start.2 = (bf16[1,136,128]{2,1,0:T(8,128)(2,1)S(1)}, bf16[1,136,128]{2,1,0:T(8,128)(2,1)S(1)}, u32[]{:S(2)}, u32[]{:S(2)}) collective-permute-start(bf16[1,136,128]{2,1,0:T(8,128)(2,1)S(1)} %get-tuple-element.21), channel_id=1, source_target_pairs={{0,4},{1,5},{2,6},{3,7},{4,0},{5,1},{6,2},{7,3},{8,12},{9,13},{10,... | collective-permute-start | bytes 104456 | tf_op jit(solution)/shard_map/ppermute | solution.py:356
  17.6 5.8 %collective-permute-start.4 = (bf16[1,136,128]{2,1,0:T(8,128)(2,1)S(1)}, bf16[1,136,128]{2,1,0:T(8,128)(2,1)S(1)}, u32[]{:S(2)}, u32[]{:S(2)}) collective-permute-start(bf16[1,136,128]{2,1,0:T(8,128)(2,1)S(1)} %get-tuple-element.24), channel_id=1, source_target_pairs={{0,12},{1,13},{2,14},{3,15},{4,8},{5,9},{6,10},{7,11},{8,4},{9,5},... | collective-permute-start | bytes 104456 | tf_op jit(solution)/shard_map/ppermute | solution.py:356
  20.8 4.8 %collective-permute-start.5 = (bf16[1,136,128]{2,1,0:T(8,128)(2,1)S(1)}, bf16[1,136,128]{2,1,0:T(8,128)(2,1)S(1)}, u32[]{:S(2)}, u32[]{:S(2)}) collective-permute-start(bf16[1,136,128]{2,1,0:T(8,128)(2,1)S(1)} %get-tuple-element.25), channel_id=1, source_target_pairs={{0,8},{1,9},{2,10},{3,11},{4,12},{5,13},{6,14},{7,15},{8,0},{9,1},... | collective-permute-start | bytes 104456 | tf_op jit(solution)/shard_map/ppermute | solution.py:356
  25.7 3.9 %collective-permute-start.6 = (bf16[4,32,128]{2,1,0:T(8,128)(2,1)S(1)}, bf16[4,32,128]{2,1,0:T(8,128)(2,1)S(1)}, u32[]{:S(2)}, u32[]{:S(2)}) collective-permute-start(bf16[4,32,128]{2,1,0:T(8,128)(2,1)S(1)} %finish.1.refs_0_), channel_id=1, source_target_pairs={{0,4},{1,5},{2,6},{3,7},{4,0},{5,1},{6,2},{7,3},{8,12},{9,13},{10,... | collective-permute-start | bytes 98312 | tf_op jit(solution)/shard_map/ppermute | solution.py:356
  25.8 5.8 %collective-permute-start.8 = (bf16[4,32,128]{2,1,0:T(8,128)(2,1)S(1)}, bf16[4,32,128]{2,1,0:T(8,128)(2,1)S(1)}, u32[]{:S(2)}, u32[]{:S(2)}) collective-permute-start(bf16[4,32,128]{2,1,0:T(8,128)(2,1)S(1)} %finish.1.refs_0_), channel_id=1, source_target_pairs={{0,12},{1,13},{2,14},{3,15},{4,8},{5,9},{6,10},{7,11},{8,4},{9,5},... | collective-permute-start | bytes 98312 | tf_op jit(solution)/shard_map/ppermute | solution.py:356
  27.7 5.2 %collective-permute-start.7 = (bf16[4,32,128]{2,1,0:T(8,128)(2,1)S(1)}, bf16[4,32,128]{2,1,0:T(8,128)(2,1)S(1)}, u32[]{:S(2)}, u32[]{:S(2)}) collective-permute-start(bf16[4,32,128]{2,1,0:T(8,128)(2,1)S(1)} %finish.1.refs_0_), channel_id=1, source_target_pairs={{0,8},{1,9},{2,10},{3,11},{4,12},{5,13},{6,14},{7,15},{8,0},{9,1},... | collective-permute-start | bytes 98312 | tf_op jit(solution)/shard_map/ppermute | solution.py:356
  29.7 4.7 %collective-permute-start.9 = (bf16[8,32,128]{2,1,0:T(8,128)(2,1)S(1)}, bf16[8,32,128]{2,1,0:T(8,128)(2,1)S(1)}, u32[]{:S(2)}, u32[]{:S(2)}) collective-permute-start(bf16[8,32,128]{2,1,0:T(8,128)(2,1)S(1)} %join.2.rest_0_), channel_id=1, source_target_pairs={{0,2},{1,3},{2,0},{3,1},{4,6},{5,7},{6,4},{7,5},{8,10},{9,11},{10,... | collective-permute-start | bytes 196616 | tf_op jit(solution)/shard_map/ppermute | solution.py:356
  32.9 4.3 %collective-permute-start.10 = (bf16[8,32,128]{2,1,0:T(8,128)(2,1)S(1)}, bf16[8,32,128]{2,1,0:T(8,128)(2,1)S(1)}, u32[]{:S(2)}, u32[]{:S(2)}) collective-permute-start(bf16[8,32,128]{2,1,0:T(8,128)(2,1)S(1)} %join.3.rest_1_), channel_id=1, source_target_pairs={{0,2},{1,3},{2,0},{3,1},{4,6},{5,7},{6,4},{7,5},{8,10},{9,11},{10,... | collective-permute-start | bytes 196616 | tf_op jit(solution)/shard_map/ppermute | solution.py:356
  33.9 3.3 %collective-permute-start.11 = (bf16[8,32,128]{2,1,0:T(8,128)(2,1)S(1)}, bf16[8,32,128]{2,1,0:T(8,128)(2,1)S(1)}, u32[]{:S(2)}, u32[]{:S(2)}) collective-permute-start(bf16[8,32,128]{2,1,0:T(8,128)(2,1)S(1)} %join.2.rest_0_), channel_id=1, source_target_pairs={{0,1},{1,0},{2,3},{3,2},{4,5},{5,4},{6,7},{7,6},{8,9},{9,8},{10,11... | collective-permute-start | bytes 196616 | tf_op jit(solution)/shard_map/ppermute | solution.py:356
  33.9 3.3 %collective-permute-start.12 = (bf16[8,32,128]{2,1,0:T(8,128)(2,1)S(1)}, bf16[8,32,128]{2,1,0:T(8,128)(2,1)S(1)}, u32[]{:S(2)}, u32[]{:S(2)}) collective-permute-start(bf16[8,32,128]{2,1,0:T(8,128)(2,1)S(1)} %join.3.rest_1_), channel_id=1, source_target_pairs={{0,1},{1,0},{2,3},{3,2},{4,5},{5,4},{6,7},{7,6},{8,9},{9,8},{10,11... | collective-permute-start | bytes 196616 | tf_op jit(solution)/shard_map/ppermute | solution.py:356
  34.4 2.7 %collective-permute-start.13 = (bf16[8,32,128]{2,1,0:T(8,128)(2,1)S(1)}, bf16[8,32,128]{2,1,0:T(8,128)(2,1)S(1)}, u32[]{:S(2)}, u32[]{:S(2)}) collective-permute-start(bf16[8,32,128]{2,1,0:T(8,128)(2,1)S(1)} %collective-permute-done.9.rest_2_), channel_id=1, source_target_pairs={{0,1},{1,0},{2,3},{3,2},{4,5},{5,4},{6,7},{7,6},{8,9},{9,8},{10,11... | collective-permute-start | bytes 196616 | tf_op jit(solution)/shard_map/ppermute | solution.py:356
  37.1 1.3 %collective-permute-start.14 = (bf16[8,32,128]{2,1,0:T(8,128)(2,1)S(1)}, bf16[8,32,128]{2,1,0:T(8,128)(2,1)S(1)}, u32[]{:S(2)}, u32[]{:S(2)}) collective-permute-start(bf16[8,32,128]{2,1,0:T(8,128)(2,1)S(1)} %collective-permute-done.10.rest_3_), channel_id=1, source_target_pairs={{0,1},{1,0},{2,3},{3,2},{4,5},{5,4},{6,7},{7,6},{8,9},{9,8},{10,11... | collective-permute-start | bytes 196616 | tf_op jit(solution)/shard_map/ppermute | solution.py:356

commit v6 on v5

--- a/solution.py
+++ b/solution.py
@@ -48,10 +48,6 @@
     return kernel_list
 
 
-def reduce_stages(band_count):
-    return gather_stages(band_count)
-
-
 def gather_stages(band_count):
     rest = band_count // 2
     inner = 1
@@ -70,11 +66,27 @@
     return place
 
 
+def send_groups(third):
+    half = third // 2
+    if third > 4:
+        return [(half, third), (0, half)]
+    return [(digit, digit + 1) for digit in reversed(range(half, third))] + [(0, half)]
+
+
+def send_place(distance, stages):
+    first, second, third = stages
+    over = distance >> (first.bit_length() - 1)
+    along = over >> (second.bit_length() - 1)
+    return ((distance & (first - 1)) * third + along) * second + (over & (second - 1))
+
+
 def smooth_kernel(
     me_ref, weight_hbm, valid_hbm, owner_hbm, local_hbm, coef_hbm, spread_hbm, column_hbm, row_hbm, image_hbm,
-    smooth_ref, *rest, factors, band_count, row_count, layers,
+    smooth_ref, *rest, factors, row_count, layers,
 ):
-    message_refs, rest = rest[:factors[0]], rest[factors[0]:]
+    first, second, third = factors
+    starts = [(core * third + low) * second for core in range(first) for low, high in send_groups(third)]
+    message_refs, rest = rest[:len(starts)], rest[len(starts):]
     weight_ref, valid_ref, owner_ref, local_ref, coef_ref, spread_ref, column_ref, row_ref, held_ref = rest[:9]
     small_sems, image_sems, total_ref, factor_ref = rest[9:13]
     mixer_refs, column_pass_refs = rest[13:13 + 2 * TOGETHER], rest[13 + 2 * TOGETHER:]
@@ -140,16 +152,16 @@
         weight = jnp.full((8, tile_side), weight_ref[0, epoch] * valid_ref[0, epoch].astype(F32), F32)
         weight = weight.astype(BF16).astype(F32)
         weights = jnp.concatenate([weight] * (tile_rows // 8), axis=0)
-        for first in range(0, per_epoch, 2):
-            both = jnp.concatenate([column_pass_ref[first], column_pass_ref[first + 1]], axis=1)
+        for left in range(0, per_epoch, 2):
+            both = jnp.concatenate([column_pass_ref[left], column_pass_ref[left + 1]], axis=1)
             spatial = jnp.dot(mixer, both, preferred_element_type=F32)
             for s in range(2):
-                t = first + s
+                t = left + s
                 across = 2.0 * (column + (t * tile_side + 0.5)) / (per_epoch * tile_side) - 1.0
                 part = spatial[:, s * tile_side:(s + 1) * tile_side]
                 value = part[:tile_rows] + across * part[tile_rows:]
                 smooth_ref[epoch, t] = value
-                place = place_of(owner_ref[epoch, t] ^ me_ref[0], factors) * PD + local_ref[epoch, t]
+                place = send_place(owner_ref[epoch, t] ^ me_ref[0], factors) * PD + local_ref[epoch, t]
                 total_ref[place, :tile_rows] = (
                     total_ref[place, :tile_rows] + weights * value.astype(BF16).astype(F32))
                 total_ref[place, tile_rows:] = (
@@ -168,18 +180,17 @@
                 slot = epoch % (2 * TOGETHER)
                 row_pass(epoch, mixer_refs[slot], column_pass_refs[slot])
 
-    per_group = band_count // factors[0]
     line = lax.broadcasted_iota(jnp.int32, (8, tile_side), 0)
-    for g in range(factors[0]):
-        @pl.loop(0, per_group)
+    for start, message_ref in zip(starts, message_refs):
+        @pl.loop(0, message_ref.shape[0])
         def _(i):
-            block = (g * per_group + i) * PD
+            block = (start + i) * PD
             marks = jnp.zeros((8, tile_side), F32)
             for q in range(PD):
-                message_refs[g][i, q * tile_rows:(q + 1) * tile_rows, :] = (
+                message_ref[i, q * tile_rows:(q + 1) * tile_rows, :] = (
                     total_ref[block + q, :tile_rows].astype(BF16))
                 marks = jnp.where(line == q, total_ref[block + q, tile_rows:], marks)
-            message_refs[g][i, PD * tile_rows:, :] = marks.astype(BF16)
+            message_ref[i, PD * tile_rows:, :] = marks.astype(BF16)
 
 
 VMEM = pl.BlockSpec(memory_space=pltpu.VMEM)
@@ -209,10 +220,12 @@
     rows = jnp.asarray(np.stack(rows))
     spread = jnp.asarray(np.concatenate(spread, axis=1), BF16)
     block_rows = PD * tile_rows + EXTRA
-    per_group = band_count // factors[0]
-    messages = [jax.ShapeDtypeStruct((per_group, block_rows, tile_side), BF16)] * factors[0]
+    first, second, third = factors
+    messages = [
+        jax.ShapeDtypeStruct(((high - low) * second, block_rows, tile_side), BF16)
+        for _ in range(first) for low, high in send_groups(third)]
     return pl.pallas_call(
-        functools.partial(smooth_kernel, factors=factors, band_count=band_count, row_count=row_count,
+        functools.partial(smooth_kernel, factors=factors, row_count=row_count,
             layers=layers),
         in_specs=[SMEM] + [pl.BlockSpec(memory_space=pltpu.HBM)] * 9,
         out_specs=[VMEM] * (1 + len(messages)),
@@ -235,22 +248,23 @@
         weights, valid_epoch, owners, locals_, coeffs, spread, columns, rows, images)])
 
 
-def add_kernel(*refs, count, groups):
+def add_kernel(*refs, count, groups, minor):
     parts, outs = refs[:count], refs[count:]
     per_group = outs[0].shape[0]
     for g in range(groups):
         for i in range(per_group):
-            total = parts[0][g * per_group + i].astype(F32)
+            place = i * groups + g if minor else g * per_group + i
+            total = parts[0][place].astype(F32)
             for part in parts[1:]:
-                total = total + part[g * per_group + i].astype(F32)
+                total = total + part[place].astype(F32)
             outs[g][i] = total.astype(BF16)
 
 
-def add_and_split(parts, groups):
+def add_and_split(parts, groups, minor=False):
     blocks, block_rows, lanes = parts[0].shape
     out = jax.ShapeDtypeStruct((blocks // groups, block_rows, lanes), BF16)
     return pl.pallas_call(
-        functools.partial(add_kernel, count=len(parts), groups=groups),
+        functools.partial(add_kernel, count=len(parts), groups=groups, minor=minor),
         in_specs=[VMEM] * len(parts), out_specs=[VMEM] * groups,
         out_shape=[out] * groups, name="add_and_split",
         compiler_params=pltpu.CompilerParams(vmem_limit_bytes=VMEM_SMALL),
@@ -344,29 +358,31 @@
 def body(images, coeffs, weights, scales, valid_epoch, patch_owner, patch_local):
     band_count = lax.axis_size("band")
     _, epochs, per_epoch, tile_rows, _ = images.shape
-    down, up = reduce_stages(band_count), gather_stages(band_count)
+    up = gather_stages(band_count)
     me = lax.axis_index("band").astype(jnp.int32).reshape(1)
     owners = patch_owner.reshape(epochs, per_epoch)
     locals_ = patch_local.reshape(epochs, per_epoch)
 
     smoothed, *messages = smooth(
-        me, coeffs[0].transpose(2, 0, 1), weights, valid_epoch, owners, locals_, images[0], down, band_count)
+        me, coeffs[0].transpose(2, 0, 1), weights, valid_epoch, owners, locals_, images[0], up, band_count)
 
     def exchange(value, step):
         return lax.ppermute(value, "band", [(d, d ^ step) for d in range(band_count)])
 
-    first, second, third = down
+    first, second, third = up
     half = third // 2
-    parts = [messages[0]] + [exchange(messages[j], j) for j in range(1, first)]
-    split = add_and_split(parts, 2 * second)
-    near, far = split[0::2], split[1::2]
-    far = [far[0]] + [exchange(far[j], j * first) for j in range(1, second)]
-    near = [near[0]] + [exchange(near[j], j * first) for j in range(1, second)]
     stride = first * second
-    far = add_and_split(far, third - half)
-    arrived = [exchange(far[j - half], j * stride) for j in reversed(range(half, third))]
-    near = add_and_split(near, half)
-    arrived = [near[0]] + [exchange(near[j], j * stride) for j in range(1, half)] + arrived
+    groups = send_groups(third)
+    arrived = []
+    for g, (low, high) in enumerate(groups):
+        parts = [messages[g]] + [
+            exchange(messages[j * len(groups) + g], j) for j in range(1, first)]
+        split = add_and_split(parts, second, minor=True)
+        parts = [split[0]] + [exchange(split[j], j * first) for j in range(1, second)]
+        split = add_and_split(parts, high - low)
+        for digit in reversed(range(low, high)):
+            block = split[digit - low]
+            arrived.append(exchange(block, digit * stride) if digit else block)
 
     pieces = [finish(arrived, tile_rows)]
     own = pieces[0]

time: 41.4 us -> 42.2 us (1.019)
  starting transfers between devices: 15.8 us -> 17.8 us
  waiting for transfers between devices: 14.3 us -> 13.1 us
    ppermute x15 -> x18, starting transfers between devices: 15.8 us -> 17.8 us  [exchange(): lax.ppermute(value, 'band', [(d, d ^ step) for d in range(band_count)])]
    ppermute x15 -> x18, waiting for transfers between devices: 14.3 us -> 13.1 us  [exchange(): lax.ppermute(value, 'band', [(d, d ^ step) for d in range(band_count)])]
  transfers between devices with their start and end apart: 15 -> 18, of which waited for: 9 -> 9; matrix products, arithmetic and copies ran while one was open for 0% -> 0% of each run, Pallas kernels for 0% -> 0%
where the time goes in v6:
time: 42.2 us; the launch traced here: 42 us
  starting transfers between devices  17.8 us (42%)
  waiting for transfers between devices  13.1 us (31%)
  Pallas kernels  10.4 us (25%)
  between operations  0.74 us (2%)
    ppermute x18, starting transfers between devices, exchange(): lax.ppermute(value, 'band', [(d, d ^ step) for d in range(band_count)])  17.8 us
    ppermute x18, waiting for transfers between devices, exchange(): lax.ppermute(value, 'band', [(d, d ^ step) for d in range(band_count)])  13.1 us
    pallas_call x1, Pallas kernels, smooth(): pl.pallas_call(functools.partial(smooth_kernel, factors=factors, row_coun...  7.33 us
    pallas_call x1, Pallas kernels, subtract(): pl.pallas_call(functools.partial(difference_kernel, factors=factors, coun...  2.82 us
  transfers between devices with their start and end apart: 18, of which 9 were waited for; matrix products, arithmetic and copies ran while one was open for 0% of the time, Pallas kernels for 0%

profile of v6, /device:TPU:0, one launch (start us, length us, event | category | flops | bytes accessed | tf_op | source)
XLA Modules:
  0.0 42.0 jit_solution(5577385807844089639)
XLA Ops:
  0.6 0.0 copy-start.1
  0.6 0.0 copy-start
  0.7 0.0 copy-start.2
  0.7 7.3 %smooth.1 = (f32[8,16,32,128]{3,2,1,0:T(8,128)S(1)}, bf16[2,136,128]{2,1,0:T(8,128)(2,1)S(1)}, bf16[2,136,128]{2,1,0:T(8,128)(2,1)S(1)}, bf16[4,136,128]{2,1,0:T...) custom-call(s32[1]{0:T(128)} %bitcast.me_ref, ...), custom_call_target="tpu_custom_call" | custom-call | tf_op jit(solution)/shard_map/smooth/pallas_call | solution.py:227
  8.0 0.6 %collective-permute-start.6 = (bf16[4,136,128]{2,1,0:T(8,128)(2,1)S(1)}, bf16[4,136,128]{2,1,0:T(8,128)(2,1)S(1)}, u32[]{:S(2)}, u32[]{:S(2)}) collective-permute-start(bf16[4,136,128]{2,1,0:T(8,128)(2,1)S(1)} %get-tuple-element.29), channel_id=1, source_target_pairs={{0,1},{1,0},{2,3},{3,2},{4,5},{5,4},{6,7},{7,6},{8,9},{9,8},{10,11... | collective-permute-start | bytes 417800 | tf_op jit(solution)/shard_map/ppermute | solution.py:370
  8.6 0.1 collective-permute-start
  8.7 0.4 %collective-permute-start.3 = (bf16[2,136,128]{2,1,0:T(8,128)(2,1)S(1)}, bf16[2,136,128]{2,1,0:T(8,128)(2,1)S(1)}, u32[]{:S(2)}, u32[]{:S(2)}) collective-permute-start(bf16[2,136,128]{2,1,0:T(8,128)(2,1)S(1)} %get-tuple-element.25), channel_id=1, source_target_pairs={{0,1},{1,0},{2,3},{3,2},{4,5},{5,4},{6,7},{7,6},{8,9},{9,8},{10,11... | collective-permute-start | bytes 208904 | tf_op jit(solution)/shard_map/ppermute | solution.py:370
  9.1 0.5 %collective-permute-done.6.refs_1_ = bf16[4,136,128]{2,1,0:T(8,128)(2,1)S(1)} collective-permute-done((bf16[4,136,128]{2,1,0:T(8,128)(2,1)S(1)}, bf16[4,136,128]{2,1,0:T(8,128)(2,1)S(1)}, u32[]{:S(2)}, u32[]{:S(2)}) %collective-permute-start.6) | collective-permute-done | bytes 139296 | tf_op jit(solution)/shard_map/ppermute | solution.py:370
  9.6 2.9 %collective-permute-start.7 = (bf16[2,136,128]{2,1,0:T(8,128)(2,1)S(1)}, bf16[2,136,128]{2,1,0:T(8,128)(2,1)S(1)}, u32[]{:S(2)}, u32[]{:S(2)}) collective-permute-start(bf16[2,136,128]{2,1,0:T(8,128)(2,1)S(1)} %get-tuple-element.31), channel_id=1, source_target_pairs={{0,2},{1,3},{2,0},{3,1},{4,6},{5,7},{6,4},{7,5},{8,10},{9,11},{10,... | collective-permute-start | bytes 208904 | tf_op jit(solution)/shard_map/ppermute | solution.py:370
  12.5 0.0 collective-permute-done.refs_1_
  12.6 0.1 collective-permute-start.1
  12.7 0.0 collective-permute-done.3.refs_1_
  12.7 2.1 %collective-permute-start.4 = (bf16[1,136,128]{2,1,0:T(8,128)(2,1)S(1)}, bf16[1,136,128]{2,1,0:T(8,128)(2,1)S(1)}, u32[]{:S(2)}, u32[]{:S(2)}) collective-permute-start(bf16[1,136,128]{2,1,0:T(8,128)(2,1)S(1)} %get-tuple-element.27), channel_id=1, source_target_pairs={{0,2},{1,3},{2,0},{3,1},{4,6},{5,7},{6,4},{7,5},{8,10},{9,11},{10,... | collective-permute-start | bytes 104456 | tf_op jit(solution)/shard_map/ppermute | solution.py:370
  14.8 1.8 %collective-permute-done.1.refs_1_ = bf16[1,136,128]{2,1,0:T(8,128)(2,1)S(1)} collective-permute-done((bf16[1,136,128]{2,1,0:T(8,128)(2,1)S(1)}, bf16[1,136,128]{2,1,0:T(8,128)(2,1)S(1)}, u32[]{:S(2)}, u32[]{:S(2)}) %collective-permute-start.1) | collective-permute-done | bytes 34848 | tf_op jit(solution)/shard_map/ppermute | solution.py:370
  16.6 3.7 %collective-permute-start.2 = (bf16[1,136,128]{2,1,0:T(8,128)(2,1)S(1)}, bf16[1,136,128]{2,1,0:T(8,128)(2,1)S(1)}, u32[]{:S(2)}, u32[]{:S(2)}) collective-permute-start(bf16[1,136,128]{2,1,0:T(8,128)(2,1)S(1)} %add_and_split.7), channel_id=1, source_target_pairs={{0,12},{1,13},{2,14},{3,15},{4,8},{5,9},{6,10},{7,11},{8,4},{9,5},... | collective-permute-start | bytes 104456 | tf_op jit(solution)/shard_map/ppermute | solution.py:370
  20.2 0.0 collective-permute-done.4.refs_1_
  20.3 0.1 collective-permute-start.5
  20.3 0.0 collective-permute-done.7.refs_1_
  20.4 1.1 %collective-permute-start.8 = (bf16[1,136,128]{2,1,0:T(8,128)(2,1)S(1)}, bf16[1,136,128]{2,1,0:T(8,128)(2,1)S(1)}, u32[]{:S(2)}, u32[]{:S(2)}) collective-permute-start(bf16[1,136,128]{2,1,0:T(8,128)(2,1)S(1)} %get-tuple-element.32), channel_id=1, source_target_pairs={{0,4},{1,5},{2,6},{3,7},{4,0},{5,1},{6,2},{7,3},{8,12},{9,13},{10,... | collective-permute-start | bytes 104456 | tf_op jit(solution)/shard_map/ppermute | solution.py:370
  21.5 1.0 %collective-permute-done.2.refs_0_ = bf16[1,136,128]{2,1,0:T(8,128)(2,1)S(1)} collective-permute-done((bf16[1,136,128]{2,1,0:T(8,128)(2,1)S(1)}, bf16[1,136,128]{2,1,0:T(8,128)(2,1)S(1)}, u32[]{:S(2)}, u32[]{:S(2)}) %collective-permute-start.2) | collective-permute-done | bytes 34848 | tf_op jit(solution)/shard_map/ppermute | solution.py:370
  22.5 2.7 %collective-permute-done.5.refs_1_ = bf16[1,136,128]{2,1,0:T(8,128)(2,1)S(1)} collective-permute-done((bf16[1,136,128]{2,1,0:T(8,128)(2,1)S(1)}, bf16[1,136,128]{2,1,0:T(8,128)(2,1)S(1)}, u32[]{:S(2)}, u32[]{:S(2)}) %collective-permute-start.5) | collective-permute-done | bytes 34848 | tf_op jit(solution)/shard_map/ppermute | solution.py:370
  25.2 0.0 collective-permute-done.8.refs_2_
  25.2 0.1 finish.1.refs_0_
  25.3 0.3 collective-permute-start.9
  25.6 3.3 %collective-permute-start.11 = (bf16[4,32,128]{2,1,0:T(8,128)(2,1)S(1)}, bf16[4,32,128]{2,1,0:T(8,128)(2,1)S(1)}, u32[]{:S(2)}, u32[]{:S(2)}) collective-permute-start(bf16[4,32,128]{2,1,0:T(8,128)(2,1)S(1)} %finish.1.refs_0_), channel_id=1, source_target_pairs={{0,12},{1,13},{2,14},{3,15},{4,8},{5,9},{6,10},{7,11},{8,4},{9,5},... | collective-permute-start | bytes 98312 | tf_op jit(solution)/shard_map/ppermute | solution.py:370
  28.9 0.0 collective-permute-start.10
  28.9 0.3 collective-permute-done.9.refs_1_
  29.2 1.3 %collective-permute-start.12 = (bf16[8,32,128]{2,1,0:T(8,128)(2,1)S(1)}, bf16[8,32,128]{2,1,0:T(8,128)(2,1)S(1)}, u32[]{:S(2)}, u32[]{:S(2)}) collective-permute-start(bf16[8,32,128]{2,1,0:T(8,128)(2,1)S(1)} %join.2.rest_0_), channel_id=1, source_target_pairs={{0,2},{1,3},{2,0},{3,1},{4,6},{5,7},{6,4},{7,5},{8,10},{9,11},{10,... | collective-permute-start | bytes 196616 | tf_op jit(solution)/shard_map/ppermute | solution.py:370
  30.5 0.7 %collective-permute-done.11.refs_1_ = bf16[4,32,128]{2,1,0:T(8,128)(2,1)S(1)} collective-permute-done((bf16[4,32,128]{2,1,0:T(8,128)(2,1)S(1)}, bf16[4,32,128]{2,1,0:T(8,128)(2,1)S(1)}, u32[]{:S(2)}, u32[]{:S(2)}) %collective-permute-start.11) | collective-permute-done | bytes 32800 | tf_op jit(solution)/shard_map/ppermute | solution.py:370
  31.3 2.4 %collective-permute-done.10.refs_0_ = bf16[4,32,128]{2,1,0:T(8,128)(2,1)S(1)} collective-permute-done((bf16[4,32,128]{2,1,0:T(8,128)(2,1)S(1)}, bf16[4,32,128]{2,1,0:T(8,128)(2,1)S(1)}, u32[]{:S(2)}, u32[]{:S(2)}) %collective-permute-start.10) | collective-permute-done | bytes 32800 | tf_op jit(solution)/shard_map/ppermute | solution.py:370
  33.7 1.3 %collective-permute-start.13 = (bf16[8,32,128]{2,1,0:T(8,128)(2,1)S(1)}, bf16[8,32,128]{2,1,0:T(8,128)(2,1)S(1)}, u32[]{:S(2)}, u32[]{:S(2)}) collective-permute-start(bf16[8,32,128]{2,1,0:T(8,128)(2,1)S(1)} %join.3.rest_1_), channel_id=1, source_target_pairs={{0,2},{1,3},{2,0},{3,1},{4,6},{5,7},{6,4},{7,5},{8,10},{9,11},{10,... | collective-permute-start | bytes 196616 | tf_op jit(solution)/shard_map/ppermute | solution.py:370
  35.0 0.0 collective-permute-start.14
  35.0 0.5 %collective-permute-start.15 = (bf16[8,32,128]{2,1,0:T(8,128)(2,1)S(1)}, bf16[8,32,128]{2,1,0:T(8,128)(2,1)S(1)}, u32[]{:S(2)}, u32[]{:S(2)}) collective-permute-start(bf16[8,32,128]{2,1,0:T(8,128)(2,1)S(1)} %join.3.rest_1_), channel_id=1, source_target_pairs={{0,1},{1,0},{2,3},{3,2},{4,5},{5,4},{6,7},{7,6},{8,9},{9,8},{10,11... | collective-permute-start | bytes 196616 | tf_op jit(solution)/shard_map/ppermute | solution.py:370
  35.5 0.0 collective-permute-done.12.rest_2_
  35.5 0.0 collective-permute-start.16
  35.5 2.4 %collective-permute-done.13.rest_3_ = bf16[8,32,128]{2,1,0:T(8,128)(2,1)S(1)} collective-permute-done((bf16[8,32,128]{2,1,0:T(8,128)(2,1)S(1)}, bf16[8,32,128]{2,1,0:T(8,128)(2,1)S(1)}, u32[]{:S(2)}, u32[]{:S(2)}) %collective-permute-start.13) | collective-permute-done | bytes 65568 | tf_op jit(solution)/shard_map/ppermute | solution.py:370
  38.0 0.0 collective-permute-start.17
  38.0 0.0 collective-permute-done.14.rest_4_
  38.0 0.0 collective-permute-done.15.rest_5_
  38.0 0.0 collective-permute-done.16.rest_6_
  38.0 1.2 %collective-permute-done.17.rest_7_ = bf16[8,32,128]{2,1,0:T(8,128)(2,1)S(1)} collective-permute-done((bf16[8,32,128]{2,1,0:T(8,128)(2,1)S(1)}, bf16[8,32,128]{2,1,0:T(8,128)(2,1)S(1)}, u32[]{:S(2)}, u32[]{:S(2)}) %collective-permute-start.17) | collective-permute-done | bytes 65568 | tf_op jit(solution)/shard_map/ppermute | solution.py:370
  39.2 0.0 copy-done.1
  39.2 0.0 copy-done
  39.2 0.0 copy-done.2
  39.2 2.8 %subtract.1 = (f32[8,16,32,128]{3,2,1,0:T(8,128)}, bf16[4,32,128]{2,1,0:T(8,128)(2,1)}) custom-call(s32[1]{0:T(128)} %bitcast.me_ref, f32[1,8]{1,0:T(1,128)S(1)} %copy-done.2, s32[8,16]{1,0:T(8,128)S(1)} %bitcast.9, s32[8,16]{1,0:T(8,128)S(1)} %bitcast.11, f32[8,16,32,128]{3,2,1,0:T(8,128)S(1)} %get-tuple-element.19.smooth_ref, ...), custom_call_target="tpu_custom_call" | custom-call | tf_op jit(solution)/shard_map/subtract/pallas_call | solution.py:337
  (8 shorter events, 0.1 us)
Async XLA Ops:
  0.6 38.6 %copy-start.1 = (s32[1,8,16]{2,1,0:T(8,128)S(1)}, s32[1,8,16]{2,1,0:T(8,128)}, u32[]{:S(2)}) copy-start(s32[1,8,16]{2,1,0:T(8,128)} %param.16) | copy-start | bytes 1540
  0.6 38.6 %copy-start = (s32[1,8,16,1]{2,3,1,0:T(1,128)S(1)}, s32[1,8,16,1]{2,3,1,0:T(1,128)}, u32[]{:S(2)}) copy-start(s32[1,8,16,1]{2,3,1,0:T(1,128)} %param.15) | copy-start | bytes 1540
  0.7 38.6 %copy-start.2 = (f32[1,8]{1,0:T(1,128)S(1)}, f32[1,8]{1,0:T(1,128)}, u32[]{:S(2)}) copy-start(f32[1,8]{1,0:T(1,128)} %scale_ref.1) | copy-start | bytes 100
  8.0 1.6 %collective-permute-start.6 = (bf16[4,136,128]{2,1,0:T(8,128)(2,1)S(1)}, bf16[4,136,128]{2,1,0:T(8,128)(2,1)S(1)}, u32[]{:S(2)}, u32[]{:S(2)}) collective-permute-start(bf16[4,136,128]{2,1,0:T(8,128)(2,1)S(1)} %get-tuple-element.29), channel_id=1, source_target_pairs={{0,1},{1,0},{2,3},{3,2},{4,5},{5,4},{6,7},{7,6},{8,9},{9,8},{10,11... | collective-permute-start | bytes 417800 | tf_op jit(solution)/shard_map/ppermute | solution.py:370
  8.6 4.0 %collective-permute-start = (bf16[2,136,128]{2,1,0:T(8,128)(2,1)S(1)}, bf16[2,136,128]{2,1,0:T(8,128)(2,1)S(1)}, u32[]{:S(2)}, u32[]{:S(2)}) collective-permute-start(bf16[2,136,128]{2,1,0:T(8,128)(2,1)S(1)} %get-tuple-element.21), channel_id=1, source_target_pairs={{0,1},{1,0},{2,3},{3,2},{4,5},{5,4},{6,7},{7,6},{8,9},{9,8},{10,11... | collective-permute-start | bytes 208904 | tf_op jit(solution)/shard_map/ppermute | solution.py:370
  8.7 4.0 %collective-permute-start.3 = (bf16[2,136,128]{2,1,0:T(8,128)(2,1)S(1)}, bf16[2,136,128]{2,1,0:T(8,128)(2,1)S(1)}, u32[]{:S(2)}, u32[]{:S(2)}) collective-permute-start(bf16[2,136,128]{2,1,0:T(8,128)(2,1)S(1)} %get-tuple-element.25), channel_id=1, source_target_pairs={{0,1},{1,0},{2,3},{3,2},{4,5},{5,4},{6,7},{7,6},{8,9},{9,8},{10,11... | collective-permute-start | bytes 208904 | tf_op jit(solution)/shard_map/ppermute | solution.py:370
  9.6 10.7 %collective-permute-start.7 = (bf16[2,136,128]{2,1,0:T(8,128)(2,1)S(1)}, bf16[2,136,128]{2,1,0:T(8,128)(2,1)S(1)}, u32[]{:S(2)}, u32[]{:S(2)}) collective-permute-start(bf16[2,136,128]{2,1,0:T(8,128)(2,1)S(1)} %get-tuple-element.31), channel_id=1, source_target_pairs={{0,2},{1,3},{2,0},{3,1},{4,6},{5,7},{6,4},{7,5},{8,10},{9,11},{10,... | collective-permute-start | bytes 208904 | tf_op jit(solution)/shard_map/ppermute | solution.py:370
  12.6 4.0 %collective-permute-start.1 = (bf16[1,136,128]{2,1,0:T(8,128)(2,1)S(1)}, bf16[1,136,128]{2,1,0:T(8,128)(2,1)S(1)}, u32[]{:S(2)}, u32[]{:S(2)}) collective-permute-start(bf16[1,136,128]{2,1,0:T(8,128)(2,1)S(1)} %get-tuple-element.23), channel_id=1, source_target_pairs={{0,2},{1,3},{2,0},{3,1},{4,6},{5,7},{6,4},{7,5},{8,10},{9,11},{10,... | collective-permute-start | bytes 104456 | tf_op jit(solution)/shard_map/ppermute | solution.py:370
  12.7 7.6 %collective-permute-start.4 = (bf16[1,136,128]{2,1,0:T(8,128)(2,1)S(1)}, bf16[1,136,128]{2,1,0:T(8,128)(2,1)S(1)}, u32[]{:S(2)}, u32[]{:S(2)}) collective-permute-start(bf16[1,136,128]{2,1,0:T(8,128)(2,1)S(1)} %get-tuple-element.27), channel_id=1, source_target_pairs={{0,2},{1,3},{2,0},{3,1},{4,6},{5,7},{6,4},{7,5},{8,10},{9,11},{10,... | collective-permute-start | bytes 104456 | tf_op jit(solution)/shard_map/ppermute | solution.py:370
  16.6 5.9 %collective-permute-start.2 = (bf16[1,136,128]{2,1,0:T(8,128)(2,1)S(1)}, bf16[1,136,128]{2,1,0:T(8,128)(2,1)S(1)}, u32[]{:S(2)}, u32[]{:S(2)}) collective-permute-start(bf16[1,136,128]{2,1,0:T(8,128)(2,1)S(1)} %add_and_split.7), channel_id=1, source_target_pairs={{0,12},{1,13},{2,14},{3,15},{4,8},{5,9},{6,10},{7,11},{8,4},{9,5},... | collective-permute-start | bytes 104456 | tf_op jit(solution)/shard_map/ppermute | solution.py:370
  20.3 4.9 %collective-permute-start.5 = (bf16[1,136,128]{2,1,0:T(8,128)(2,1)S(1)}, bf16[1,136,128]{2,1,0:T(8,128)(2,1)S(1)}, u32[]{:S(2)}, u32[]{:S(2)}) collective-permute-start(bf16[1,136,128]{2,1,0:T(8,128)(2,1)S(1)} %add_and_split.9), channel_id=1, source_target_pairs={{0,8},{1,9},{2,10},{3,11},{4,12},{5,13},{6,14},{7,15},{8,0},{9,1},... | collective-permute-start | bytes 104456 | tf_op jit(solution)/shard_map/ppermute | solution.py:370
  20.4 4.8 %collective-permute-start.8 = (bf16[1,136,128]{2,1,0:T(8,128)(2,1)S(1)}, bf16[1,136,128]{2,1,0:T(8,128)(2,1)S(1)}, u32[]{:S(2)}, u32[]{:S(2)}) collective-permute-start(bf16[1,136,128]{2,1,0:T(8,128)(2,1)S(1)} %get-tuple-element.32), channel_id=1, source_target_pairs={{0,4},{1,5},{2,6},{3,7},{4,0},{5,1},{6,2},{7,3},{8,12},{9,13},{10,... | collective-permute-start | bytes 104456 | tf_op jit(solution)/shard_map/ppermute | solution.py:370
  25.3 3.9 %collective-permute-start.9 = (bf16[4,32,128]{2,1,0:T(8,128)(2,1)S(1)}, bf16[4,32,128]{2,1,0:T(8,128)(2,1)S(1)}, u32[]{:S(2)}, u32[]{:S(2)}) collective-permute-start(bf16[4,32,128]{2,1,0:T(8,128)(2,1)S(1)} %finish.1.refs_0_), channel_id=1, source_target_pairs={{0,4},{1,5},{2,6},{3,7},{4,0},{5,1},{6,2},{7,3},{8,12},{9,13},{10,... | collective-permute-start | bytes 98312 | tf_op jit(solution)/shard_map/ppermute | solution.py:370
  25.6 5.7 %collective-permute-start.11 = (bf16[4,32,128]{2,1,0:T(8,128)(2,1)S(1)}, bf16[4,32,128]{2,1,0:T(8,128)(2,1)S(1)}, u32[]{:S(2)}, u32[]{:S(2)}) collective-permute-start(bf16[4,32,128]{2,1,0:T(8,128)(2,1)S(1)} %finish.1.refs_0_), channel_id=1, source_target_pairs={{0,12},{1,13},{2,14},{3,15},{4,8},{5,9},{6,10},{7,11},{8,4},{9,5},... | collective-permute-start | bytes 98312 | tf_op jit(solution)/shard_map/ppermute | solution.py:370
  28.9 4.8 %collective-permute-start.10 = (bf16[4,32,128]{2,1,0:T(8,128)(2,1)S(1)}, bf16[4,32,128]{2,1,0:T(8,128)(2,1)S(1)}, u32[]{:S(2)}, u32[]{:S(2)}) collective-permute-start(bf16[4,32,128]{2,1,0:T(8,128)(2,1)S(1)} %finish.1.refs_0_), channel_id=1, source_target_pairs={{0,8},{1,9},{2,10},{3,11},{4,12},{5,13},{6,14},{7,15},{8,0},{9,1},... | collective-permute-start | bytes 98312 | tf_op jit(solution)/shard_map/ppermute | solution.py:370
  29.2 6.3 %collective-permute-start.12 = (bf16[8,32,128]{2,1,0:T(8,128)(2,1)S(1)}, bf16[8,32,128]{2,1,0:T(8,128)(2,1)S(1)}, u32[]{:S(2)}, u32[]{:S(2)}) collective-permute-start(bf16[8,32,128]{2,1,0:T(8,128)(2,1)S(1)} %join.2.rest_0_), channel_id=1, source_target_pairs={{0,2},{1,3},{2,0},{3,1},{4,6},{5,7},{6,4},{7,5},{8,10},{9,11},{10,... | collective-permute-start | bytes 196616 | tf_op jit(solution)/shard_map/ppermute | solution.py:370
  33.7 4.3 %collective-permute-start.13 = (bf16[8,32,128]{2,1,0:T(8,128)(2,1)S(1)}, bf16[8,32,128]{2,1,0:T(8,128)(2,1)S(1)}, u32[]{:S(2)}, u32[]{:S(2)}) collective-permute-start(bf16[8,32,128]{2,1,0:T(8,128)(2,1)S(1)} %join.3.rest_1_), channel_id=1, source_target_pairs={{0,2},{1,3},{2,0},{3,1},{4,6},{5,7},{6,4},{7,5},{8,10},{9,11},{10,... | collective-permute-start | bytes 196616 | tf_op jit(solution)/shard_map/ppermute | solution.py:370
  35.0 2.9 %collective-permute-start.14 = (bf16[8,32,128]{2,1,0:T(8,128)(2,1)S(1)}, bf16[8,32,128]{2,1,0:T(8,128)(2,1)S(1)}, u32[]{:S(2)}, u32[]{:S(2)}) collective-permute-start(bf16[8,32,128]{2,1,0:T(8,128)(2,1)S(1)} %join.2.rest_0_), channel_id=1, source_target_pairs={{0,1},{1,0},{2,3},{3,2},{4,5},{5,4},{6,7},{7,6},{8,9},{9,8},{10,11... | collective-permute-start | bytes 196616 | tf_op jit(solution)/shard_map/ppermute | solution.py:370
  35.0 2.9 %collective-permute-start.15 = (bf16[8,32,128]{2,1,0:T(8,128)(2,1)S(1)}, bf16[8,32,128]{2,1,0:T(8,128)(2,1)S(1)}, u32[]{:S(2)}, u32[]{:S(2)}) collective-permute-start(bf16[8,32,128]{2,1,0:T(8,128)(2,1)S(1)} %join.3.rest_1_), channel_id=1, source_target_pairs={{0,1},{1,0},{2,3},{3,2},{4,5},{5,4},{6,7},{7,6},{8,9},{9,8},{10,11... | collective-permute-start | bytes 196616 | tf_op jit(solution)/shard_map/ppermute | solution.py:370
  35.5 2.4 %collective-permute-start.16 = (bf16[8,32,128]{2,1,0:T(8,128)(2,1)S(1)}, bf16[8,32,128]{2,1,0:T(8,128)(2,1)S(1)}, u32[]{:S(2)}, u32[]{:S(2)}) collective-permute-start(bf16[8,32,128]{2,1,0:T(8,128)(2,1)S(1)} %collective-permute-done.12.rest_2_), channel_id=1, source_target_pairs={{0,1},{1,0},{2,3},{3,2},{4,5},{5,4},{6,7},{7,6},{8,9},{9,8},{10,11... | collective-permute-start | bytes 196616 | tf_op jit(solution)/shard_map/ppermute | solution.py:370
  38.0 1.3 %collective-permute-start.17 = (bf16[8,32,128]{2,1,0:T(8,128)(2,1)S(1)}, bf16[8,32,128]{2,1,0:T(8,128)(2,1)S(1)}, u32[]{:S(2)}, u32[]{:S(2)}) collective-permute-start(bf16[8,32,128]{2,1,0:T(8,128)(2,1)S(1)} %collective-permute-done.13.rest_3_), channel_id=1, source_target_pairs={{0,1},{1,0},{2,3},{3,2},{4,5},{5,4},{6,7},{7,6},{8,9},{9,8},{10,11... | collective-permute-start | bytes 196616 | tf_op jit(solution)/shard_map/ppermute | solution.py:370

commit v7 on v6

--- a/solution.py
+++ b/solution.py
@@ -118,8 +118,8 @@
         copy.wait()
 
     row = lax.broadcasted_iota(jnp.int32, (tile_rows, tile_side), 0).astype(F32)
-    column = lax.broadcasted_iota(jnp.int32, (tile_rows, tile_side), 1).astype(F32)
     lane = lax.broadcasted_iota(jnp.int32, (8, tile_side), 1)
+    column = lane.astype(F32)
     down = 2.0 * (row + 0.5) / tile_rows - 1.0
 
     def mixers(epoch, mixer_ref):
@@ -157,13 +157,14 @@
             spatial = jnp.dot(mixer, both, preferred_element_type=F32)
             for s in range(2):
                 t = left + s
-                across = 2.0 * (column + (t * tile_side + 0.5)) / (per_epoch * tile_side) - 1.0
+                across = (column + (t * tile_side + 0.5)) * (2.0 / (per_epoch * tile_side)) - 1.0
+                across = jnp.concatenate([across] * (tile_rows // 8), axis=0)
                 part = spatial[:, s * tile_side:(s + 1) * tile_side]
                 value = part[:tile_rows] + across * part[tile_rows:]
                 smooth_ref[epoch, t] = value
                 place = send_place(owner_ref[epoch, t] ^ me_ref[0], factors) * PD + local_ref[epoch, t]
                 total_ref[place, :tile_rows] = (
-                    total_ref[place, :tile_rows] + weights * value.astype(BF16).astype(F32))
+                    total_ref[place, :tile_rows] + weights * value)
                 total_ref[place, tile_rows:] = (
                     total_ref[place, tile_rows:] + jnp.where(lane == t % tile_side, weight, 0.0))
 
@@ -349,7 +350,7 @@
     )(me, scales, owners, locals_, smoothed, *pieces)
 
 
-TOGETHER = 2
+TOGETHER = 4
 VMEM_SMOOTH = 48 * 1024 * 1024
 VMEM_SMALL = 16 * 1024 * 1024
 VMEM_SUBTRACT = 40 * 1024 * 1024

time: 42.2 us -> 41.7 us (0.988)
  Pallas kernels: 10.4 us -> 9.9 us
    pallas_call x1, Pallas kernels: 7.33 us -> 6.85 us  [smooth(): pl.pallas_call(functools.partial(smooth_kernel, factors=factors, row_coun...]
where the time goes in v7:
time: 41.7 us; the launch traced here: 41.6 us
  starting transfers between devices  17.8 us (43%)
  waiting for transfers between devices  13.1 us (31%)
  Pallas kernels  9.9 us (24%)
  between operations  0.74 us (2%)
    ppermute x18, starting transfers between devices, exchange(): lax.ppermute(value, 'band', [(d, d ^ step) for d in range(band_count)])  17.8 us
    ppermute x18, waiting for transfers between devices, exchange(): lax.ppermute(value, 'band', [(d, d ^ step) for d in range(band_count)])  13.1 us
    pallas_call x1, Pallas kernels, smooth(): pl.pallas_call(functools.partial(smooth_kernel, factors=factors, row_coun...  6.85 us
    pallas_call x1, Pallas kernels, subtract(): pl.pallas_call(functools.partial(difference_kernel, factors=factors, coun...  2.82 us
  transfers between devices with their start and end apart: 18, of which 9 were waited for; matrix products, arithmetic and copies ran while one was open for 0% of the time, Pallas kernels for 0%

profile of v7, /device:TPU:0, one launch (start us, length us, event | category | flops | bytes accessed | tf_op | source)
XLA Modules:
  0.0 41.6 jit_solution(34034126376776436)
XLA Ops:
  0.6 0.0 copy-start.1
  0.6 0.0 copy-start
  0.7 0.0 copy-start.2
  0.7 6.8 %smooth.1 = (f32[8,16,32,128]{3,2,1,0:T(8,128)S(1)}, bf16[2,136,128]{2,1,0:T(8,128)(2,1)S(1)}, bf16[2,136,128]{2,1,0:T(8,128)(2,1)S(1)}, bf16[4,136,128]{2,1,0:T...) custom-call(s32[1]{0:T(128)} %bitcast.me_ref, ...), custom_call_target="tpu_custom_call" | custom-call | tf_op jit(solution)/shard_map/smooth/pallas_call | solution.py:228
  7.5 0.6 %collective-permute-start.6 = (bf16[4,136,128]{2,1,0:T(8,128)(2,1)S(1)}, bf16[4,136,128]{2,1,0:T(8,128)(2,1)S(1)}, u32[]{:S(2)}, u32[]{:S(2)}) collective-permute-start(bf16[4,136,128]{2,1,0:T(8,128)(2,1)S(1)} %get-tuple-element.29), channel_id=1, source_target_pairs={{0,1},{1,0},{2,3},{3,2},{4,5},{5,4},{6,7},{7,6},{8,9},{9,8},{10,11... | collective-permute-start | bytes 417800 | tf_op jit(solution)/shard_map/ppermute | solution.py:371
  8.1 0.1 collective-permute-start
  8.2 0.4 %collective-permute-start.3 = (bf16[2,136,128]{2,1,0:T(8,128)(2,1)S(1)}, bf16[2,136,128]{2,1,0:T(8,128)(2,1)S(1)}, u32[]{:S(2)}, u32[]{:S(2)}) collective-permute-start(bf16[2,136,128]{2,1,0:T(8,128)(2,1)S(1)} %get-tuple-element.25), channel_id=1, source_target_pairs={{0,1},{1,0},{2,3},{3,2},{4,5},{5,4},{6,7},{7,6},{8,9},{9,8},{10,11... | collective-permute-start | bytes 208904 | tf_op jit(solution)/shard_map/ppermute | solution.py:371
  8.6 0.5 %collective-permute-done.6.refs_1_ = bf16[4,136,128]{2,1,0:T(8,128)(2,1)S(1)} collective-permute-done((bf16[4,136,128]{2,1,0:T(8,128)(2,1)S(1)}, bf16[4,136,128]{2,1,0:T(8,128)(2,1)S(1)}, u32[]{:S(2)}, u32[]{:S(2)}) %collective-permute-start.6) | collective-permute-done | bytes 139296 | tf_op jit(solution)/shard_map/ppermute | solution.py:371
  9.1 2.9 %collective-permute-start.7 = (bf16[2,136,128]{2,1,0:T(8,128)(2,1)S(1)}, bf16[2,136,128]{2,1,0:T(8,128)(2,1)S(1)}, u32[]{:S(2)}, u32[]{:S(2)}) collective-permute-start(bf16[2,136,128]{2,1,0:T(8,128)(2,1)S(1)} %get-tuple-element.31), channel_id=1, source_target_pairs={{0,2},{1,3},{2,0},{3,1},{4,6},{5,7},{6,4},{7,5},{8,10},{9,11},{10,... | collective-permute-start | bytes 208904 | tf_op jit(solution)/shard_map/ppermute | solution.py:371
  12.1 0.0 collective-permute-done.refs_1_
  12.1 0.1 collective-permute-start.1
  12.2 0.0 collective-permute-done.3.refs_1_
  12.2 2.1 %collective-permute-start.4 = (bf16[1,136,128]{2,1,0:T(8,128)(2,1)S(1)}, bf16[1,136,128]{2,1,0:T(8,128)(2,1)S(1)}, u32[]{:S(2)}, u32[]{:S(2)}) collective-permute-start(bf16[1,136,128]{2,1,0:T(8,128)(2,1)S(1)} %get-tuple-element.27), channel_id=1, source_target_pairs={{0,2},{1,3},{2,0},{3,1},{4,6},{5,7},{6,4},{7,5},{8,10},{9,11},{10,... | collective-permute-start | bytes 104456 | tf_op jit(solution)/shard_map/ppermute | solution.py:371
  14.3 1.8 %collective-permute-done.1.refs_1_ = bf16[1,136,128]{2,1,0:T(8,128)(2,1)S(1)} collective-permute-done((bf16[1,136,128]{2,1,0:T(8,128)(2,1)S(1)}, bf16[1,136,128]{2,1,0:T(8,128)(2,1)S(1)}, u32[]{:S(2)}, u32[]{:S(2)}) %collective-permute-start.1) | collective-permute-done | bytes 34848 | tf_op jit(solution)/shard_map/ppermute | solution.py:371
  16.1 3.7 %collective-permute-start.2 = (bf16[1,136,128]{2,1,0:T(8,128)(2,1)S(1)}, bf16[1,136,128]{2,1,0:T(8,128)(2,1)S(1)}, u32[]{:S(2)}, u32[]{:S(2)}) collective-permute-start(bf16[1,136,128]{2,1,0:T(8,128)(2,1)S(1)} %add_and_split.7), channel_id=1, source_target_pairs={{0,12},{1,13},{2,14},{3,15},{4,8},{5,9},{6,10},{7,11},{8,4},{9,5},... | collective-permute-start | bytes 104456 | tf_op jit(solution)/shard_map/ppermute | solution.py:371
  19.8 0.0 collective-permute-done.4.refs_1_
  19.8 0.1 collective-permute-start.5
  19.9 0.0 collective-permute-done.7.refs_1_
  19.9 1.1 %collective-permute-start.8 = (bf16[1,136,128]{2,1,0:T(8,128)(2,1)S(1)}, bf16[1,136,128]{2,1,0:T(8,128)(2,1)S(1)}, u32[]{:S(2)}, u32[]{:S(2)}) collective-permute-start(bf16[1,136,128]{2,1,0:T(8,128)(2,1)S(1)} %get-tuple-element.32), channel_id=1, source_target_pairs={{0,4},{1,5},{2,6},{3,7},{4,0},{5,1},{6,2},{7,3},{8,12},{9,13},{10,... | collective-permute-start | bytes 104456 | tf_op jit(solution)/shard_map/ppermute | solution.py:371
  21.0 1.0 %collective-permute-done.2.refs_0_ = bf16[1,136,128]{2,1,0:T(8,128)(2,1)S(1)} collective-permute-done((bf16[1,136,128]{2,1,0:T(8,128)(2,1)S(1)}, bf16[1,136,128]{2,1,0:T(8,128)(2,1)S(1)}, u32[]{:S(2)}, u32[]{:S(2)}) %collective-permute-start.2) | collective-permute-done | bytes 34848 | tf_op jit(solution)/shard_map/ppermute | solution.py:371
  22.0 2.7 %collective-permute-done.5.refs_1_ = bf16[1,136,128]{2,1,0:T(8,128)(2,1)S(1)} collective-permute-done((bf16[1,136,128]{2,1,0:T(8,128)(2,1)S(1)}, bf16[1,136,128]{2,1,0:T(8,128)(2,1)S(1)}, u32[]{:S(2)}, u32[]{:S(2)}) %collective-permute-start.5) | collective-permute-done | bytes 34848 | tf_op jit(solution)/shard_map/ppermute | solution.py:371
  24.7 0.0 collective-permute-done.8.refs_2_
  24.7 0.1 finish.1.refs_0_
  24.8 0.3 collective-permute-start.9
  25.1 3.3 %collective-permute-start.11 = (bf16[4,32,128]{2,1,0:T(8,128)(2,1)S(1)}, bf16[4,32,128]{2,1,0:T(8,128)(2,1)S(1)}, u32[]{:S(2)}, u32[]{:S(2)}) collective-permute-start(bf16[4,32,128]{2,1,0:T(8,128)(2,1)S(1)} %finish.1.refs_0_), channel_id=1, source_target_pairs={{0,12},{1,13},{2,14},{3,15},{4,8},{5,9},{6,10},{7,11},{8,4},{9,5},... | collective-permute-start | bytes 98312 | tf_op jit(solution)/shard_map/ppermute | solution.py:371
  28.4 0.0 collective-permute-start.10
  28.4 0.3 collective-permute-done.9.refs_1_
  28.7 1.3 %collective-permute-start.12 = (bf16[8,32,128]{2,1,0:T(8,128)(2,1)S(1)}, bf16[8,32,128]{2,1,0:T(8,128)(2,1)S(1)}, u32[]{:S(2)}, u32[]{:S(2)}) collective-permute-start(bf16[8,32,128]{2,1,0:T(8,128)(2,1)S(1)} %join.2.rest_0_), channel_id=1, source_target_pairs={{0,2},{1,3},{2,0},{3,1},{4,6},{5,7},{6,4},{7,5},{8,10},{9,11},{10,... | collective-permute-start | bytes 196616 | tf_op jit(solution)/shard_map/ppermute | solution.py:371
  30.1 0.7 %collective-permute-done.11.refs_1_ = bf16[4,32,128]{2,1,0:T(8,128)(2,1)S(1)} collective-permute-done((bf16[4,32,128]{2,1,0:T(8,128)(2,1)S(1)}, bf16[4,32,128]{2,1,0:T(8,128)(2,1)S(1)}, u32[]{:S(2)}, u32[]{:S(2)}) %collective-permute-start.11) | collective-permute-done | bytes 32800 | tf_op jit(solution)/shard_map/ppermute | solution.py:371
  30.8 2.4 %collective-permute-done.10.refs_0_ = bf16[4,32,128]{2,1,0:T(8,128)(2,1)S(1)} collective-permute-done((bf16[4,32,128]{2,1,0:T(8,128)(2,1)S(1)}, bf16[4,32,128]{2,1,0:T(8,128)(2,1)S(1)}, u32[]{:S(2)}, u32[]{:S(2)}) %collective-permute-start.10) | collective-permute-done | bytes 32800 | tf_op jit(solution)/shard_map/ppermute | solution.py:371
  33.2 1.3 %collective-permute-start.13 = (bf16[8,32,128]{2,1,0:T(8,128)(2,1)S(1)}, bf16[8,32,128]{2,1,0:T(8,128)(2,1)S(1)}, u32[]{:S(2)}, u32[]{:S(2)}) collective-permute-start(bf16[8,32,128]{2,1,0:T(8,128)(2,1)S(1)} %join.3.rest_1_), channel_id=1, source_target_pairs={{0,2},{1,3},{2,0},{3,1},{4,6},{5,7},{6,4},{7,5},{8,10},{9,11},{10,... | collective-permute-start | bytes 196616 | tf_op jit(solution)/shard_map/ppermute | solution.py:371
  34.5 0.0 collective-permute-start.14
  34.5 0.5 %collective-permute-start.15 = (bf16[8,32,128]{2,1,0:T(8,128)(2,1)S(1)}, bf16[8,32,128]{2,1,0:T(8,128)(2,1)S(1)}, u32[]{:S(2)}, u32[]{:S(2)}) collective-permute-start(bf16[8,32,128]{2,1,0:T(8,128)(2,1)S(1)} %join.3.rest_1_), channel_id=1, source_target_pairs={{0,1},{1,0},{2,3},{3,2},{4,5},{5,4},{6,7},{7,6},{8,9},{9,8},{10,11... | collective-permute-start | bytes 196616 | tf_op jit(solution)/shard_map/ppermute | solution.py:371
  35.0 0.0 collective-permute-done.12.rest_2_
  35.1 0.0 collective-permute-start.16
  35.1 2.4 %collective-permute-done.13.rest_3_ = bf16[8,32,128]{2,1,0:T(8,128)(2,1)S(1)} collective-permute-done((bf16[8,32,128]{2,1,0:T(8,128)(2,1)S(1)}, bf16[8,32,128]{2,1,0:T(8,128)(2,1)S(1)}, u32[]{:S(2)}, u32[]{:S(2)}) %collective-permute-start.13) | collective-permute-done | bytes 65568 | tf_op jit(solution)/shard_map/ppermute | solution.py:371
  37.5 0.0 collective-permute-start.17
  37.5 0.0 collective-permute-done.14.rest_4_
  37.5 0.0 collective-permute-done.15.rest_5_
  37.5 0.0 collective-permute-done.16.rest_6_
  37.5 1.2 %collective-permute-done.17.rest_7_ = bf16[8,32,128]{2,1,0:T(8,128)(2,1)S(1)} collective-permute-done((bf16[8,32,128]{2,1,0:T(8,128)(2,1)S(1)}, bf16[8,32,128]{2,1,0:T(8,128)(2,1)S(1)}, u32[]{:S(2)}, u32[]{:S(2)}) %collective-permute-start.17) | collective-permute-done | bytes 65568 | tf_op jit(solution)/shard_map/ppermute | solution.py:371
  38.7 0.0 copy-done.1
  38.7 0.0 copy-done
  38.7 0.0 copy-done.2
  38.7 2.8 %subtract.1 = (f32[8,16,32,128]{3,2,1,0:T(8,128)}, bf16[4,32,128]{2,1,0:T(8,128)(2,1)}) custom-call(s32[1]{0:T(128)} %bitcast.me_ref, f32[1,8]{1,0:T(1,128)S(1)} %copy-done.2, s32[8,16]{1,0:T(8,128)S(1)} %bitcast.9, s32[8,16]{1,0:T(8,128)S(1)} %bitcast.11, f32[8,16,32,128]{3,2,1,0:T(8,128)S(1)} %get-tuple-element.19.smooth_ref, ...), custom_call_target="tpu_custom_call" | custom-call | tf_op jit(solution)/shard_map/subtract/pallas_call | solution.py:338
  (8 shorter events, 0.1 us)
Async XLA Ops:
  0.6 38.1 %copy-start.1 = (s32[1,8,16]{2,1,0:T(8,128)S(1)}, s32[1,8,16]{2,1,0:T(8,128)}, u32[]{:S(2)}) copy-start(s32[1,8,16]{2,1,0:T(8,128)} %param.16) | copy-start | bytes 1540
  0.6 38.1 %copy-start = (s32[1,8,16,1]{2,3,1,0:T(1,128)S(1)}, s32[1,8,16,1]{2,3,1,0:T(1,128)}, u32[]{:S(2)}) copy-start(s32[1,8,16,1]{2,3,1,0:T(1,128)} %param.15) | copy-start | bytes 1540
  0.7 38.1 %copy-start.2 = (f32[1,8]{1,0:T(1,128)S(1)}, f32[1,8]{1,0:T(1,128)}, u32[]{:S(2)}) copy-start(f32[1,8]{1,0:T(1,128)} %scale_ref.1) | copy-start | bytes 100
  7.5 1.6 %collective-permute-start.6 = (bf16[4,136,128]{2,1,0:T(8,128)(2,1)S(1)}, bf16[4,136,128]{2,1,0:T(8,128)(2,1)S(1)}, u32[]{:S(2)}, u32[]{:S(2)}) collective-permute-start(bf16[4,136,128]{2,1,0:T(8,128)(2,1)S(1)} %get-tuple-element.29), channel_id=1, source_target_pairs={{0,1},{1,0},{2,3},{3,2},{4,5},{5,4},{6,7},{7,6},{8,9},{9,8},{10,11... | collective-permute-start | bytes 417800 | tf_op jit(solution)/shard_map/ppermute | solution.py:371
  8.1 4.0 %collective-permute-start = (bf16[2,136,128]{2,1,0:T(8,128)(2,1)S(1)}, bf16[2,136,128]{2,1,0:T(8,128)(2,1)S(1)}, u32[]{:S(2)}, u32[]{:S(2)}) collective-permute-start(bf16[2,136,128]{2,1,0:T(8,128)(2,1)S(1)} %get-tuple-element.21), channel_id=1, source_target_pairs={{0,1},{1,0},{2,3},{3,2},{4,5},{5,4},{6,7},{7,6},{8,9},{9,8},{10,11... | collective-permute-start | bytes 208904 | tf_op jit(solution)/shard_map/ppermute | solution.py:371
  8.2 4.0 %collective-permute-start.3 = (bf16[2,136,128]{2,1,0:T(8,128)(2,1)S(1)}, bf16[2,136,128]{2,1,0:T(8,128)(2,1)S(1)}, u32[]{:S(2)}, u32[]{:S(2)}) collective-permute-start(bf16[2,136,128]{2,1,0:T(8,128)(2,1)S(1)} %get-tuple-element.25), channel_id=1, source_target_pairs={{0,1},{1,0},{2,3},{3,2},{4,5},{5,4},{6,7},{7,6},{8,9},{9,8},{10,11... | collective-permute-start | bytes 208904 | tf_op jit(solution)/shard_map/ppermute | solution.py:371
  9.1 10.7 %collective-permute-start.7 = (bf16[2,136,128]{2,1,0:T(8,128)(2,1)S(1)}, bf16[2,136,128]{2,1,0:T(8,128)(2,1)S(1)}, u32[]{:S(2)}, u32[]{:S(2)}) collective-permute-start(bf16[2,136,128]{2,1,0:T(8,128)(2,1)S(1)} %get-tuple-element.31), channel_id=1, source_target_pairs={{0,2},{1,3},{2,0},{3,1},{4,6},{5,7},{6,4},{7,5},{8,10},{9,11},{10,... | collective-permute-start | bytes 208904 | tf_op jit(solution)/shard_map/ppermute | solution.py:371
  12.1 4.0 %collective-permute-start.1 = (bf16[1,136,128]{2,1,0:T(8,128)(2,1)S(1)}, bf16[1,136,128]{2,1,0:T(8,128)(2,1)S(1)}, u32[]{:S(2)}, u32[]{:S(2)}) collective-permute-start(bf16[1,136,128]{2,1,0:T(8,128)(2,1)S(1)} %get-tuple-element.23), channel_id=1, source_target_pairs={{0,2},{1,3},{2,0},{3,1},{4,6},{5,7},{6,4},{7,5},{8,10},{9,11},{10,... | collective-permute-start | bytes 104456 | tf_op jit(solution)/shard_map/ppermute | solution.py:371
  12.2 7.6 %collective-permute-start.4 = (bf16[1,136,128]{2,1,0:T(8,128)(2,1)S(1)}, bf16[1,136,128]{2,1,0:T(8,128)(2,1)S(1)}, u32[]{:S(2)}, u32[]{:S(2)}) collective-permute-start(bf16[1,136,128]{2,1,0:T(8,128)(2,1)S(1)} %get-tuple-element.27), channel_id=1, source_target_pairs={{0,2},{1,3},{2,0},{3,1},{4,6},{5,7},{6,4},{7,5},{8,10},{9,11},{10,... | collective-permute-start | bytes 104456 | tf_op jit(solution)/shard_map/ppermute | solution.py:371
  16.1 5.9 %collective-permute-start.2 = (bf16[1,136,128]{2,1,0:T(8,128)(2,1)S(1)}, bf16[1,136,128]{2,1,0:T(8,128)(2,1)S(1)}, u32[]{:S(2)}, u32[]{:S(2)}) collective-permute-start(bf16[1,136,128]{2,1,0:T(8,128)(2,1)S(1)} %add_and_split.7), channel_id=1, source_target_pairs={{0,12},{1,13},{2,14},{3,15},{4,8},{5,9},{6,10},{7,11},{8,4},{9,5},... | collective-permute-start | bytes 104456 | tf_op jit(solution)/shard_map/ppermute | solution.py:371
  19.8 4.9 %collective-permute-start.5 = (bf16[1,136,128]{2,1,0:T(8,128)(2,1)S(1)}, bf16[1,136,128]{2,1,0:T(8,128)(2,1)S(1)}, u32[]{:S(2)}, u32[]{:S(2)}) collective-permute-start(bf16[1,136,128]{2,1,0:T(8,128)(2,1)S(1)} %add_and_split.9), channel_id=1, source_target_pairs={{0,8},{1,9},{2,10},{3,11},{4,12},{5,13},{6,14},{7,15},{8,0},{9,1},... | collective-permute-start | bytes 104456 | tf_op jit(solution)/shard_map/ppermute | solution.py:371
  19.9 4.8 %collective-permute-start.8 = (bf16[1,136,128]{2,1,0:T(8,128)(2,1)S(1)}, bf16[1,136,128]{2,1,0:T(8,128)(2,1)S(1)}, u32[]{:S(2)}, u32[]{:S(2)}) collective-permute-start(bf16[1,136,128]{2,1,0:T(8,128)(2,1)S(1)} %get-tuple-element.32), channel_id=1, source_target_pairs={{0,4},{1,5},{2,6},{3,7},{4,0},{5,1},{6,2},{7,3},{8,12},{9,13},{10,... | collective-permute-start | bytes 104456 | tf_op jit(solution)/shard_map/ppermute | solution.py:371
  24.8 3.9 %collective-permute-start.9 = (bf16[4,32,128]{2,1,0:T(8,128)(2,1)S(1)}, bf16[4,32,128]{2,1,0:T(8,128)(2,1)S(1)}, u32[]{:S(2)}, u32[]{:S(2)}) collective-permute-start(bf16[4,32,128]{2,1,0:T(8,128)(2,1)S(1)} %finish.1.refs_0_), channel_id=1, source_target_pairs={{0,4},{1,5},{2,6},{3,7},{4,0},{5,1},{6,2},{7,3},{8,12},{9,13},{10,... | collective-permute-start | bytes 98312 | tf_op jit(solution)/shard_map/ppermute | solution.py:371
  25.1 5.7 %collective-permute-start.11 = (bf16[4,32,128]{2,1,0:T(8,128)(2,1)S(1)}, bf16[4,32,128]{2,1,0:T(8,128)(2,1)S(1)}, u32[]{:S(2)}, u32[]{:S(2)}) collective-permute-start(bf16[4,32,128]{2,1,0:T(8,128)(2,1)S(1)} %finish.1.refs_0_), channel_id=1, source_target_pairs={{0,12},{1,13},{2,14},{3,15},{4,8},{5,9},{6,10},{7,11},{8,4},{9,5},... | collective-permute-start | bytes 98312 | tf_op jit(solution)/shard_map/ppermute | solution.py:371
  28.4 4.8 %collective-permute-start.10 = (bf16[4,32,128]{2,1,0:T(8,128)(2,1)S(1)}, bf16[4,32,128]{2,1,0:T(8,128)(2,1)S(1)}, u32[]{:S(2)}, u32[]{:S(2)}) collective-permute-start(bf16[4,32,128]{2,1,0:T(8,128)(2,1)S(1)} %finish.1.refs_0_), channel_id=1, source_target_pairs={{0,8},{1,9},{2,10},{3,11},{4,12},{5,13},{6,14},{7,15},{8,0},{9,1},... | collective-permute-start | bytes 98312 | tf_op jit(solution)/shard_map/ppermute | solution.py:371
  28.7 6.3 %collective-permute-start.12 = (bf16[8,32,128]{2,1,0:T(8,128)(2,1)S(1)}, bf16[8,32,128]{2,1,0:T(8,128)(2,1)S(1)}, u32[]{:S(2)}, u32[]{:S(2)}) collective-permute-start(bf16[8,32,128]{2,1,0:T(8,128)(2,1)S(1)} %join.2.rest_0_), channel_id=1, source_target_pairs={{0,2},{1,3},{2,0},{3,1},{4,6},{5,7},{6,4},{7,5},{8,10},{9,11},{10,... | collective-permute-start | bytes 196616 | tf_op jit(solution)/shard_map/ppermute | solution.py:371
  33.2 4.3 %collective-permute-start.13 = (bf16[8,32,128]{2,1,0:T(8,128)(2,1)S(1)}, bf16[8,32,128]{2,1,0:T(8,128)(2,1)S(1)}, u32[]{:S(2)}, u32[]{:S(2)}) collective-permute-start(bf16[8,32,128]{2,1,0:T(8,128)(2,1)S(1)} %join.3.rest_1_), channel_id=1, source_target_pairs={{0,2},{1,3},{2,0},{3,1},{4,6},{5,7},{6,4},{7,5},{8,10},{9,11},{10,... | collective-permute-start | bytes 196616 | tf_op jit(solution)/shard_map/ppermute | solution.py:371
  34.5 2.9 %collective-permute-start.14 = (bf16[8,32,128]{2,1,0:T(8,128)(2,1)S(1)}, bf16[8,32,128]{2,1,0:T(8,128)(2,1)S(1)}, u32[]{:S(2)}, u32[]{:S(2)}) collective-permute-start(bf16[8,32,128]{2,1,0:T(8,128)(2,1)S(1)} %join.2.rest_0_), channel_id=1, source_target_pairs={{0,1},{1,0},{2,3},{3,2},{4,5},{5,4},{6,7},{7,6},{8,9},{9,8},{10,11... | collective-permute-start | bytes 196616 | tf_op jit(solution)/shard_map/ppermute | solution.py:371
  34.5 2.9 %collective-permute-start.15 = (bf16[8,32,128]{2,1,0:T(8,128)(2,1)S(1)}, bf16[8,32,128]{2,1,0:T(8,128)(2,1)S(1)}, u32[]{:S(2)}, u32[]{:S(2)}) collective-permute-start(bf16[8,32,128]{2,1,0:T(8,128)(2,1)S(1)} %join.3.rest_1_), channel_id=1, source_target_pairs={{0,1},{1,0},{2,3},{3,2},{4,5},{5,4},{6,7},{7,6},{8,9},{9,8},{10,11... | collective-permute-start | bytes 196616 | tf_op jit(solution)/shard_map/ppermute | solution.py:371
  35.1 2.4 %collective-permute-start.16 = (bf16[8,32,128]{2,1,0:T(8,128)(2,1)S(1)}, bf16[8,32,128]{2,1,0:T(8,128)(2,1)S(1)}, u32[]{:S(2)}, u32[]{:S(2)}) collective-permute-start(bf16[8,32,128]{2,1,0:T(8,128)(2,1)S(1)} %collective-permute-done.12.rest_2_), channel_id=1, source_target_pairs={{0,1},{1,0},{2,3},{3,2},{4,5},{5,4},{6,7},{7,6},{8,9},{9,8},{10,11... | collective-permute-start | bytes 196616 | tf_op jit(solution)/shard_map/ppermute | solution.py:371
  37.5 1.3 %collective-permute-start.17 = (bf16[8,32,128]{2,1,0:T(8,128)(2,1)S(1)}, bf16[8,32,128]{2,1,0:T(8,128)(2,1)S(1)}, u32[]{:S(2)}, u32[]{:S(2)}) collective-permute-start(bf16[8,32,128]{2,1,0:T(8,128)(2,1)S(1)} %collective-permute-done.13.rest_3_), channel_id=1, source_target_pairs={{0,1},{1,0},{2,3},{3,2},{4,5},{5,4},{6,7},{7,6},{8,9},{9,8},{10,11... | collective-permute-start | bytes 196616 | tf_op jit(solution)/shard_map/ppermute | solution.py:371

commit v8 on v7

--- a/solution.py
+++ b/solution.py
@@ -316,20 +316,25 @@
         table_ref[start:start + piece.shape[0]] = piece[...]
         start += piece.shape[0]
 
-    def copy(e):
-        return pltpu.make_async_copy(ready_ref.at[e], out_ref.at[e], sems.at[e])
-
-    for e in range(epochs):
+    part = max(1, per_epoch // 2)
+    parts = [(e, first) for e in range(epochs) for first in range(0, per_epoch, part)]
+
+    def copy(k):
+        e, first = parts[k]
+        return pltpu.make_async_copy(
+            ready_ref.at[e, first:first + part], out_ref.at[e, first:first + part], sems.at[k])
+
+    for k, (e, first) in enumerate(parts):
         scale = scale_ref[0, e]
-        for t in range(per_epoch):
+        for t in range(first, min(first + part, per_epoch)):
             place = place_of(owner_ref[e, t] ^ me_ref[0], factors) * PD + local_ref[e, t]
             ready_ref[e, t] = smooth_ref[e, t] - scale * table_ref[place].astype(F32)
-        if e > 0:
-            copy(e - 1).start()
+        if k > 0:
+            copy(k - 1).start()
     template_ref[...] = table_ref[:PD]
-    copy(epochs - 1).start()
-    for e in range(epochs):
-        copy(e).wait()
+    copy(len(parts) - 1).start()
+    for k in range(len(parts)):
+        copy(k).wait()
 
 
 def subtract(me, scales, owners, locals_, pieces, smoothed, factors):
@@ -343,7 +348,7 @@
         scratch_shapes=[
             pltpu.VMEM((PD * int(np.prod(factors)), tile_rows, tile_side), BF16),
             pltpu.VMEM(smoothed.shape, F32),
-            pltpu.SemaphoreType.DMA((smoothed.shape[0],)),
+            pltpu.SemaphoreType.DMA((2 * smoothed.shape[0],)),
         ],
         compiler_params=pltpu.CompilerParams(vmem_limit_bytes=VMEM_SUBTRACT),
         name="subtract",

time: 41.7 us -> 41.7 us (level)
  no operation moved by 1% of the time
where the time goes in v8:
time: 41.7 us; the launch traced here: 41.6 us
  starting transfers between devices  17.8 us (43%)
  waiting for transfers between devices  13.1 us (31%)
  Pallas kernels  9.89 us (24%)
  between operations  0.74 us (2%)
    ppermute x18, starting transfers between devices, exchange(): lax.ppermute(value, 'band', [(d, d ^ step) for d in range(band_count)])  17.8 us
    ppermute x18, waiting for transfers between devices, exchange(): lax.ppermute(value, 'band', [(d, d ^ step) for d in range(band_count)])  13.1 us
    pallas_call x1, Pallas kernels, smooth(): pl.pallas_call(functools.partial(smooth_kernel, factors=factors, row_coun...  6.85 us
    pallas_call x1, Pallas kernels, subtract(): pl.pallas_call(functools.partial(difference_kernel, factors=factors, coun...  2.81 us
  transfers between devices with their start and end apart: 18, of which 9 were waited for; matrix products, arithmetic and copies ran while one was open for 0% of the time, Pallas kernels for 0%

profile of v8, /device:TPU:0, one launch (start us, length us, event | category | flops | bytes accessed | tf_op | source)
XLA Modules:
  0.0 41.6 jit_solution(18059252409647941483)
XLA Ops:
  0.6 0.0 copy-start.1
  0.6 0.0 copy-start
  0.7 0.0 copy-start.2
  0.7 6.8 %smooth.1 = (f32[8,16,32,128]{3,2,1,0:T(8,128)S(1)}, bf16[2,136,128]{2,1,0:T(8,128)(2,1)S(1)}, bf16[2,136,128]{2,1,0:T(8,128)(2,1)S(1)}, bf16[4,136,128]{2,1,0:T...) custom-call(s32[1]{0:T(128)} %bitcast.me_ref, ...), custom_call_target="tpu_custom_call" | custom-call | tf_op jit(solution)/shard_map/smooth/pallas_call | solution.py:228
  7.5 0.6 %collective-permute-start.6 = (bf16[4,136,128]{2,1,0:T(8,128)(2,1)S(1)}, bf16[4,136,128]{2,1,0:T(8,128)(2,1)S(1)}, u32[]{:S(2)}, u32[]{:S(2)}) collective-permute-start(bf16[4,136,128]{2,1,0:T(8,128)(2,1)S(1)} %get-tuple-element.29), channel_id=1, source_target_pairs={{0,1},{1,0},{2,3},{3,2},{4,5},{5,4},{6,7},{7,6},{8,9},{9,8},{10,11... | collective-permute-start | bytes 417800 | tf_op jit(solution)/shard_map/ppermute | solution.py:376
  8.1 0.1 collective-permute-start
  8.2 0.4 %collective-permute-start.3 = (bf16[2,136,128]{2,1,0:T(8,128)(2,1)S(1)}, bf16[2,136,128]{2,1,0:T(8,128)(2,1)S(1)}, u32[]{:S(2)}, u32[]{:S(2)}) collective-permute-start(bf16[2,136,128]{2,1,0:T(8,128)(2,1)S(1)} %get-tuple-element.25), channel_id=1, source_target_pairs={{0,1},{1,0},{2,3},{3,2},{4,5},{5,4},{6,7},{7,6},{8,9},{9,8},{10,11... | collective-permute-start | bytes 208904 | tf_op jit(solution)/shard_map/ppermute | solution.py:376
  8.6 0.5 %collective-permute-done.6.refs_1_ = bf16[4,136,128]{2,1,0:T(8,128)(2,1)S(1)} collective-permute-done((bf16[4,136,128]{2,1,0:T(8,128)(2,1)S(1)}, bf16[4,136,128]{2,1,0:T(8,128)(2,1)S(1)}, u32[]{:S(2)}, u32[]{:S(2)}) %collective-permute-start.6) | collective-permute-done | bytes 139296 | tf_op jit(solution)/shard_map/ppermute | solution.py:376
  9.1 2.9 %collective-permute-start.7 = (bf16[2,136,128]{2,1,0:T(8,128)(2,1)S(1)}, bf16[2,136,128]{2,1,0:T(8,128)(2,1)S(1)}, u32[]{:S(2)}, u32[]{:S(2)}) collective-permute-start(bf16[2,136,128]{2,1,0:T(8,128)(2,1)S(1)} %get-tuple-element.31), channel_id=1, source_target_pairs={{0,2},{1,3},{2,0},{3,1},{4,6},{5,7},{6,4},{7,5},{8,10},{9,11},{10,... | collective-permute-start | bytes 208904 | tf_op jit(solution)/shard_map/ppermute | solution.py:376
  12.1 0.0 collective-permute-done.refs_1_
  12.1 0.1 collective-permute-start.1
  12.2 0.0 collective-permute-done.3.refs_1_
  12.2 2.1 %collective-permute-start.4 = (bf16[1,136,128]{2,1,0:T(8,128)(2,1)S(1)}, bf16[1,136,128]{2,1,0:T(8,128)(2,1)S(1)}, u32[]{:S(2)}, u32[]{:S(2)}) collective-permute-start(bf16[1,136,128]{2,1,0:T(8,128)(2,1)S(1)} %get-tuple-element.27), channel_id=1, source_target_pairs={{0,2},{1,3},{2,0},{3,1},{4,6},{5,7},{6,4},{7,5},{8,10},{9,11},{10,... | collective-permute-start | bytes 104456 | tf_op jit(solution)/shard_map/ppermute | solution.py:376
  14.3 1.8 %collective-permute-done.1.refs_1_ = bf16[1,136,128]{2,1,0:T(8,128)(2,1)S(1)} collective-permute-done((bf16[1,136,128]{2,1,0:T(8,128)(2,1)S(1)}, bf16[1,136,128]{2,1,0:T(8,128)(2,1)S(1)}, u32[]{:S(2)}, u32[]{:S(2)}) %collective-permute-start.1) | collective-permute-done | bytes 34848 | tf_op jit(solution)/shard_map/ppermute | solution.py:376
  16.1 3.7 %collective-permute-start.2 = (bf16[1,136,128]{2,1,0:T(8,128)(2,1)S(1)}, bf16[1,136,128]{2,1,0:T(8,128)(2,1)S(1)}, u32[]{:S(2)}, u32[]{:S(2)}) collective-permute-start(bf16[1,136,128]{2,1,0:T(8,128)(2,1)S(1)} %add_and_split.7), channel_id=1, source_target_pairs={{0,12},{1,13},{2,14},{3,15},{4,8},{5,9},{6,10},{7,11},{8,4},{9,5},... | collective-permute-start | bytes 104456 | tf_op jit(solution)/shard_map/ppermute | solution.py:376
  19.8 0.0 collective-permute-done.4.refs_1_
  19.8 0.1 collective-permute-start.5
  19.9 0.0 collective-permute-done.7.refs_1_
  19.9 1.1 %collective-permute-start.8 = (bf16[1,136,128]{2,1,0:T(8,128)(2,1)S(1)}, bf16[1,136,128]{2,1,0:T(8,128)(2,1)S(1)}, u32[]{:S(2)}, u32[]{:S(2)}) collective-permute-start(bf16[1,136,128]{2,1,0:T(8,128)(2,1)S(1)} %get-tuple-element.32), channel_id=1, source_target_pairs={{0,4},{1,5},{2,6},{3,7},{4,0},{5,1},{6,2},{7,3},{8,12},{9,13},{10,... | collective-permute-start | bytes 104456 | tf_op jit(solution)/shard_map/ppermute | solution.py:376
  21.0 1.0 %collective-permute-done.2.refs_0_ = bf16[1,136,128]{2,1,0:T(8,128)(2,1)S(1)} collective-permute-done((bf16[1,136,128]{2,1,0:T(8,128)(2,1)S(1)}, bf16[1,136,128]{2,1,0:T(8,128)(2,1)S(1)}, u32[]{:S(2)}, u32[]{:S(2)}) %collective-permute-start.2) | collective-permute-done | bytes 34848 | tf_op jit(solution)/shard_map/ppermute | solution.py:376
  22.0 2.7 %collective-permute-done.5.refs_1_ = bf16[1,136,128]{2,1,0:T(8,128)(2,1)S(1)} collective-permute-done((bf16[1,136,128]{2,1,0:T(8,128)(2,1)S(1)}, bf16[1,136,128]{2,1,0:T(8,128)(2,1)S(1)}, u32[]{:S(2)}, u32[]{:S(2)}) %collective-permute-start.5) | collective-permute-done | bytes 34848 | tf_op jit(solution)/shard_map/ppermute | solution.py:376
  24.7 0.0 collective-permute-done.8.refs_2_
  24.7 0.1 finish.1.refs_0_
  24.8 0.3 collective-permute-start.9
  25.1 3.3 %collective-permute-start.11 = (bf16[4,32,128]{2,1,0:T(8,128)(2,1)S(1)}, bf16[4,32,128]{2,1,0:T(8,128)(2,1)S(1)}, u32[]{:S(2)}, u32[]{:S(2)}) collective-permute-start(bf16[4,32,128]{2,1,0:T(8,128)(2,1)S(1)} %finish.1.refs_0_), channel_id=1, source_target_pairs={{0,12},{1,13},{2,14},{3,15},{4,8},{5,9},{6,10},{7,11},{8,4},{9,5},... | collective-permute-start | bytes 98312 | tf_op jit(solution)/shard_map/ppermute | solution.py:376
  28.4 0.0 collective-permute-start.10
  28.4 0.3 collective-permute-done.9.refs_1_
  28.7 1.3 %collective-permute-start.12 = (bf16[8,32,128]{2,1,0:T(8,128)(2,1)S(1)}, bf16[8,32,128]{2,1,0:T(8,128)(2,1)S(1)}, u32[]{:S(2)}, u32[]{:S(2)}) collective-permute-start(bf16[8,32,128]{2,1,0:T(8,128)(2,1)S(1)} %join.2.rest_0_), channel_id=1, source_target_pairs={{0,2},{1,3},{2,0},{3,1},{4,6},{5,7},{6,4},{7,5},{8,10},{9,11},{10,... | collective-permute-start | bytes 196616 | tf_op jit(solution)/shard_map/ppermute | solution.py:376
  30.1 0.7 %collective-permute-done.11.refs_1_ = bf16[4,32,128]{2,1,0:T(8,128)(2,1)S(1)} collective-permute-done((bf16[4,32,128]{2,1,0:T(8,128)(2,1)S(1)}, bf16[4,32,128]{2,1,0:T(8,128)(2,1)S(1)}, u32[]{:S(2)}, u32[]{:S(2)}) %collective-permute-start.11) | collective-permute-done | bytes 32800 | tf_op jit(solution)/shard_map/ppermute | solution.py:376
  30.8 2.4 %collective-permute-done.10.refs_0_ = bf16[4,32,128]{2,1,0:T(8,128)(2,1)S(1)} collective-permute-done((bf16[4,32,128]{2,1,0:T(8,128)(2,1)S(1)}, bf16[4,32,128]{2,1,0:T(8,128)(2,1)S(1)}, u32[]{:S(2)}, u32[]{:S(2)}) %collective-permute-start.10) | collective-permute-done | bytes 32800 | tf_op jit(solution)/shard_map/ppermute | solution.py:376
  33.2 1.3 %collective-permute-start.13 = (bf16[8,32,128]{2,1,0:T(8,128)(2,1)S(1)}, bf16[8,32,128]{2,1,0:T(8,128)(2,1)S(1)}, u32[]{:S(2)}, u32[]{:S(2)}) collective-permute-start(bf16[8,32,128]{2,1,0:T(8,128)(2,1)S(1)} %join.3.rest_1_), channel_id=1, source_target_pairs={{0,2},{1,3},{2,0},{3,1},{4,6},{5,7},{6,4},{7,5},{8,10},{9,11},{10,... | collective-permute-start | bytes 196616 | tf_op jit(solution)/shard_map/ppermute | solution.py:376
  34.5 0.0 collective-permute-start.14
  34.5 0.5 %collective-permute-start.15 = (bf16[8,32,128]{2,1,0:T(8,128)(2,1)S(1)}, bf16[8,32,128]{2,1,0:T(8,128)(2,1)S(1)}, u32[]{:S(2)}, u32[]{:S(2)}) collective-permute-start(bf16[8,32,128]{2,1,0:T(8,128)(2,1)S(1)} %join.3.rest_1_), channel_id=1, source_target_pairs={{0,1},{1,0},{2,3},{3,2},{4,5},{5,4},{6,7},{7,6},{8,9},{9,8},{10,11... | collective-permute-start | bytes 196616 | tf_op jit(solution)/shard_map/ppermute | solution.py:376
  35.0 0.0 collective-permute-done.12.rest_2_
  35.1 0.0 collective-permute-start.16
  35.1 2.4 %collective-permute-done.13.rest_3_ = bf16[8,32,128]{2,1,0:T(8,128)(2,1)S(1)} collective-permute-done((bf16[8,32,128]{2,1,0:T(8,128)(2,1)S(1)}, bf16[8,32,128]{2,1,0:T(8,128)(2,1)S(1)}, u32[]{:S(2)}, u32[]{:S(2)}) %collective-permute-start.13) | collective-permute-done | bytes 65568 | tf_op jit(solution)/shard_map/ppermute | solution.py:376
  37.5 0.0 collective-permute-start.17
  37.5 0.0 collective-permute-done.14.rest_4_
  37.5 0.0 collective-permute-done.15.rest_5_
  37.5 0.0 collective-permute-done.16.rest_6_
  37.5 1.2 %collective-permute-done.17.rest_7_ = bf16[8,32,128]{2,1,0:T(8,128)(2,1)S(1)} collective-permute-done((bf16[8,32,128]{2,1,0:T(8,128)(2,1)S(1)}, bf16[8,32,128]{2,1,0:T(8,128)(2,1)S(1)}, u32[]{:S(2)}, u32[]{:S(2)}) %collective-permute-start.17) | collective-permute-done | bytes 65568 | tf_op jit(solution)/shard_map/ppermute | solution.py:376
  38.7 0.0 copy-done.1
  38.7 0.0 copy-done
  38.7 0.0 copy-done.2
  38.7 2.8 %subtract.1 = (f32[8,16,32,128]{3,2,1,0:T(8,128)}, bf16[4,32,128]{2,1,0:T(8,128)(2,1)}) custom-call(s32[1]{0:T(128)} %bitcast.me_ref, f32[1,8]{1,0:T(1,128)S(1)} %copy-done.2, s32[8,16]{1,0:T(8,128)S(1)} %bitcast.9, s32[8,16]{1,0:T(8,128)S(1)} %bitcast.11, f32[8,16,32,128]{3,2,1,0:T(8,128)S(1)} %get-tuple-element.19.smooth_ref, ...), custom_call_target="tpu_custom_call" | custom-call | tf_op jit(solution)/shard_map/subtract/pallas_call | solution.py:343
  (8 shorter events, 0.1 us)
Async XLA Ops:
  0.6 38.1 %copy-start.1 = (s32[1,8,16]{2,1,0:T(8,128)S(1)}, s32[1,8,16]{2,1,0:T(8,128)}, u32[]{:S(2)}) copy-start(s32[1,8,16]{2,1,0:T(8,128)} %param.16) | copy-start | bytes 1540
  0.6 38.1 %copy-start = (s32[1,8,16,1]{2,3,1,0:T(1,128)S(1)}, s32[1,8,16,1]{2,3,1,0:T(1,128)}, u32[]{:S(2)}) copy-start(s32[1,8,16,1]{2,3,1,0:T(1,128)} %param.15) | copy-start | bytes 1540
  0.7 38.1 %copy-start.2 = (f32[1,8]{1,0:T(1,128)S(1)}, f32[1,8]{1,0:T(1,128)}, u32[]{:S(2)}) copy-start(f32[1,8]{1,0:T(1,128)} %scale_ref.1) | copy-start | bytes 100
  7.5 1.6 %collective-permute-start.6 = (bf16[4,136,128]{2,1,0:T(8,128)(2,1)S(1)}, bf16[4,136,128]{2,1,0:T(8,128)(2,1)S(1)}, u32[]{:S(2)}, u32[]{:S(2)}) collective-permute-start(bf16[4,136,128]{2,1,0:T(8,128)(2,1)S(1)} %get-tuple-element.29), channel_id=1, source_target_pairs={{0,1},{1,0},{2,3},{3,2},{4,5},{5,4},{6,7},{7,6},{8,9},{9,8},{10,11... | collective-permute-start | bytes 417800 | tf_op jit(solution)/shard_map/ppermute | solution.py:376
  8.1 4.0 %collective-permute-start = (bf16[2,136,128]{2,1,0:T(8,128)(2,1)S(1)}, bf16[2,136,128]{2,1,0:T(8,128)(2,1)S(1)}, u32[]{:S(2)}, u32[]{:S(2)}) collective-permute-start(bf16[2,136,128]{2,1,0:T(8,128)(2,1)S(1)} %get-tuple-element.21), channel_id=1, source_target_pairs={{0,1},{1,0},{2,3},{3,2},{4,5},{5,4},{6,7},{7,6},{8,9},{9,8},{10,11... | collective-permute-start | bytes 208904 | tf_op jit(solution)/shard_map/ppermute | solution.py:376
  8.2 4.0 %collective-permute-start.3 = (bf16[2,136,128]{2,1,0:T(8,128)(2,1)S(1)}, bf16[2,136,128]{2,1,0:T(8,128)(2,1)S(1)}, u32[]{:S(2)}, u32[]{:S(2)}) collective-permute-start(bf16[2,136,128]{2,1,0:T(8,128)(2,1)S(1)} %get-tuple-element.25), channel_id=1, source_target_pairs={{0,1},{1,0},{2,3},{3,2},{4,5},{5,4},{6,7},{7,6},{8,9},{9,8},{10,11... | collective-permute-start | bytes 208904 | tf_op jit(solution)/shard_map/ppermute | solution.py:376
  9.1 10.7 %collective-permute-start.7 = (bf16[2,136,128]{2,1,0:T(8,128)(2,1)S(1)}, bf16[2,136,128]{2,1,0:T(8,128)(2,1)S(1)}, u32[]{:S(2)}, u32[]{:S(2)}) collective-permute-start(bf16[2,136,128]{2,1,0:T(8,128)(2,1)S(1)} %get-tuple-element.31), channel_id=1, source_target_pairs={{0,2},{1,3},{2,0},{3,1},{4,6},{5,7},{6,4},{7,5},{8,10},{9,11},{10,... | collective-permute-start | bytes 208904 | tf_op jit(solution)/shard_map/ppermute | solution.py:376
  12.1 4.0 %collective-permute-start.1 = (bf16[1,136,128]{2,1,0:T(8,128)(2,1)S(1)}, bf16[1,136,128]{2,1,0:T(8,128)(2,1)S(1)}, u32[]{:S(2)}, u32[]{:S(2)}) collective-permute-start(bf16[1,136,128]{2,1,0:T(8,128)(2,1)S(1)} %get-tuple-element.23), channel_id=1, source_target_pairs={{0,2},{1,3},{2,0},{3,1},{4,6},{5,7},{6,4},{7,5},{8,10},{9,11},{10,... | collective-permute-start | bytes 104456 | tf_op jit(solution)/shard_map/ppermute | solution.py:376
  12.2 7.6 %collective-permute-start.4 = (bf16[1,136,128]{2,1,0:T(8,128)(2,1)S(1)}, bf16[1,136,128]{2,1,0:T(8,128)(2,1)S(1)}, u32[]{:S(2)}, u32[]{:S(2)}) collective-permute-start(bf16[1,136,128]{2,1,0:T(8,128)(2,1)S(1)} %get-tuple-element.27), channel_id=1, source_target_pairs={{0,2},{1,3},{2,0},{3,1},{4,6},{5,7},{6,4},{7,5},{8,10},{9,11},{10,... | collective-permute-start | bytes 104456 | tf_op jit(solution)/shard_map/ppermute | solution.py:376
  16.1 5.9 %collective-permute-start.2 = (bf16[1,136,128]{2,1,0:T(8,128)(2,1)S(1)}, bf16[1,136,128]{2,1,0:T(8,128)(2,1)S(1)}, u32[]{:S(2)}, u32[]{:S(2)}) collective-permute-start(bf16[1,136,128]{2,1,0:T(8,128)(2,1)S(1)} %add_and_split.7), channel_id=1, source_target_pairs={{0,12},{1,13},{2,14},{3,15},{4,8},{5,9},{6,10},{7,11},{8,4},{9,5},... | collective-permute-start | bytes 104456 | tf_op jit(solution)/shard_map/ppermute | solution.py:376
  19.8 4.9 %collective-permute-start.5 = (bf16[1,136,128]{2,1,0:T(8,128)(2,1)S(1)}, bf16[1,136,128]{2,1,0:T(8,128)(2,1)S(1)}, u32[]{:S(2)}, u32[]{:S(2)}) collective-permute-start(bf16[1,136,128]{2,1,0:T(8,128)(2,1)S(1)} %add_and_split.9), channel_id=1, source_target_pairs={{0,8},{1,9},{2,10},{3,11},{4,12},{5,13},{6,14},{7,15},{8,0},{9,1},... | collective-permute-start | bytes 104456 | tf_op jit(solution)/shard_map/ppermute | solution.py:376
  19.9 4.8 %collective-permute-start.8 = (bf16[1,136,128]{2,1,0:T(8,128)(2,1)S(1)}, bf16[1,136,128]{2,1,0:T(8,128)(2,1)S(1)}, u32[]{:S(2)}, u32[]{:S(2)}) collective-permute-start(bf16[1,136,128]{2,1,0:T(8,128)(2,1)S(1)} %get-tuple-element.32), channel_id=1, source_target_pairs={{0,4},{1,5},{2,6},{3,7},{4,0},{5,1},{6,2},{7,3},{8,12},{9,13},{10,... | collective-permute-start | bytes 104456 | tf_op jit(solution)/shard_map/ppermute | solution.py:376
  24.8 3.9 %collective-permute-start.9 = (bf16[4,32,128]{2,1,0:T(8,128)(2,1)S(1)}, bf16[4,32,128]{2,1,0:T(8,128)(2,1)S(1)}, u32[]{:S(2)}, u32[]{:S(2)}) collective-permute-start(bf16[4,32,128]{2,1,0:T(8,128)(2,1)S(1)} %finish.1.refs_0_), channel_id=1, source_target_pairs={{0,4},{1,5},{2,6},{3,7},{4,0},{5,1},{6,2},{7,3},{8,12},{9,13},{10,... | collective-permute-start | bytes 98312 | tf_op jit(solution)/shard_map/ppermute | solution.py:376
  25.1 5.7 %collective-permute-start.11 = (bf16[4,32,128]{2,1,0:T(8,128)(2,1)S(1)}, bf16[4,32,128]{2,1,0:T(8,128)(2,1)S(1)}, u32[]{:S(2)}, u32[]{:S(2)}) collective-permute-start(bf16[4,32,128]{2,1,0:T(8,128)(2,1)S(1)} %finish.1.refs_0_), channel_id=1, source_target_pairs={{0,12},{1,13},{2,14},{3,15},{4,8},{5,9},{6,10},{7,11},{8,4},{9,5},... | collective-permute-start | bytes 98312 | tf_op jit(solution)/shard_map/ppermute | solution.py:376
  28.4 4.8 %collective-permute-start.10 = (bf16[4,32,128]{2,1,0:T(8,128)(2,1)S(1)}, bf16[4,32,128]{2,1,0:T(8,128)(2,1)S(1)}, u32[]{:S(2)}, u32[]{:S(2)}) collective-permute-start(bf16[4,32,128]{2,1,0:T(8,128)(2,1)S(1)} %finish.1.refs_0_), channel_id=1, source_target_pairs={{0,8},{1,9},{2,10},{3,11},{4,12},{5,13},{6,14},{7,15},{8,0},{9,1},... | collective-permute-start | bytes 98312 | tf_op jit(solution)/shard_map/ppermute | solution.py:376
  28.7 6.3 %collective-permute-start.12 = (bf16[8,32,128]{2,1,0:T(8,128)(2,1)S(1)}, bf16[8,32,128]{2,1,0:T(8,128)(2,1)S(1)}, u32[]{:S(2)}, u32[]{:S(2)}) collective-permute-start(bf16[8,32,128]{2,1,0:T(8,128)(2,1)S(1)} %join.2.rest_0_), channel_id=1, source_target_pairs={{0,2},{1,3},{2,0},{3,1},{4,6},{5,7},{6,4},{7,5},{8,10},{9,11},{10,... | collective-permute-start | bytes 196616 | tf_op jit(solution)/shard_map/ppermute | solution.py:376
  33.2 4.3 %collective-permute-start.13 = (bf16[8,32,128]{2,1,0:T(8,128)(2,1)S(1)}, bf16[8,32,128]{2,1,0:T(8,128)(2,1)S(1)}, u32[]{:S(2)}, u32[]{:S(2)}) collective-permute-start(bf16[8,32,128]{2,1,0:T(8,128)(2,1)S(1)} %join.3.rest_1_), channel_id=1, source_target_pairs={{0,2},{1,3},{2,0},{3,1},{4,6},{5,7},{6,4},{7,5},{8,10},{9,11},{10,... | collective-permute-start | bytes 196616 | tf_op jit(solution)/shard_map/ppermute | solution.py:376
  34.5 2.9 %collective-permute-start.14 = (bf16[8,32,128]{2,1,0:T(8,128)(2,1)S(1)}, bf16[8,32,128]{2,1,0:T(8,128)(2,1)S(1)}, u32[]{:S(2)}, u32[]{:S(2)}) collective-permute-start(bf16[8,32,128]{2,1,0:T(8,128)(2,1)S(1)} %join.2.rest_0_), channel_id=1, source_target_pairs={{0,1},{1,0},{2,3},{3,2},{4,5},{5,4},{6,7},{7,6},{8,9},{9,8},{10,11... | collective-permute-start | bytes 196616 | tf_op jit(solution)/shard_map/ppermute | solution.py:376
  34.5 2.9 %collective-permute-start.15 = (bf16[8,32,128]{2,1,0:T(8,128)(2,1)S(1)}, bf16[8,32,128]{2,1,0:T(8,128)(2,1)S(1)}, u32[]{:S(2)}, u32[]{:S(2)}) collective-permute-start(bf16[8,32,128]{2,1,0:T(8,128)(2,1)S(1)} %join.3.rest_1_), channel_id=1, source_target_pairs={{0,1},{1,0},{2,3},{3,2},{4,5},{5,4},{6,7},{7,6},{8,9},{9,8},{10,11... | collective-permute-start | bytes 196616 | tf_op jit(solution)/shard_map/ppermute | solution.py:376
  35.1 2.4 %collective-permute-start.16 = (bf16[8,32,128]{2,1,0:T(8,128)(2,1)S(1)}, bf16[8,32,128]{2,1,0:T(8,128)(2,1)S(1)}, u32[]{:S(2)}, u32[]{:S(2)}) collective-permute-start(bf16[8,32,128]{2,1,0:T(8,128)(2,1)S(1)} %collective-permute-done.12.rest_2_), channel_id=1, source_target_pairs={{0,1},{1,0},{2,3},{3,2},{4,5},{5,4},{6,7},{7,6},{8,9},{9,8},{10,11... | collective-permute-start | bytes 196616 | tf_op jit(solution)/shard_map/ppermute | solution.py:376
  37.5 1.3 %collective-permute-start.17 = (bf16[8,32,128]{2,1,0:T(8,128)(2,1)S(1)}, bf16[8,32,128]{2,1,0:T(8,128)(2,1)S(1)}, u32[]{:S(2)}, u32[]{:S(2)}) collective-permute-start(bf16[8,32,128]{2,1,0:T(8,128)(2,1)S(1)} %collective-permute-done.13.rest_3_), channel_id=1, source_target_pairs={{0,1},{1,0},{2,3},{3,2},{4,5},{5,4},{6,7},{7,6},{8,9},{9,8},{10,11... | collective-permute-start | bytes 196616 | tf_op jit(solution)/shard_map/ppermute | solution.py:376

commit v9 on v7

--- a/solution.py
+++ b/solution.py
@@ -168,15 +168,16 @@
                 total_ref[place, tile_rows:] = (
                     total_ref[place, tile_rows:] + jnp.where(lane == t % tile_side, weight, 0.0))
 
-    for step in range(epochs // TOGETHER + 1):
-        now = range(step * TOGETHER, min(epochs, (step + 1) * TOGETHER))
+    cuts = [0, *range(1, epochs, TOGETHER), epochs]
+    steps = [range(a, b) for a, b in zip(cuts, cuts[1:])]
+    for now, before in zip(steps + [range(0)], [range(0)] + steps):
         for epoch in now:
             images[epoch].wait()
-        before = range((step - 1) * TOGETHER, step * TOGETHER) if step else ()
         for k in range(TOGETHER):
             for epoch in now[k:k + 1]:
-                column_pass(epoch, column_pass_refs[epoch % (2 * TOGETHER)])
-                mixers(epoch, mixer_refs[epoch % (2 * TOGETHER)])
+                slot = epoch % (2 * TOGETHER)
+                column_pass(epoch, column_pass_refs[slot])
+                mixers(epoch, mixer_refs[slot])
             for epoch in before[k:k + 1]:
                 slot = epoch % (2 * TOGETHER)
                 row_pass(epoch, mixer_refs[slot], column_pass_refs[slot])

time: 41.7 us -> 42 us (level)
  no operation moved by 1% of the time
where the time goes in v9:
time: 42 us; the launch traced here: 41.8 us
  starting transfers between devices  17.8 us (42%)
  waiting for transfers between devices  13.1 us (31%)
  Pallas kernels  10.1 us (24%)
  between operations  0.74 us (2%)
    ppermute x18, starting transfers between devices, exchange(): lax.ppermute(value, 'band', [(d, d ^ step) for d in range(band_count)])  17.8 us
    ppermute x18, waiting for transfers between devices, exchange(): lax.ppermute(value, 'band', [(d, d ^ step) for d in range(band_count)])  13.1 us
    pallas_call x1, Pallas kernels, smooth(): pl.pallas_call(functools.partial(smooth_kernel, factors=factors, row_coun...  7.08 us
    pallas_call x1, Pallas kernels, subtract(): pl.pallas_call(functools.partial(difference_kernel, factors=factors, coun...  2.82 us
  transfers between devices with their start and end apart: 18, of which 9 were waited for; matrix products, arithmetic and copies ran while one was open for 0% of the time, Pallas kernels for 0%

profile of v9, /device:TPU:0, one launch (start us, length us, event | category | flops | bytes accessed | tf_op | source)
XLA Modules:
  0.0 41.8 jit_solution(8672017982913381010)
XLA Ops:
  0.6 0.0 copy-start.1
  0.6 0.0 copy-start
  0.7 0.0 copy-start.2
  0.7 7.1 %smooth.1 = (f32[8,16,32,128]{3,2,1,0:T(8,128)S(1)}, bf16[2,136,128]{2,1,0:T(8,128)(2,1)S(1)}, bf16[2,136,128]{2,1,0:T(8,128)(2,1)S(1)}, bf16[4,136,128]{2,1,0:T...) custom-call(s32[1]{0:T(128)} %bitcast.me_ref, ...), custom_call_target="tpu_custom_call" | custom-call | tf_op jit(solution)/shard_map/smooth/pallas_call | solution.py:229
  7.7 0.6 %collective-permute-start.6 = (bf16[4,136,128]{2,1,0:T(8,128)(2,1)S(1)}, bf16[4,136,128]{2,1,0:T(8,128)(2,1)S(1)}, u32[]{:S(2)}, u32[]{:S(2)}) collective-permute-start(bf16[4,136,128]{2,1,0:T(8,128)(2,1)S(1)} %get-tuple-element.29), channel_id=1, source_target_pairs={{0,1},{1,0},{2,3},{3,2},{4,5},{5,4},{6,7},{7,6},{8,9},{9,8},{10,11... | collective-permute-start | bytes 417800 | tf_op jit(solution)/shard_map/ppermute | solution.py:372
  8.3 0.1 collective-permute-start
  8.4 0.4 %collective-permute-start.3 = (bf16[2,136,128]{2,1,0:T(8,128)(2,1)S(1)}, bf16[2,136,128]{2,1,0:T(8,128)(2,1)S(1)}, u32[]{:S(2)}, u32[]{:S(2)}) collective-permute-start(bf16[2,136,128]{2,1,0:T(8,128)(2,1)S(1)} %get-tuple-element.25), channel_id=1, source_target_pairs={{0,1},{1,0},{2,3},{3,2},{4,5},{5,4},{6,7},{7,6},{8,9},{9,8},{10,11... | collective-permute-start | bytes 208904 | tf_op jit(solution)/shard_map/ppermute | solution.py:372
  8.8 0.5 %collective-permute-done.6.refs_1_ = bf16[4,136,128]{2,1,0:T(8,128)(2,1)S(1)} collective-permute-done((bf16[4,136,128]{2,1,0:T(8,128)(2,1)S(1)}, bf16[4,136,128]{2,1,0:T(8,128)(2,1)S(1)}, u32[]{:S(2)}, u32[]{:S(2)}) %collective-permute-start.6) | collective-permute-done | bytes 139296 | tf_op jit(solution)/shard_map/ppermute | solution.py:372
  9.3 2.9 %collective-permute-start.7 = (bf16[2,136,128]{2,1,0:T(8,128)(2,1)S(1)}, bf16[2,136,128]{2,1,0:T(8,128)(2,1)S(1)}, u32[]{:S(2)}, u32[]{:S(2)}) collective-permute-start(bf16[2,136,128]{2,1,0:T(8,128)(2,1)S(1)} %get-tuple-element.31), channel_id=1, source_target_pairs={{0,2},{1,3},{2,0},{3,1},{4,6},{5,7},{6,4},{7,5},{8,10},{9,11},{10,... | collective-permute-start | bytes 208904 | tf_op jit(solution)/shard_map/ppermute | solution.py:372
  12.3 0.0 collective-permute-done.refs_1_
  12.3 0.1 collective-permute-start.1
  12.4 0.0 collective-permute-done.3.refs_1_
  12.4 2.1 %collective-permute-start.4 = (bf16[1,136,128]{2,1,0:T(8,128)(2,1)S(1)}, bf16[1,136,128]{2,1,0:T(8,128)(2,1)S(1)}, u32[]{:S(2)}, u32[]{:S(2)}) collective-permute-start(bf16[1,136,128]{2,1,0:T(8,128)(2,1)S(1)} %get-tuple-element.27), channel_id=1, source_target_pairs={{0,2},{1,3},{2,0},{3,1},{4,6},{5,7},{6,4},{7,5},{8,10},{9,11},{10,... | collective-permute-start | bytes 104456 | tf_op jit(solution)/shard_map/ppermute | solution.py:372
  14.5 1.8 %collective-permute-done.1.refs_1_ = bf16[1,136,128]{2,1,0:T(8,128)(2,1)S(1)} collective-permute-done((bf16[1,136,128]{2,1,0:T(8,128)(2,1)S(1)}, bf16[1,136,128]{2,1,0:T(8,128)(2,1)S(1)}, u32[]{:S(2)}, u32[]{:S(2)}) %collective-permute-start.1) | collective-permute-done | bytes 34848 | tf_op jit(solution)/shard_map/ppermute | solution.py:372
  16.3 3.7 %collective-permute-start.2 = (bf16[1,136,128]{2,1,0:T(8,128)(2,1)S(1)}, bf16[1,136,128]{2,1,0:T(8,128)(2,1)S(1)}, u32[]{:S(2)}, u32[]{:S(2)}) collective-permute-start(bf16[1,136,128]{2,1,0:T(8,128)(2,1)S(1)} %add_and_split.7), channel_id=1, source_target_pairs={{0,12},{1,13},{2,14},{3,15},{4,8},{5,9},{6,10},{7,11},{8,4},{9,5},... | collective-permute-start | bytes 104456 | tf_op jit(solution)/shard_map/ppermute | solution.py:372
  20.0 0.0 collective-permute-done.4.refs_1_
  20.0 0.1 collective-permute-start.5
  20.1 0.0 collective-permute-done.7.refs_1_
  20.1 1.1 %collective-permute-start.8 = (bf16[1,136,128]{2,1,0:T(8,128)(2,1)S(1)}, bf16[1,136,128]{2,1,0:T(8,128)(2,1)S(1)}, u32[]{:S(2)}, u32[]{:S(2)}) collective-permute-start(bf16[1,136,128]{2,1,0:T(8,128)(2,1)S(1)} %get-tuple-element.32), channel_id=1, source_target_pairs={{0,4},{1,5},{2,6},{3,7},{4,0},{5,1},{6,2},{7,3},{8,12},{9,13},{10,... | collective-permute-start | bytes 104456 | tf_op jit(solution)/shard_map/ppermute | solution.py:372
  21.2 1.0 %collective-permute-done.2.refs_0_ = bf16[1,136,128]{2,1,0:T(8,128)(2,1)S(1)} collective-permute-done((bf16[1,136,128]{2,1,0:T(8,128)(2,1)S(1)}, bf16[1,136,128]{2,1,0:T(8,128)(2,1)S(1)}, u32[]{:S(2)}, u32[]{:S(2)}) %collective-permute-start.2) | collective-permute-done | bytes 34848 | tf_op jit(solution)/shard_map/ppermute | solution.py:372
  22.2 2.7 %collective-permute-done.5.refs_1_ = bf16[1,136,128]{2,1,0:T(8,128)(2,1)S(1)} collective-permute-done((bf16[1,136,128]{2,1,0:T(8,128)(2,1)S(1)}, bf16[1,136,128]{2,1,0:T(8,128)(2,1)S(1)}, u32[]{:S(2)}, u32[]{:S(2)}) %collective-permute-start.5) | collective-permute-done | bytes 34848 | tf_op jit(solution)/shard_map/ppermute | solution.py:372
  24.9 0.0 collective-permute-done.8.refs_2_
  24.9 0.1 finish.1.refs_0_
  25.0 0.3 collective-permute-start.9
  25.3 3.3 %collective-permute-start.11 = (bf16[4,32,128]{2,1,0:T(8,128)(2,1)S(1)}, bf16[4,32,128]{2,1,0:T(8,128)(2,1)S(1)}, u32[]{:S(2)}, u32[]{:S(2)}) collective-permute-start(bf16[4,32,128]{2,1,0:T(8,128)(2,1)S(1)} %finish.1.refs_0_), channel_id=1, source_target_pairs={{0,12},{1,13},{2,14},{3,15},{4,8},{5,9},{6,10},{7,11},{8,4},{9,5},... | collective-permute-start | bytes 98312 | tf_op jit(solution)/shard_map/ppermute | solution.py:372
  28.6 0.0 collective-permute-start.10
  28.6 0.3 collective-permute-done.9.refs_1_
  29.0 1.3 %collective-permute-start.12 = (bf16[8,32,128]{2,1,0:T(8,128)(2,1)S(1)}, bf16[8,32,128]{2,1,0:T(8,128)(2,1)S(1)}, u32[]{:S(2)}, u32[]{:S(2)}) collective-permute-start(bf16[8,32,128]{2,1,0:T(8,128)(2,1)S(1)} %join.2.rest_0_), channel_id=1, source_target_pairs={{0,2},{1,3},{2,0},{3,1},{4,6},{5,7},{6,4},{7,5},{8,10},{9,11},{10,... | collective-permute-start | bytes 196616 | tf_op jit(solution)/shard_map/ppermute | solution.py:372
  30.3 0.7 %collective-permute-done.11.refs_1_ = bf16[4,32,128]{2,1,0:T(8,128)(2,1)S(1)} collective-permute-done((bf16[4,32,128]{2,1,0:T(8,128)(2,1)S(1)}, bf16[4,32,128]{2,1,0:T(8,128)(2,1)S(1)}, u32[]{:S(2)}, u32[]{:S(2)}) %collective-permute-start.11) | collective-permute-done | bytes 32800 | tf_op jit(solution)/shard_map/ppermute | solution.py:372
  31.0 2.4 %collective-permute-done.10.refs_0_ = bf16[4,32,128]{2,1,0:T(8,128)(2,1)S(1)} collective-permute-done((bf16[4,32,128]{2,1,0:T(8,128)(2,1)S(1)}, bf16[4,32,128]{2,1,0:T(8,128)(2,1)S(1)}, u32[]{:S(2)}, u32[]{:S(2)}) %collective-permute-start.10) | collective-permute-done | bytes 32800 | tf_op jit(solution)/shard_map/ppermute | solution.py:372
  33.4 1.3 %collective-permute-start.13 = (bf16[8,32,128]{2,1,0:T(8,128)(2,1)S(1)}, bf16[8,32,128]{2,1,0:T(8,128)(2,1)S(1)}, u32[]{:S(2)}, u32[]{:S(2)}) collective-permute-start(bf16[8,32,128]{2,1,0:T(8,128)(2,1)S(1)} %join.3.rest_1_), channel_id=1, source_target_pairs={{0,2},{1,3},{2,0},{3,1},{4,6},{5,7},{6,4},{7,5},{8,10},{9,11},{10,... | collective-permute-start | bytes 196616 | tf_op jit(solution)/shard_map/ppermute | solution.py:372
  34.8 0.0 collective-permute-start.14
  34.8 0.5 %collective-permute-start.15 = (bf16[8,32,128]{2,1,0:T(8,128)(2,1)S(1)}, bf16[8,32,128]{2,1,0:T(8,128)(2,1)S(1)}, u32[]{:S(2)}, u32[]{:S(2)}) collective-permute-start(bf16[8,32,128]{2,1,0:T(8,128)(2,1)S(1)} %join.3.rest_1_), channel_id=1, source_target_pairs={{0,1},{1,0},{2,3},{3,2},{4,5},{5,4},{6,7},{7,6},{8,9},{9,8},{10,11... | collective-permute-start | bytes 196616 | tf_op jit(solution)/shard_map/ppermute | solution.py:372
  35.3 0.0 collective-permute-done.12.rest_2_
  35.3 0.0 collective-permute-start.16
  35.3 2.4 %collective-permute-done.13.rest_3_ = bf16[8,32,128]{2,1,0:T(8,128)(2,1)S(1)} collective-permute-done((bf16[8,32,128]{2,1,0:T(8,128)(2,1)S(1)}, bf16[8,32,128]{2,1,0:T(8,128)(2,1)S(1)}, u32[]{:S(2)}, u32[]{:S(2)}) %collective-permute-start.13) | collective-permute-done | bytes 65568 | tf_op jit(solution)/shard_map/ppermute | solution.py:372
  37.7 0.0 collective-permute-start.17
  37.7 0.0 collective-permute-done.14.rest_4_
  37.7 0.0 collective-permute-done.15.rest_5_
  37.7 0.0 collective-permute-done.16.rest_6_
  37.7 1.2 %collective-permute-done.17.rest_7_ = bf16[8,32,128]{2,1,0:T(8,128)(2,1)S(1)} collective-permute-done((bf16[8,32,128]{2,1,0:T(8,128)(2,1)S(1)}, bf16[8,32,128]{2,1,0:T(8,128)(2,1)S(1)}, u32[]{:S(2)}, u32[]{:S(2)}) %collective-permute-start.17) | collective-permute-done | bytes 65568 | tf_op jit(solution)/shard_map/ppermute | solution.py:372
  39.0 0.0 copy-done.1
  39.0 0.0 copy-done
  39.0 0.0 copy-done.2
  39.0 2.8 %subtract.1 = (f32[8,16,32,128]{3,2,1,0:T(8,128)}, bf16[4,32,128]{2,1,0:T(8,128)(2,1)}) custom-call(s32[1]{0:T(128)} %bitcast.me_ref, f32[1,8]{1,0:T(1,128)S(1)} %copy-done.2, s32[8,16]{1,0:T(8,128)S(1)} %bitcast.9, s32[8,16]{1,0:T(8,128)S(1)} %bitcast.11, f32[8,16,32,128]{3,2,1,0:T(8,128)S(1)} %get-tuple-element.19.smooth_ref, ...), custom_call_target="tpu_custom_call" | custom-call | tf_op jit(solution)/shard_map/subtract/pallas_call | solution.py:339
  (8 shorter events, 0.1 us)
Async XLA Ops:
  0.6 38.3 %copy-start.1 = (s32[1,8,16]{2,1,0:T(8,128)S(1)}, s32[1,8,16]{2,1,0:T(8,128)}, u32[]{:S(2)}) copy-start(s32[1,8,16]{2,1,0:T(8,128)} %param.16) | copy-start | bytes 1540
  0.6 38.3 %copy-start = (s32[1,8,16,1]{2,3,1,0:T(1,128)S(1)}, s32[1,8,16,1]{2,3,1,0:T(1,128)}, u32[]{:S(2)}) copy-start(s32[1,8,16,1]{2,3,1,0:T(1,128)} %param.15) | copy-start | bytes 1540
  0.7 38.3 %copy-start.2 = (f32[1,8]{1,0:T(1,128)S(1)}, f32[1,8]{1,0:T(1,128)}, u32[]{:S(2)}) copy-start(f32[1,8]{1,0:T(1,128)} %scale_ref.1) | copy-start | bytes 100
  7.7 1.5 %collective-permute-start.6 = (bf16[4,136,128]{2,1,0:T(8,128)(2,1)S(1)}, bf16[4,136,128]{2,1,0:T(8,128)(2,1)S(1)}, u32[]{:S(2)}, u32[]{:S(2)}) collective-permute-start(bf16[4,136,128]{2,1,0:T(8,128)(2,1)S(1)} %get-tuple-element.29), channel_id=1, source_target_pairs={{0,1},{1,0},{2,3},{3,2},{4,5},{5,4},{6,7},{7,6},{8,9},{9,8},{10,11... | collective-permute-start | bytes 417800 | tf_op jit(solution)/shard_map/ppermute | solution.py:372
  8.3 4.0 %collective-permute-start = (bf16[2,136,128]{2,1,0:T(8,128)(2,1)S(1)}, bf16[2,136,128]{2,1,0:T(8,128)(2,1)S(1)}, u32[]{:S(2)}, u32[]{:S(2)}) collective-permute-start(bf16[2,136,128]{2,1,0:T(8,128)(2,1)S(1)} %get-tuple-element.21), channel_id=1, source_target_pairs={{0,1},{1,0},{2,3},{3,2},{4,5},{5,4},{6,7},{7,6},{8,9},{9,8},{10,11... | collective-permute-start | bytes 208904 | tf_op jit(solution)/shard_map/ppermute | solution.py:372
  8.4 4.0 %collective-permute-start.3 = (bf16[2,136,128]{2,1,0:T(8,128)(2,1)S(1)}, bf16[2,136,128]{2,1,0:T(8,128)(2,1)S(1)}, u32[]{:S(2)}, u32[]{:S(2)}) collective-permute-start(bf16[2,136,128]{2,1,0:T(8,128)(2,1)S(1)} %get-tuple-element.25), channel_id=1, source_target_pairs={{0,1},{1,0},{2,3},{3,2},{4,5},{5,4},{6,7},{7,6},{8,9},{9,8},{10,11... | collective-permute-start | bytes 208904 | tf_op jit(solution)/shard_map/ppermute | solution.py:372
  9.3 10.8 %collective-permute-start.7 = (bf16[2,136,128]{2,1,0:T(8,128)(2,1)S(1)}, bf16[2,136,128]{2,1,0:T(8,128)(2,1)S(1)}, u32[]{:S(2)}, u32[]{:S(2)}) collective-permute-start(bf16[2,136,128]{2,1,0:T(8,128)(2,1)S(1)} %get-tuple-element.31), channel_id=1, source_target_pairs={{0,2},{1,3},{2,0},{3,1},{4,6},{5,7},{6,4},{7,5},{8,10},{9,11},{10,... | collective-permute-start | bytes 208904 | tf_op jit(solution)/shard_map/ppermute | solution.py:372
  12.3 4.0 %collective-permute-start.1 = (bf16[1,136,128]{2,1,0:T(8,128)(2,1)S(1)}, bf16[1,136,128]{2,1,0:T(8,128)(2,1)S(1)}, u32[]{:S(2)}, u32[]{:S(2)}) collective-permute-start(bf16[1,136,128]{2,1,0:T(8,128)(2,1)S(1)} %get-tuple-element.23), channel_id=1, source_target_pairs={{0,2},{1,3},{2,0},{3,1},{4,6},{5,7},{6,4},{7,5},{8,10},{9,11},{10,... | collective-permute-start | bytes 104456 | tf_op jit(solution)/shard_map/ppermute | solution.py:372
  12.4 7.6 %collective-permute-start.4 = (bf16[1,136,128]{2,1,0:T(8,128)(2,1)S(1)}, bf16[1,136,128]{2,1,0:T(8,128)(2,1)S(1)}, u32[]{:S(2)}, u32[]{:S(2)}) collective-permute-start(bf16[1,136,128]{2,1,0:T(8,128)(2,1)S(1)} %get-tuple-element.27), channel_id=1, source_target_pairs={{0,2},{1,3},{2,0},{3,1},{4,6},{5,7},{6,4},{7,5},{8,10},{9,11},{10,... | collective-permute-start | bytes 104456 | tf_op jit(solution)/shard_map/ppermute | solution.py:372
  16.3 5.9 %collective-permute-start.2 = (bf16[1,136,128]{2,1,0:T(8,128)(2,1)S(1)}, bf16[1,136,128]{2,1,0:T(8,128)(2,1)S(1)}, u32[]{:S(2)}, u32[]{:S(2)}) collective-permute-start(bf16[1,136,128]{2,1,0:T(8,128)(2,1)S(1)} %add_and_split.7), channel_id=1, source_target_pairs={{0,12},{1,13},{2,14},{3,15},{4,8},{5,9},{6,10},{7,11},{8,4},{9,5},... | collective-permute-start | bytes 104456 | tf_op jit(solution)/shard_map/ppermute | solution.py:372
  20.0 4.9 %collective-permute-start.5 = (bf16[1,136,128]{2,1,0:T(8,128)(2,1)S(1)}, bf16[1,136,128]{2,1,0:T(8,128)(2,1)S(1)}, u32[]{:S(2)}, u32[]{:S(2)}) collective-permute-start(bf16[1,136,128]{2,1,0:T(8,128)(2,1)S(1)} %add_and_split.9), channel_id=1, source_target_pairs={{0,8},{1,9},{2,10},{3,11},{4,12},{5,13},{6,14},{7,15},{8,0},{9,1},... | collective-permute-start | bytes 104456 | tf_op jit(solution)/shard_map/ppermute | solution.py:372
  20.1 4.8 %collective-permute-start.8 = (bf16[1,136,128]{2,1,0:T(8,128)(2,1)S(1)}, bf16[1,136,128]{2,1,0:T(8,128)(2,1)S(1)}, u32[]{:S(2)}, u32[]{:S(2)}) collective-permute-start(bf16[1,136,128]{2,1,0:T(8,128)(2,1)S(1)} %get-tuple-element.32), channel_id=1, source_target_pairs={{0,4},{1,5},{2,6},{3,7},{4,0},{5,1},{6,2},{7,3},{8,12},{9,13},{10,... | collective-permute-start | bytes 104456 | tf_op jit(solution)/shard_map/ppermute | solution.py:372
  25.0 3.9 %collective-permute-start.9 = (bf16[4,32,128]{2,1,0:T(8,128)(2,1)S(1)}, bf16[4,32,128]{2,1,0:T(8,128)(2,1)S(1)}, u32[]{:S(2)}, u32[]{:S(2)}) collective-permute-start(bf16[4,32,128]{2,1,0:T(8,128)(2,1)S(1)} %finish.1.refs_0_), channel_id=1, source_target_pairs={{0,4},{1,5},{2,6},{3,7},{4,0},{5,1},{6,2},{7,3},{8,12},{9,13},{10,... | collective-permute-start | bytes 98312 | tf_op jit(solution)/shard_map/ppermute | solution.py:372
  25.3 5.7 %collective-permute-start.11 = (bf16[4,32,128]{2,1,0:T(8,128)(2,1)S(1)}, bf16[4,32,128]{2,1,0:T(8,128)(2,1)S(1)}, u32[]{:S(2)}, u32[]{:S(2)}) collective-permute-start(bf16[4,32,128]{2,1,0:T(8,128)(2,1)S(1)} %finish.1.refs_0_), channel_id=1, source_target_pairs={{0,12},{1,13},{2,14},{3,15},{4,8},{5,9},{6,10},{7,11},{8,4},{9,5},... | collective-permute-start | bytes 98312 | tf_op jit(solution)/shard_map/ppermute | solution.py:372
  28.6 4.8 %collective-permute-start.10 = (bf16[4,32,128]{2,1,0:T(8,128)(2,1)S(1)}, bf16[4,32,128]{2,1,0:T(8,128)(2,1)S(1)}, u32[]{:S(2)}, u32[]{:S(2)}) collective-permute-start(bf16[4,32,128]{2,1,0:T(8,128)(2,1)S(1)} %finish.1.refs_0_), channel_id=1, source_target_pairs={{0,8},{1,9},{2,10},{3,11},{4,12},{5,13},{6,14},{7,15},{8,0},{9,1},... | collective-permute-start | bytes 98312 | tf_op jit(solution)/shard_map/ppermute | solution.py:372
  29.0 6.3 %collective-permute-start.12 = (bf16[8,32,128]{2,1,0:T(8,128)(2,1)S(1)}, bf16[8,32,128]{2,1,0:T(8,128)(2,1)S(1)}, u32[]{:S(2)}, u32[]{:S(2)}) collective-permute-start(bf16[8,32,128]{2,1,0:T(8,128)(2,1)S(1)} %join.2.rest_0_), channel_id=1, source_target_pairs={{0,2},{1,3},{2,0},{3,1},{4,6},{5,7},{6,4},{7,5},{8,10},{9,11},{10,... | collective-permute-start | bytes 196616 | tf_op jit(solution)/shard_map/ppermute | solution.py:372
  33.4 4.3 %collective-permute-start.13 = (bf16[8,32,128]{2,1,0:T(8,128)(2,1)S(1)}, bf16[8,32,128]{2,1,0:T(8,128)(2,1)S(1)}, u32[]{:S(2)}, u32[]{:S(2)}) collective-permute-start(bf16[8,32,128]{2,1,0:T(8,128)(2,1)S(1)} %join.3.rest_1_), channel_id=1, source_target_pairs={{0,2},{1,3},{2,0},{3,1},{4,6},{5,7},{6,4},{7,5},{8,10},{9,11},{10,... | collective-permute-start | bytes 196616 | tf_op jit(solution)/shard_map/ppermute | solution.py:372
  34.8 2.9 %collective-permute-start.14 = (bf16[8,32,128]{2,1,0:T(8,128)(2,1)S(1)}, bf16[8,32,128]{2,1,0:T(8,128)(2,1)S(1)}, u32[]{:S(2)}, u32[]{:S(2)}) collective-permute-start(bf16[8,32,128]{2,1,0:T(8,128)(2,1)S(1)} %join.2.rest_0_), channel_id=1, source_target_pairs={{0,1},{1,0},{2,3},{3,2},{4,5},{5,4},{6,7},{7,6},{8,9},{9,8},{10,11... | collective-permute-start | bytes 196616 | tf_op jit(solution)/shard_map/ppermute | solution.py:372
  34.8 2.9 %collective-permute-start.15 = (bf16[8,32,128]{2,1,0:T(8,128)(2,1)S(1)}, bf16[8,32,128]{2,1,0:T(8,128)(2,1)S(1)}, u32[]{:S(2)}, u32[]{:S(2)}) collective-permute-start(bf16[8,32,128]{2,1,0:T(8,128)(2,1)S(1)} %join.3.rest_1_), channel_id=1, source_target_pairs={{0,1},{1,0},{2,3},{3,2},{4,5},{5,4},{6,7},{7,6},{8,9},{9,8},{10,11... | collective-permute-start | bytes 196616 | tf_op jit(solution)/shard_map/ppermute | solution.py:372
  35.3 2.4 %collective-permute-start.16 = (bf16[8,32,128]{2,1,0:T(8,128)(2,1)S(1)}, bf16[8,32,128]{2,1,0:T(8,128)(2,1)S(1)}, u32[]{:S(2)}, u32[]{:S(2)}) collective-permute-start(bf16[8,32,128]{2,1,0:T(8,128)(2,1)S(1)} %collective-permute-done.12.rest_2_), channel_id=1, source_target_pairs={{0,1},{1,0},{2,3},{3,2},{4,5},{5,4},{6,7},{7,6},{8,9},{9,8},{10,11... | collective-permute-start | bytes 196616 | tf_op jit(solution)/shard_map/ppermute | solution.py:372
  37.7 1.3 %collective-permute-start.17 = (bf16[8,32,128]{2,1,0:T(8,128)(2,1)S(1)}, bf16[8,32,128]{2,1,0:T(8,128)(2,1)S(1)}, u32[]{:S(2)}, u32[]{:S(2)}) collective-permute-start(bf16[8,32,128]{2,1,0:T(8,128)(2,1)S(1)} %collective-permute-done.13.rest_3_), channel_id=1, source_target_pairs={{0,1},{1,0},{2,3},{3,2},{4,5},{5,4},{6,7},{7,6},{8,9},{9,8},{10,11... | collective-permute-start | bytes 196616 | tf_op jit(solution)/shard_map/ppermute | solution.py:372
